TPU v7x, 256 devices: a whole 4x4x8 slice. The times are simulated.
256 devices in a mesh: pair: 64 (over z, x, core), orb: 4 (over y).
Axes of the slice: x: 4, y: 4, z: 8, core: 2. Of those that a mesh axis runs over, the one named last changes fastest.
Arguments:
- integrals: bfloat16 [4096, 8, 128, 128], P('pair'), may hold values from -6 to 6
- screen: int32 [2, 4096, 8], P(None, 'pair'), may hold values from 0 to 95
- occupied: bfloat16 [12288, 32], P(('pair', 'orb')), may hold values from -0.3125 to 0.3125
- virtual: bfloat16 [12288, 512], P(('pair', 'orb')), may hold values from -0.5 to 0.5
- pair_index: int32 [2, 4096], replicated, may hold values from 0 to 12287
Outputs:
- mo_block: bfloat16 [4, 256, 512, 512], P('orb', 'pair')
All inputs are finite; a program needn't handle non-finite values.
Results may differ from a plain program's by a relative error of at most 0.0064.
Values may be sent and summed in bfloat16 or wider, within the bound.
No kernel may reach another device: no remote copies, remote signals or barrier semaphores. Data moves between devices by JAX's collectives and lax.ppermute only.
A program may use at most 192 MiB of HBM per device.

v0:
```python
import jax
import jax.numpy as jnp
from jax import lax
from jax.sharding import PartitionSpec as P

BLK = 128


def body(integrals, screen, occupied, virtual, pair_index):
    occ_all, vir_all = (
        lax.all_gather(occupied, ("pair", "orb"), axis=0, tiled=True),
        lax.all_gather(virtual, ("pair", "orb"), axis=0, tiled=True),
    )
    orb_count = lax.axis_size("orb")
    first_count = occ_all.shape[1] // orb_count
    own_cols = lax.dynamic_slice_in_dim(
        occ_all, lax.axis_index("orb") * first_count, first_count, 1
    )
    block_count = occ_all.shape[0] // BLK
    blocks_all = occ_all.reshape(block_count, BLK, occ_all.shape[1])
    blocks_own = own_cols.reshape(block_count, BLK, first_count)
    coef_m = blocks_own[screen[0]]
    coef_n = blocks_all[screen[1]]
    half_one = jnp.einsum(
        "pkmn,pkmi->pkni", integrals, coef_m, preferred_element_type=jnp.float32
    ).astype(jnp.bfloat16)
    half = jnp.einsum(
        "pknj,pkni->pji", coef_n, half_one, preferred_element_type=jnp.float32
    ).astype(jnp.bfloat16)
    local_rows = half.reshape(half.shape[0], half.shape[1] * first_count)
    owned = lax.all_to_all(local_rows, "pair", split_axis=1, concat_axis=0, tiled=True)
    left = vir_all[pair_index[0]]
    right = vir_all[pair_index[1]]
    weighted = (
        left[:, None, :].astype(jnp.float32) * owned[:, :, None].astype(jnp.float32)
    ).astype(jnp.bfloat16)
    pair_total = weighted.shape[0]
    owned_count = weighted.shape[1]
    width = weighted.shape[2]
    flat = weighted.reshape(pair_total, owned_count * width)
    result = lax.dot_general(
        flat, right, (((0,), (0,)), ((), ())), preferred_element_type=jnp.float32
    )
    return result.astype(jnp.bfloat16).reshape(1, owned_count, width, width)


def solution(mesh):
    placed = (
        P("pair", None, None, None),
        P(None, "pair", None),
        P(("pair", "orb"), None),
        P(("pair", "orb"), None),
        P(),
    )
    return jax.shard_map(
        body, mesh=mesh, in_specs=placed, out_specs=P("orb", "pair", None, None), check_vma=False
    )
```

profile of v0, /device:TPU:1, one launch (start us, length us, event | category | flops | bytes accessed | tf_op | source)
XLA Modules:
  0.0 238.8 jit_solution(517363970379179676)
XLA Ops:
  6.5 0.7 all-gather.3.cloned.1.call-update
  7.3 77.0 %all-gather = bf16[256,48,32]{1,2,0:T(8,128)(2,1)S(1)} all-gather(bf16[1,48,32]{1,2,0:T(8,128)(2,1)} %bitcast.55), channel_id=1, replica_groups=mesh['pair'=64,'orb'=4] {'pair','orb'}, dimensions={0}, use_global_device_ids=true | all-gather | bytes 789504 | tf_op jit(solution)/shard_map/all_gather | solution.py:11
  84.2 0.8 copy.20
  85.1 4.8 %reshape.184 = bf16[12288,32]{0,1:T(8,128)(2,1)} reshape(bf16[256,48,32]{1,0,2:T(8,128)(2,1)S(1)} %copy.20) | data formatting | bytes 1572864
  89.9 2.7 %reshape.145 = bf16[96,128,32]{1,0,2:T(8,128)(2,1)S(1)} reshape(bf16[256,48,32]{1,0,2:T(8,128)(2,1)S(1)} %copy.20) | data formatting | bytes 1572864 | tf_op jit(solution)/shard_map/reshape | solution.py:20
  92.7 0.1 reshape.167
  92.8 0.1 reshape.159
  92.9 0.3 copy.22
  93.3 0.9 dynamic-slice_bitcast_fusion
  94.2 1.8 gather_fusion.2
  96.0 3.4 %gather_fusion.1 = bf16[512,128,32]{1,2,0:T(8,128)(2,1)} fusion(bf16[96,128,32]{1,2,0:T(8,128)(2,1)S(1)} %copy.22, s32[1024]{0:T(1024)S(1)} %pad_clamp_fusion.1), kind=kCustom, calls=%fused_computation.1 | custom fusion | bytes 8390656 | tf_op jit(solution)/shard_map/gather | solution.py:23
  99.5 10.7 %fusion.1 = bf16[64,32,8]{1,2,0:T(8,128)(2,1)S(1)} fusion(bf16[64,8,128,32]{2,3,1,0:T(8,128)(2,1)} %bitcast.48, bf16[64,8,128,8]{2,3,1,0:T(8,128)(2,1)S(1)} %bitcast.47, bf16[64,8,128,128]{3,2,1,0:T(8,128)(2,1)} %param.5), kind=kOutput, calls=%fused_computation.9 | convolution fusion | flops 168312832 | bytes 22052864 | tf_op jit(solution)/shard_map/pknj,pkni->pji/dot_general | solution.py:27
  110.2 0.1 copy.25
  110.4 0.7 reshape.187
  111.1 9.3 %all-to-all-start = ((bf16[64,2,128]{2,1,0:T(2,128)(2,1)}), bf16[64,2,128]{2,1,0:T(2,128)(2,1)S(1)}, u32[]{:S(2)}, u32[]{:S(2)}) async-start(bf16[64,2,128]{2,1,0:T(2,128)(2,1)} %reshape.187), calls=%async_computation | async-start | bytes 65536 | tf_op jit(solution)/shard_map/all_to_all | solution.py:31
  120.4 9.3 %all-to-all-done = bf16[64,2,128]{2,1,0:T(2,128)(2,1)S(1)} async-done(((bf16[64,2,128]{2,1,0:T(2,128)(2,1)}), bf16[64,2,128]{2,1,0:T(2,128)(2,1)S(1)}, u32[]{:S(2)}, u32[]{:S(2)}) %all-to-all-start) | async-done | bytes 32800 | tf_op jit(solution)/shard_map/all_to_all | solution.py:31
  129.9 0.7 copy.29
  130.6 5.9 %all-gather.3.cloned.1.call-done = bf16[12288,512]{1,0:T(8,128)(2,1)} async-done(((bf16[48,512]{1,0:T(8,128)(2,1)}), bf16[12288,512]{1,0:T(8,128)(2,1)}) %all-gather.3.cloned.1.call-update) | async-done | bytes 12582928 | tf_op jit(solution)/shard_map/all_gather | solution.py:12
  136.5 23.7 %gather_fusion = bf16[4096,512]{1,0:T(8,128)(2,1)} fusion(bf16[12288,512]{1,0:T(8,128)(2,1)} %all-gather.3.cloned.1.call-done, s32[4096]{0:T(1024)S(1)} %broadcast_clamp_fusion.1), kind=kCustom, calls=%fused_computation | custom fusion | bytes 8404992 | tf_op jit(solution)/shard_map/gather | solution.py:32
  160.1 6.6 %convert_element_type.41 = f32[4096,512]{1,0:T(8,128)} convert(bf16[4096,512]{1,0:T(8,128)(2,1)} %gather_fusion) | non-fusion elementwise | flops 2097152 | bytes 12582912 | tf_op jit(solution)/shard_map/convert_element_type | solution.py:35
  166.8 10.0 %multiply_convert_fusion = bf16[4096,4,512]{2,1,0:T(4,128)(2,1)} fusion(f32[4096,4]{1,0:T(8,128)S(1)} %bitcast.51, f32[4096,512]{1,0:T(8,128)} %convert_element_type.41), kind=kLoop, calls=%fused_computation.4 | loop fusion | flops 16777216 | bytes 25231360 | tf_op jit(solution)/shard_map/convert_element_type | solution.py:36
  176.8 16.8 %copy.31 = bf16[512,8,4,512]{3,1,2,0:T(8,128)(2,1)} copy(bf16[512,8,4,512]{3,2,1,0:T(4,128)(2,1)} %bitcast.49) | data formatting | bytes 33554432
  193.7 23.7 %gather_fusion.3 = bf16[4096,512]{1,0:T(8,128)(2,1)} fusion(bf16[12288,512]{1,0:T(8,128)(2,1)} %all-gather.3.cloned.1.call-done, s32[4096]{0:T(1024)S(1)} %broadcast_clamp_fusion), kind=kCustom, calls=%fused_computation.3 | custom fusion | bytes 8404992 | tf_op jit(solution)/shard_map/gather | solution.py:33
  217.3 14.6 %convolution_convert_fusion = bf16[2048,512]{1,0:T(8,128)(2,1)} fusion(bf16[4096,2048]{1,0:T(8,128)(2,1)} %bitcast.50, bf16[4096,512]{1,0:T(8,128)(2,1)} %gather_fusion.3), kind=kOutput, calls=%fused_computation.5 | convolution fusion | flops 8590983168 | bytes 23068672 | tf_op jit(solution)/shard_map/dot_general | solution.py:41
  (15 shorter events, 0.4 us)
Async XLA Ops:
  6.5 129.9 %all-gather.3.cloned.1.call-start = ((), (), s32[]{:S(2)}) async-start(), calls=%async_computation.1 | async-start | bytes 12632064 | tf_op jit(solution)/shard_map/all_gather | solution.py:12
  84.2 8.3 %copy-start.1 = (s32[2,64,8]{1,2,0:T(8,128)S(1)}, s32[2,64,8]{1,2,0:T(8,128)}, u32[]{:S(2)}) copy-start(s32[2,64,8]{1,2,0:T(8,128)} %param.6) | copy-start | bytes 12292
  99.5 20.9 %copy-start = (s32[2,4096]{1,0:T(2,128)S(1)}, s32[2,4096]{1,0:T(2,128)}, u32[]{:S(2)}) copy-start(s32[2,4096]{1,0:T(2,128)} %param.9) | copy-start | bytes 98308
  111.1 18.7 %all-to-all-start = ((bf16[64,2,128]{2,1,0:T(2,128)(2,1)}), bf16[64,2,128]{2,1,0:T(2,128)(2,1)S(1)}, u32[]{:S(2)}, u32[]{:S(2)}) async-start(bf16[64,2,128]{2,1,0:T(2,128)(2,1)} %reshape.187), calls=%async_computation | async-start | bytes 65536 | tf_op jit(solution)/shard_map/all_to_all | solution.py:31
Sparse Core Ops, SparseCore 0:
  11.2 125.2 all-gather.2
where the time goes:
time: 239 us
  local copies, waits for them, and re-layouts  81 us (34%)
  blocking collectives  77 us (32%)
  matrix products  25.3 us (11%)
  other arithmetic  16.7 us (7%)
  waiting for transfers between devices  15.9 us (7%)
  between operations  13.5 us (6%)
  starting transfers between devices  9.26 us (4%)
    all_gather x1, blocking collectives, body(): lax.all_gather(occupied, ('pair', 'orb'), axis=0, tiled=True)  77 us
    gather x1, local copies, waits for them, and re-layouts, body(): left = vir_all[pair_index[0]]  23.7 us
    gather x1, local copies, waits for them, and re-layouts, body(): right = vir_all[pair_index[1]]  23.7 us
    unnamed x8, local copies, waits for them, and re-layouts  22.5 us
    dot_general x1, matrix products, body(): lax.dot_general(flat, right, (((0,), (0,)), ((), ())), preferred_element_...  14.6 us
    dot_general x1, matrix products, body(): jnp.einsum('pknj,pkni->pji', coef_n, half_one, preferred_element_type=jnp...  10.7 us
    convert_element_type x1, other arithmetic, body(): weighted = (left[:, None, :].astype(jnp.float32) * owned[:, :, None].asty...  10 us
    all_to_all x1, waiting for transfers between devices, body(): lax.all_to_all(local_rows, 'pair', split_axis=1, concat_axis=0, tiled=True)  9.33 us
  transfers between devices with their start and end apart: 2, of which 2 were waited for; matrix products, arithmetic and copies ran while one was open for 12% of the time, Pallas kernels for 0%

commit v1 on v0

--- a/solution.py
+++ b/solution.py
@@ -1,9 +1,70 @@
+import functools
+
 import jax
 import jax.numpy as jnp
 from jax import lax
 from jax.sharding import PartitionSpec as P
+from jax.experimental import pallas as pl
+from jax.experimental.pallas import tpu as pltpu
 
 BLK = 128
+
+
+def k2_body(npc, rows, nr, idx_ref, h_ref, *refs):
+    pieces = refs[:npc]; out_ref = refs[npc]
+    stage, V, L, LT, R, W, sem = refs[npc+1:]
+    offs=[0]
+    for n in rows: offs.append(offs[-1]+n)
+    for i in range(npc):
+        pltpu.make_async_copy(pieces[i], stage.at[pl.ds(offs[i],rows[i])], sem.at[i]).start()
+    for i in range(npc):
+        pltpu.make_async_copy(pieces[i], stage.at[pl.ds(offs[i],rows[i])], sem.at[i]).wait()
+        step=64
+        while rows[i]%step: step//=2
+        def conv(t,_,base=offs[i],step=step):
+            r0=pl.multiple_of(base+t*step,16)
+            for c in range(4):
+                x=stage[pl.ds(r0,step),c*128:(c+1)*128].astype(jnp.float32)
+                V[pl.ds(r0*4+c,step,stride=4),:]=x
+            return 0
+        lax.fori_loop(0,rows[i]//step,conv,0)
+    CH=128
+    def chunk(ci,_):
+        p0=pl.multiple_of(ci*CH,CH)
+        for side in range(2):
+            def g(t,_):
+                for u in range(16):
+                    i=t*16+u
+                    r=idx_ref[side,p0+i]
+                    L[pl.ds(pl.multiple_of(side*CH*4+i*4,4),4),:]=V[pl.ds(pl.multiple_of(r*4,4),4),:]
+                return 0
+            lax.fori_loop(0,CH//16,g,0)
+        for c in range(4):
+            a=L[pl.ds(c,CH,stride=4),:]
+            LT[c*128:(c+1)*128,pl.ds(p0,CH)]=a.T.astype(jnp.bfloat16)
+            b=L[pl.ds(CH*4+c,CH,stride=4),:]
+            R[pl.ds(p0,CH),c*128:(c+1)*128]=b.astype(jnp.bfloat16)
+        return 0
+    lax.fori_loop(0,nr//CH,chunk,0)
+    AB=256
+    def mm(t,_):
+        jk=t//2; a0=pl.multiple_of((t%2)*AB,AB)
+        h=h_ref[pl.ds(jk,1),:].astype(jnp.bfloat16)
+        W[...]=LT[pl.ds(a0,AB),:]*h
+        out_ref[jk,pl.ds(a0,AB),:]=jnp.dot(W[...],R[...],preferred_element_type=jnp.float32).astype(jnp.bfloat16)
+        return 0
+    lax.fori_loop(0,8,mm,0)
+def k2(idx,h,pieces):
+    rows=[p.shape[0] for p in pieces]; n=len(pieces); tot=sum(rows); nr=idx.shape[1]
+    return pl.pallas_call(functools.partial(k2_body,n,rows,nr),
+        out_shape=jax.ShapeDtypeStruct((4,512,512),jnp.bfloat16),
+        in_specs=[pl.BlockSpec(memory_space=pltpu.SMEM),pl.BlockSpec(memory_space=pltpu.VMEM)]+[pl.BlockSpec(memory_space=pl.ANY)]*n,
+        out_specs=pl.BlockSpec(memory_space=pltpu.VMEM),
+        scratch_shapes=[pltpu.VMEM((tot,512),jnp.bfloat16),pltpu.VMEM((tot*4,128),jnp.float32),
+            pltpu.VMEM((128*8,128),jnp.float32),pltpu.VMEM((512,nr),jnp.bfloat16),pltpu.VMEM((nr,512),jnp.bfloat16),
+            pltpu.VMEM((256,nr),jnp.bfloat16),pltpu.SemaphoreType.DMA((n,))],
+        compiler_params=pltpu.CompilerParams(vmem_limit_bytes=60*1024*1024),
+        name="gather_scale_dot")(idx,h,*pieces)
 
 
 def body(integrals, screen, occupied, virtual, pair_index):
@@ -29,19 +90,8 @@
     ).astype(jnp.bfloat16)
     local_rows = half.reshape(half.shape[0], half.shape[1] * first_count)
     owned = lax.all_to_all(local_rows, "pair", split_axis=1, concat_axis=0, tiled=True)
-    left = vir_all[pair_index[0]]
-    right = vir_all[pair_index[1]]
-    weighted = (
-        left[:, None, :].astype(jnp.float32) * owned[:, :, None].astype(jnp.float32)
-    ).astype(jnp.bfloat16)
-    pair_total = weighted.shape[0]
-    owned_count = weighted.shape[1]
-    width = weighted.shape[2]
-    flat = weighted.reshape(pair_total, owned_count * width)
-    result = lax.dot_general(
-        flat, right, (((0,), (0,)), ((), ())), preferred_element_type=jnp.float32
-    )
-    return result.astype(jnp.bfloat16).reshape(1, owned_count, width, width)
+    out = k2(pair_index, owned.T.astype(jnp.float32), [vir_all])
+    return out[None]
 
 
 def solution(mesh):

time: 239 us -> 190 us (0.79)
  local copies, waits for them, and re-layouts: 81 us -> 16.2 us
  Pallas kernels: 0 us -> 46.3 us
  blocking collectives: 77 us -> 95.3 us
  other arithmetic: 16.7 us -> 0.74 us
  matrix products: 25.3 us -> 11 us
  waiting for transfers between devices: 15.9 us -> 6.64 us
  starting transfers between devices: 9.26 us -> 0.01 us
    gather x2 -> x0, local copies, waits for them, and re-layouts: 47.3 us -> none  [the longest x1 23.7 us: body(): left = vir_all[pair_index[0]]]
    pallas_call x0 -> x1, Pallas kernels: none -> 46.3 us  [k2(): pl.pallas_call(functools.partial(k2_body, n, rows, nr), out_shape=jax.Sha...]
    all_to_all x0 -> x1, blocking collectives: none -> 18.4 us  [body(): lax.all_to_all(local_rows, 'pair', split_axis=1, concat_axis=0, tiled=True)]
    unnamed x8 -> x3, local copies, waits for them, and re-layouts: 22.5 us -> 5 us
    convert_element_type x3 -> x1, other arithmetic: 16.7 us -> 0.02 us  [body(): out = k2(pair_index, owned.T.astype(jnp.float32), [vir_all])]
    dot_general x1 -> x0, matrix products: 14.6 us -> none  [body(): lax.dot_general(flat, right, (((0,), (0,)), ((), ())), preferred_element_...]
    all_to_all x1 -> x0, waiting for transfers between devices: 9.33 us -> none  [body(): lax.all_to_all(local_rows, 'pair', split_axis=1, concat_axis=0, tiled=True)]
    all_to_all x1 -> x0, starting transfers between devices: 9.26 us -> none  [body(): lax.all_to_all(local_rows, 'pair', split_axis=1, concat_axis=0, tiled=True)]
  transfers between devices with their start and end apart: 2 -> 1, of which waited for: 2 -> 1; matrix products, arithmetic and copies ran while one was open for 12% -> 15% of each run, Pallas kernels for 0% -> 0%
where the time goes in v1:
time: 190 us
  blocking collectives  95.3 us (50%)
  Pallas kernels  46.3 us (24%)
  local copies, waits for them, and re-layouts  16.2 us (9%)
  between operations  13.5 us (7%)
  matrix products  11 us (6%)
  waiting for transfers between devices  6.64 us (3%)
    all_gather x1, blocking collectives, body(): lax.all_gather(occupied, ('pair', 'orb'), axis=0, tiled=True)  77 us
    pallas_call x1, Pallas kernels, k2(): pl.pallas_call(functools.partial(k2_body, n, rows, nr), out_shape=jax.Sha...  46.3 us
    all_to_all x1, blocking collectives, body(): lax.all_to_all(local_rows, 'pair', split_axis=1, concat_axis=0, tiled=True)  18.4 us
    dot_general x1, matrix products, body(): jnp.einsum('pknj,pkni->pji', coef_n, half_one, preferred_element_type=jnp...  11 us
    all_gather x1, waiting for transfers between devices, body(): lax.all_gather(virtual, ('pair', 'orb'), axis=0, tiled=True)  5.93 us
    unnamed x3, local copies, waits for them, and re-layouts  5 us
  transfers between devices with their start and end apart: 1, of which 1 were waited for; matrix products, arithmetic and copies ran while one was open for 15% of the time, Pallas kernels for 0%

profile of v1, /device:TPU:1, one launch (start us, length us, event | category | flops | bytes accessed | tf_op | source)
XLA Modules:
  0.0 189.7 jit_solution(567432403976408849)
XLA Ops:
  6.5 0.0 all-gather.3.cloned.1.call-start
  6.5 0.7 all-gather.3.cloned.1.call-update
  7.3 77.0 %all-gather = bf16[256,48,32]{1,2,0:T(8,128)(2,1)S(1)} all-gather(bf16[1,48,32]{1,2,0:T(8,128)(2,1)} %bitcast.43), channel_id=1, replica_groups=mesh['pair'=64,'orb'=4] {'pair','orb'}, dimensions={0}, use_global_device_ids=true | all-gather | bytes 789504 | tf_op jit(solution)/shard_map/all_gather | solution.py:72
  84.2 0.8 copy.13
  85.0 4.8 %reshape.91 = bf16[12288,32]{0,1:T(8,128)(2,1)} reshape(bf16[256,48,32]{1,0,2:T(8,128)(2,1)S(1)} %copy.13) | data formatting | bytes 1572864
  89.9 2.7 %reshape.69 = bf16[96,128,32]{1,0,2:T(8,128)(2,1)S(1)} reshape(bf16[256,48,32]{1,0,2:T(8,128)(2,1)S(1)} %copy.13) | data formatting | bytes 1572864 | tf_op jit(solution)/shard_map/reshape | solution.py:81
  92.5 0.7 compare_select_fusion
  93.2 0.1 copy.17
  93.3 0.1 reshape.82
  93.4 0.3 copy.15
  93.7 0.1 copy.14
  93.8 0.1 reshape.74
  93.9 0.9 dynamic-slice_bitcast_fusion
  94.9 1.8 gather_fusion.1
  96.7 3.4 %gather_fusion = bf16[512,128,32]{1,2,0:T(8,128)(2,1)} fusion(bf16[96,128,32]{1,2,0:T(8,128)(2,1)S(1)} %copy.15, s32[1024]{0:T(1024)S(1)} %pad_clamp_fusion.1), kind=kCustom, calls=%fused_computation | custom fusion | bytes 8390656 | tf_op jit(solution)/shard_map/gather | solution.py:84
  100.1 11.0 %fusion.1 = bf16[64,32,8]{1,2,0:T(8,128)(2,1)S(1)} fusion(bf16[64,8,128,32]{2,3,1,0:T(8,128)(2,1)} %bitcast.40, bf16[64,8,128,8]{2,3,1,0:T(8,128)(2,1)S(1)} %bitcast.39, bf16[64,8,128,128]{3,2,1,0:T(8,128)(2,1)} %param.5), kind=kOutput, calls=%fused_computation.5 | convolution fusion | flops 168312832 | bytes 22052864 | tf_op jit(solution)/shard_map/pknj,pkni->pji/dot_general | solution.py:88
  111.1 0.1 copy.18
  111.3 0.1 reshape.94
  111.4 18.4 %all_to_all.13 = bf16[64,2,128]{2,1,0:T(2,128)(2,1)S(1)} all-to-all(bf16[64,2,128]{2,1,0:T(2,128)(2,1)S(1)} %reshape.94), channel_id=1, replica_groups=mesh['pair'=64,'orb'=4] {'pair'}, dimensions={0} | all-to-all | bytes 65536 | tf_op jit(solution)/shard_map/all_to_all | solution.py:92
  129.7 0.1 reshape.95
  129.9 0.7 reshape.71
  130.6 5.9 %all-gather.3.cloned.1.call-done.refs_0_ = bf16[12288,512]{1,0:T(8,128)(2,1)} async-done(((bf16[48,512]{1,0:T(8,128)(2,1)}), bf16[12288,512]{1,0:T(8,128)(2,1)}) %all-gather.3.cloned.1.call-update) | async-done | bytes 12582928 | tf_op jit(solution)/shard_map/all_gather | solution.py:73
  136.5 46.3 %gather_scale_dot.1 = bf16[4,512,512]{2,1,0:T(8,128)(2,1)} custom-call(s32[2,4096]{1,0:T(2,128)} %idx_ref.1, f32[4,4096]{1,0:T(4,128)} %bitcast.41, bf16[12288,512]{1,0:T(8,128)(2,1)} %all-gather.3.cloned.1.call-done.refs_0_), custom_call_target="tpu_custom_call" | custom-call | tf_op jit(solution)/shard_map/gather_scale_dot/pallas_call | solution.py:59
  (4 shorter events, 0.0 us)
Async XLA Ops:
  6.5 130.0 %all-gather.3.cloned.1.call-start = ((), (), s32[]{:S(2)}) async-start(), calls=%async_computation.1 | async-start | bytes 12632064 | tf_op jit(solution)/shard_map/all_gather | solution.py:73
Sparse Core Ops, SparseCore 0:
  11.2 125.3 all-gather.2

commit v2 on v0

v2 whole, which is shorter than its diff:
```python
import functools

import jax
import jax.numpy as jnp
from jax import lax
from jax.experimental import pallas as pl
from jax.experimental.pallas import tpu as pltpu
from jax.sharding import PartitionSpec as P

BLK = 128
NZ, NX, NY = 8, 4, 4
BF, F32 = jnp.bfloat16, jnp.float32


def pair_moves(dz=0, dx=0, dc=0):
    moves = []
    for z in range(NZ):
        for x in range(NX):
            for c in range(2):
                src = (((z + dz) % NZ) * NX + (x + dx) % NX) * 2 + (c + dc) % 2
                moves.append((src, (z * NX + x) * 2 + c))
    return moves


def fetch(value, axis, step):
    if axis == "y":
        return lax.ppermute(value, "orb", [((y + step) % NY, y) for y in range(NY)])
    return lax.ppermute(value, "pair", pair_moves(**{"d" + axis: step}))


def rows(*parts):
    return jnp.concatenate(parts, axis=0)


def four(value, axis):
    return [value] + [fetch(value, axis, step) for step in (1, 2, 3)]


def cross(value, step, swap):
    moves = []
    for z in range(NZ):
        for x in range(NX):
            for c in range(2):
                for y in range(NY):
                    ex, ey = (x, (y + step) % NY) if c == swap else ((x + step) % NX, y)
                    src = ((z * NX + ex) * 2 + c) * NY + ey
                    moves.append((src, ((z * NX + x) * 2 + c) * NY + y))
    return lax.ppermute(value, ("pair", "orb"), moves)


def ring(value, move):
    half = value.shape[0] // 2
    up, down = move(value, 1), move(value, -1)
    far = [move(up[:half], 1), move(down[half:], -1)]
    return [value, up, *far, down]


def gather_virtual(v):
    near = rows(fetch(v, "z", -1), v, fetch(v, "z", 1))
    far_up = fetch(near, "z", 3)
    far_down = fetch(near[48:], "z", -3)
    z_all = rows(near, far_up, far_down)
    b = rows(*ring(z_all, lambda t, d: cross(t, d, 0)))
    arrays = ring(b, lambda t, d: cross(t, d, 1))
    arrays = arrays + [fetch(t, "c", 1) for t in arrays]
    copies, at = [], 0
    for k, t in enumerate(arrays):
        copies.append((k, 0, at, t.shape[0]))
        at += t.shape[0]
    return arrays, copies


def place():
    pair, y = lax.axis_index("pair"), lax.axis_index("orb")
    return pair // 8, (pair // 2) % NX, pair % 2, y


def virtual_place(index):
    mz, mx, mc, my = place()
    device, local = index // 48, index % 48
    pair = device // NY
    dy = (device - my) % NY
    dc = (pair - mc) % 2
    dx = (pair // 2 - mx) % NX
    dz = (pair // 8 - mz) % NZ
    inner, outer = jnp.where(pair % 2 == 0, dy, dx), jnp.where(pair % 2 == 0, dx, dy)
    return dc * 6144 + outer * 1536 + inner * 384 + (dz + 1) % NZ * 48 + local


def gather_occupied(o):
    _, _, mc, my = place()
    ot = o.T
    row = jnp.zeros((32, 192), BF)
    for step, piece in enumerate(four(ot, "y")):
        row = lax.dynamic_update_slice(row, piece, (0, ((my + step) % NY) * 48))
    other = fetch(row, "c", 1)
    chip = jnp.where(mc == 0, jnp.concatenate([row, other], 1), jnp.concatenate([other, row], 1))
    mine = lax.dynamic_slice_in_dim(chip, mc * 16, 16, 0)
    cols = lambda *t: jnp.concatenate(t, axis=1)
    near = cols(fetch(mine, "z", -1), mine, fetch(mine, "z", 1))
    z_all = cols(near, fetch(near, "z", 3), fetch(near[:, 384:], "z", -3))
    mine = cols(*four(z_all, "x"))
    other = fetch(mine, "c", 1)
    return jnp.where(mc == 0, rows(mine, other), rows(other, mine))


def block_place(block):
    mz, mx, _, _ = place()
    chip = block // 3
    dx = (chip - mx) % NX
    dz = (chip // NX - mz) % NZ
    return (dx * 8 + (dz + 1) % NZ) * 3 + block % 3


def half_kernel(count, scr_ref, ints_ref, own_ref, occ_ref, out_ref):
    step = pl.program_id(0)
    firsts, coefs = [], []
    for t in range(count):
        p = step * count + t
        for s in range(8):
            m = pl.multiple_of(scr_ref[0, p, s] * BLK, BLK)
            first = jnp.dot(own_ref[:, pl.ds(m, BLK)], ints_ref[t, s], preferred_element_type=F32)
            firsts.append(first.astype(BF))
    for t in range(count):
        p = step * count + t
        coefs = []
        for s in range(8):
            n = pl.multiple_of(scr_ref[1, p, s] * BLK, BLK)
            coefs.append(occ_ref[:, pl.ds(n, BLK)])
        out_ref[t] = lax.dot_general(
            jnp.concatenate(coefs, axis=1), jnp.concatenate(firsts[8 * t : 8 * t + 8], axis=1),
            (((1,), (1,)), ((), ())), preferred_element_type=F32,
        ).astype(out_ref.dtype)


def half_transform(integrals, blocks, own, occ):
    pairs, count = integrals.shape[0], 8
    return pl.pallas_call(
        functools.partial(half_kernel, count),
        grid_spec=pltpu.PrefetchScalarGridSpec(
            num_scalar_prefetch=1,
            grid=(pairs // count,),
            in_specs=[
                pl.BlockSpec((count, 8, BLK, BLK), lambda i, s: (i, 0, 0, 0)),
                pl.BlockSpec(own.shape, lambda i, s: (0, 0)),
                pl.BlockSpec(occ.shape, lambda i, s: (0, 0)),
            ],
            out_specs=pl.BlockSpec((count, 32, own.shape[0]), lambda i, s: (i, 0, 0)),
        ),
        out_shape=jax.ShapeDtypeStruct((pairs, 32, own.shape[0]), BF),
        compiler_params=pltpu.CompilerParams(vmem_limit_bytes=56 * 1024 * 1024),
        cost_estimate=pl.CostEstimate(flops=3 * 10**8, bytes_accessed=18 * 10**6, transcendentals=0),
        name="half_transform",
    )(blocks, integrals, own, occ)


def last_kernel(copies, arrays, idx_ref, h_ref, *refs):
    pieces, out_ref = refs[:arrays], refs[arrays]
    stage, table, picked, left, right, scaled, sem = refs[arrays + 1 :]
    total, pairs = stage.shape[0], idx_ref.shape[0] // 2
    order = sorted(copies, key=lambda c: c[2])
    dma = [
        pltpu.make_async_copy(pieces[k].at[pl.ds(src, n)], stage.at[pl.ds(dst, n)], sem.at[j])
        for j, (k, src, dst, n) in enumerate(order)
    ]
    for copy in dma:
        copy.start()
    done = 0
    for part in range(6):
        end = (part + 1) * (total // 6)
        while done < len(dma) and order[done][2] < end:
            dma[done].wait()
            done += 1

        def widen(t, _, base=part * (total // 6)):
            r0 = pl.multiple_of(base + t * 64, 64)
            for c in range(4):
                block = stage[pl.ds(r0, 64), c * 128 : (c + 1) * 128].astype(F32)
                table[pl.ds(r0 * 4 + c, 64, stride=4), :] = block
            return 0

        lax.fori_loop(0, total // 6 // 64, widen, 0)
    CH = 128

    def chunk(ci, _):
        p0 = pl.multiple_of(ci * CH, CH)
        for side in range(2):

            def pick(t, _):
                base = side * pairs + p0 + t * 32
                got = [table[pl.ds(pl.multiple_of(idx_ref[base + u], 4), 4), :] for u in range(32)]
                to = pl.multiple_of((side * CH + t * 32) * 4, 128)
                for u in range(32):
                    picked[pl.ds(to + 4 * u, 4), :] = got[u]
                return 0

            lax.fori_loop(0, CH // 32, pick, 0)
        for c in range(4):
            block = picked[pl.ds(c, CH, stride=4), :]
            left[c * 128 : (c + 1) * 128, pl.ds(p0, CH)] = block.T.astype(BF)
            block = picked[pl.ds(CH * 4 + c, CH, stride=4), :]
            right[pl.ds(p0, CH), c * 128 : (c + 1) * 128] = block.astype(BF)
        return 0

    lax.fori_loop(0, pairs // CH, chunk, 0)

    def multiply(t, _):
        jk, a0 = t // 2, pl.multiple_of((t % 2) * 256, 256)
        h = h_ref[pl.ds(jk, 1), :].astype(BF)
        scaled[...] = left[pl.ds(a0, 256), :] * h
        out_ref[jk, pl.ds(a0, 256), :] = jnp.dot(scaled[...], right[...], preferred_element_type=F32).astype(BF)
        return 0

    lax.fori_loop(0, 8, multiply, 0)


def last_stage(index, h, arrays, copies):
    pairs, total = index.shape[0] // 2, sum(c[3] for c in copies)
    return pl.pallas_call(
        functools.partial(last_kernel, copies, len(arrays)),
        out_shape=jax.ShapeDtypeStruct((4, 512, 512), BF),
        in_specs=[pl.BlockSpec(memory_space=pltpu.SMEM), pl.BlockSpec(memory_space=pltpu.VMEM)]
        + [pl.BlockSpec(memory_space=pl.ANY)] * len(arrays),
        out_specs=pl.BlockSpec(memory_space=pltpu.VMEM),
        scratch_shapes=[
            pltpu.VMEM((total, 512), BF),
            pltpu.VMEM((total * 4, 128), F32),
            pltpu.VMEM((128 * 8, 128), F32),
            pltpu.VMEM((512, pairs), BF),
            pltpu.VMEM((pairs, 512), BF),
            pltpu.VMEM((256, pairs), BF),
            pltpu.SemaphoreType.DMA((len(copies),)),
        ],
        compiler_params=pltpu.CompilerParams(vmem_limit_bytes=60 * 1024 * 1024),
        cost_estimate=pl.CostEstimate(flops=9 * 10**9, bytes_accessed=15 * 10**6, transcendentals=0),
        name="gather_scale_dot",
    )(index, h, *arrays)


def stages(integrals, screen, occupied, virtual, pair_index):
    arrays, copies = gather_virtual(virtual)
    occ = gather_occupied(occupied)
    own = lax.dynamic_slice_in_dim(occ, lax.axis_index("orb") * 8, 8, 0)
    half = half_transform(integrals, block_place(screen), own, occ)
    sent = half.transpose(1, 2, 0).reshape(64, 4, half.shape[0])
    owned = lax.all_to_all(sent, "pair", 0, 0)
    h = owned.transpose(1, 0, 2).reshape(4, -1).astype(F32)
    return last_stage(virtual_place(pair_index).reshape(-1) * 4, h, arrays, copies)[None]


def solution(mesh):
    placed = (
        P("pair", None, None, None),
        P(None, "pair", None),
        P(("pair", "orb"), None),
        P(("pair", "orb"), None),
        P(),
    )
    return jax.shard_map(stages, mesh=mesh, in_specs=placed, out_specs=P("orb", "pair", None, None), check_vma=False)
```

time: 239 us -> 173 us (0.72)
  blocking collectives: 77 us -> 0 us
  local copies, waits for them, and re-layouts: 81 us -> 14 us
  starting transfers between devices: 9.26 us -> 75.9 us
  Pallas kernels: 0 us -> 42.6 us
  matrix products: 25.3 us -> 0 us
  waiting for transfers between devices: 15.9 us -> 33.6 us
  between operations: 13.5 us -> 0.42 us
  other arithmetic: 16.7 us -> 5.32 us
    all_gather x1 -> x0, blocking collectives: 77 us -> none  [body(): lax.all_gather(occupied, ('pair', 'orb'), axis=0, tiled=True)]
    ppermute x0 -> x29, starting transfers between devices: none -> 64.5 us  [the longest x18 47.2 us: fetch(): return lax.ppermute(value, 'pair', pair_moves(**{'d' + axis: step}))]
    gather x4 -> x0, local copies, waits for them, and re-layouts: 52.6 us -> none  [the longest x1 23.7 us: body(): left = vir_all[pair_index[0]]]
    pallas_call x0 -> x2, Pallas kernels: none -> 42.6 us  [the longest x1 28.8 us: last_stage(): pl.pallas_call(functools.partial(last_kernel, copies, len(arrays)), out_s...]
    ppermute x0 -> x29, waiting for transfers between devices: none -> 25.5 us  [the longest x8 13.3 us: cross(): return lax.ppermute(value, ('pair', 'orb'), moves)]
    dot_general x2 -> x0, matrix products: 25.3 us -> none  [the longest x1 14.6 us: body(): lax.dot_general(flat, right, (((0,), (0,)), ((), ())), preferred_element_...]
    convert_element_type x3 -> x1, other arithmetic: 16.7 us -> 0.02 us  [stages(): h = owned.transpose(1, 0, 2).reshape(4, -1).astype(F32)]
    unnamed x8 -> x27, local copies, waits for them, and re-layouts: 22.5 us -> 7.75 us
  transfers between devices with their start and end apart: 2 -> 30, of which waited for: 2 -> 11; matrix products, arithmetic and copies ran while one was open for 12% -> 11% of each run, Pallas kernels for 0% -> 8%
where the time goes in v2:
time: 173 us; the launch traced here: 172 us
  starting transfers between devices  75.9 us (44%)
  Pallas kernels  42.6 us (25%)
  waiting for transfers between devices  33.6 us (19%)
  local copies, waits for them, and re-layouts  14 us (8%)
  other arithmetic  5.32 us (3%)
    ppermute x18, starting transfers between devices, fetch(): return lax.ppermute(value, 'pair', pair_moves(**{'d' + axis: step}))  47.2 us
    pallas_call x1, Pallas kernels, last_stage(): pl.pallas_call(functools.partial(last_kernel, copies, len(arrays)), out_s...  28.8 us
    pallas_call x1, Pallas kernels, half_transform(): pl.pallas_call(functools.partial(half_kernel, count), grid_spec=pltpu.Pre...  13.8 us
    ppermute x8, waiting for transfers between devices, cross(): return lax.ppermute(value, ('pair', 'orb'), moves)  13.3 us
    all_to_all x1, starting transfers between devices, stages(): owned = lax.all_to_all(sent, 'pair', 0, 0)  11.4 us
    ppermute x8, starting transfers between devices, cross(): return lax.ppermute(value, ('pair', 'orb'), moves)  11.4 us
    ppermute x18, waiting for transfers between devices, fetch(): return lax.ppermute(value, 'pair', pair_moves(**{'d' + axis: step}))  11.1 us
    all_to_all x1, waiting for transfers between devices, stages(): owned = lax.all_to_all(sent, 'pair', 0, 0)  8.04 us
  transfers between devices with their start and end apart: 30, of which 11 were waited for; matrix products, arithmetic and copies ran while one was open for 11% of the time, Pallas kernels for 8%

profile of v2, /device:TPU:1, one launch (start us, length us, event | category | flops | bytes accessed | tf_op | source)
XLA Modules:
  0.0 171.8 jit_solution(3834344528571470145)
XLA Ops:
  0.0 2.1 %collective-permute-start.2 = (bf16[32,48]{1,0:T(8,128)(2,1)}, bf16[32,48]{1,0:T(8,128)(2,1)S(1)}, u32[]{:S(2)}, u32[]{:S(2)}) collective-permute-start(bf16[32,48]{1,0:T(8,128)(2,1)} %bitcast.12), channel_id=1, source_target_pairs={{3,0},{0,1},{1,2},{2,3},{7,4},{4,5},{5,6},{6,7},{11,8},{8,9},{9,10... | collective-permute-start | bytes 9224 | tf_op jit(solution)/shard_map/ppermute | solution.py:27
  2.1 2.6 %collective-permute-start.1 = (bf16[32,48]{1,0:T(8,128)(2,1)}, bf16[32,48]{1,0:T(8,128)(2,1)S(1)}, u32[]{:S(2)}, u32[]{:S(2)}) collective-permute-start(bf16[32,48]{1,0:T(8,128)(2,1)} %bitcast.13), channel_id=1, source_target_pairs={{2,0},{3,1},{0,2},{1,3},{6,4},{7,5},{4,6},{5,7},{10,8},{11,9},{8,1... | collective-permute-start | bytes 9224 | tf_op jit(solution)/shard_map/ppermute | solution.py:27
  8.7 2.2 %collective-permute-start.3 = (bf16[32,192]{1,0:T(8,128)(2,1)S(1)}, bf16[32,192]{1,0:T(8,128)(2,1)S(1)}, u32[]{:S(2)}, u32[]{:S(2)}) collective-permute-start(bf16[32,192]{1,0:T(8,128)(2,1)S(1)} %dynamic_update_slice.15), channel_id=1, source_target_pairs={{4,0},{0,4},{12,8},{8,12},{20,16},{16,20},{28,24},{24,28},{36,32},... | collective-permute-start | bytes 36872 | tf_op jit(solution)/shard_map/ppermute | solution.py:28
  11.8 5.6 %collective-permute-start.5 = (bf16[16,384]{1,0:T(8,128)(2,1)S(1)}, bf16[16,384]{1,0:T(8,128)(2,1)S(1)}, u32[]{:S(2)}, u32[]{:S(2)}) collective-permute-start(bf16[16,384]{1,0:T(8,128)(2,1)S(1)} %fusion.26), channel_id=1, source_target_pairs={{32,0},{36,4},{40,8},{44,12},{48,16},{52,20},{56,24},{60,28},{64,3... | collective-permute-start | bytes 36872 | tf_op jit(solution)/shard_map/ppermute | solution.py:28
  18.9 1.7 collective-permute-start.7
  21.4 3.5 %collective-permute-start.15 = (bf16[96,512]{1,0:T(8,128)(2,1)S(1)}, bf16[96,512]{1,0:T(8,128)(2,1)S(1)}, u32[]{:S(2)}, u32[]{:S(2)}) collective-permute-start(bf16[96,512]{1,0:T(8,128)(2,1)S(1)} %pad_maximum_fusion.1), channel_id=1, source_target_pairs={{160,0},{164,4},{168,8},{172,12},{176,16},{180,20},{184,24},{188,2... | collective-permute-start | bytes 294920 | tf_op jit(solution)/shard_map/ppermute | solution.py:28
  29.4 2.6 %collective-permute-done.14 = bf16[144,512]{1,0:T(8,128)(2,1)S(1)} collective-permute-done((bf16[144,512]{1,0:T(8,128)(2,1)S(1)}, bf16[144,512]{1,0:T(8,128)(2,1)S(1)}, u32[]{:S(2)}, u32[]{:S(2)}) %collective-permute-start.14) | collective-permute-done | bytes 147488 | tf_op jit(solution)/shard_map/ppermute | solution.py:28
  33.3 2.5 %collective-permute-start.16 = (bf16[384,512]{1,0:T(8,128)(2,1)S(1)}, bf16[384,512]{1,0:T(8,128)(2,1)S(1)}, u32[]{:S(2)}, u32[]{:S(2)}) collective-permute-start(bf16[384,512]{1,0:T(8,128)(2,1)S(1)} %get-tuple-element.7), channel_id=1, source_target_pairs={{1,0},{2,1},{3,2},{0,3},{12,4},{13,5},{14,6},{15,7},{9,8},{10,9},{... | collective-permute-start | bytes 1179656 | tf_op jit(solution)/shard_map/ppermute | solution.py:48
  35.8 3.5 %collective-permute-start.6 = (bf16[16,1152]{1,0:T(8,128)(2,1)S(1)}, bf16[16,1152]{1,0:T(8,128)(2,1)S(1)}, u32[]{:S(2)}, u32[]{:S(2)}) collective-permute-start(bf16[16,1152]{1,0:T(8,128)(2,1)S(1)} %pad_maximum_fusion.2), channel_id=1, source_target_pairs={{96,0},{100,4},{104,8},{108,12},{112,16},{116,20},{120,24},{124,28... | collective-permute-start | bytes 110600 | tf_op jit(solution)/shard_map/ppermute | solution.py:28
  40.5 3.4 %collective-permute-start.17 = (bf16[192,512]{1,0:T(8,128)(2,1)S(1)}, bf16[192,512]{1,0:T(8,128)(2,1)S(1)}, u32[]{:S(2)}, u32[]{:S(2)}) collective-permute-start(bf16[192,512]{1,0:T(8,128)(2,1)S(1)} %slice.20), channel_id=1, source_target_pairs={{1,0},{2,1},{3,2},{0,3},{12,4},{13,5},{14,6},{15,7},{9,8},{10,9},{... | collective-permute-start | bytes 589832 | tf_op jit(solution)/shard_map/ppermute | solution.py:48
  43.9 2.8 %collective-permute-done.6 = bf16[16,1152]{1,0:T(8,128)(2,1)S(1)} collective-permute-done((bf16[16,1152]{1,0:T(8,128)(2,1)S(1)}, bf16[16,1152]{1,0:T(8,128)(2,1)S(1)}, u32[]{:S(2)}, u32[]{:S(2)}) %collective-permute-start.6) | collective-permute-done | bytes 36896 | tf_op jit(solution)/shard_map/ppermute | solution.py:28
  49.0 4.2 %collective-permute-done.19 = bf16[192,512]{1,0:T(8,128)(2,1)S(1)} collective-permute-done((bf16[192,512]{1,0:T(8,128)(2,1)S(1)}, bf16[192,512]{1,0:T(8,128)(2,1)S(1)}, u32[]{:S(2)}, u32[]{:S(2)}) %collective-permute-start.19) | collective-permute-done | bytes 196640 | tf_op jit(solution)/shard_map/ppermute | solution.py:48
  54.7 2.7 %collective-permute-start.20 = (bf16[1536,512]{1,0:T(8,128)(2,1)}, bf16[1536,512]{1,0:T(8,128)(2,1)S(1)}, u32[]{:S(2)}, u32[]{:S(2)}) collective-permute-start(bf16[1536,512]{1,0:T(8,128)(2,1)} %constant_dynamic-update-slice_fusion.18.refs_0_), channel_id=1, source_target_pairs={{8,0},{9,1},{10,2},{11,3},{5,4},{6,5},{7,6},{4,7},{16,8},{17,9},{1... | collective-permute-start | bytes 4718600 | tf_op jit(solution)/shard_map/ppermute | solution.py:48
  58.9 2.0 %collective-permute-done.8 = bf16[16,3072]{1,0:T(8,128)(2,1)S(1)} collective-permute-done((bf16[16,3072]{1,0:T(8,128)(2,1)S(1)}, bf16[16,3072]{1,0:T(8,128)(2,1)S(1)}, u32[]{:S(2)}, u32[]{:S(2)}) %collective-permute-start.8) | collective-permute-done | bytes 98336 | tf_op jit(solution)/shard_map/ppermute | solution.py:28
  60.9 3.0 %collective-permute-done.9 = bf16[16,3072]{1,0:T(8,128)(2,1)S(1)} collective-permute-done((bf16[16,3072]{1,0:T(8,128)(2,1)S(1)}, bf16[16,3072]{1,0:T(8,128)(2,1)S(1)}, u32[]{:S(2)}, u32[]{:S(2)}) %collective-permute-start.9) | collective-permute-done | bytes 98336 | tf_op jit(solution)/shard_map/ppermute | solution.py:28
  63.9 24.3 %collective-permute-start.11 = (bf16[16,12288]{1,0:T(8,128)(2,1)S(1)}, bf16[16,12288]{1,0:T(8,128)(2,1)}, u32[]{:S(2)}, u32[]{:S(2)}) collective-permute-start(bf16[16,12288]{1,0:T(8,128)(2,1)S(1)} %constant_dynamic-update-slice_fusion.5), channel_id=1, source_target_pairs={{4,0},{0,4},{12,8},{8,12},{20,16},{16,20},{28,24},{24,28},{36,32},... | collective-permute-start | bytes 1179656 | tf_op jit(solution)/shard_map/ppermute | solution.py:28
  88.9 1.6 fusion.4.scr_ref
  90.8 2.7 %collective-permute-start.21 = (bf16[768,512]{1,0:T(8,128)(2,1)S(1)}, bf16[768,512]{1,0:T(8,128)(2,1)}, u32[]{:S(2)}, u32[]{:S(2)}) collective-permute-start(bf16[768,512]{1,0:T(8,128)(2,1)S(1)} %slice.22), channel_id=1, source_target_pairs={{8,0},{9,1},{10,2},{11,3},{5,4},{6,5},{7,6},{4,7},{16,8},{17,9},{1... | collective-permute-start | bytes 2359304 | tf_op jit(solution)/shard_map/ppermute | solution.py:48
  96.0 7.1 %collective-permute-done.23.refs_3_ = bf16[768,512]{1,0:T(8,128)(2,1)} collective-permute-done((bf16[768,512]{1,0:T(8,128)(2,1)S(1)}, bf16[768,512]{1,0:T(8,128)(2,1)}, u32[]{:S(2)}, u32[]{:S(2)}) %collective-permute-start.23) | collective-permute-done | bytes 786464 | tf_op jit(solution)/shard_map/ppermute | solution.py:48
  105.1 13.8 %half_transform.1 = bf16[64,32,8]{2,1,0:T(8,128)(2,1)} custom-call(s32[2,64,8]{2,1,0:T(8,128)} %fusion.4.scr_ref, bf16[64,8,128,128]{3,2,1,0:T(8,128)(2,1)} %ints_ref.1, bf16[8,12288]{1,0:T(8,128)(2,1)} %constant_dynamic-slice_fusion.own_ref, bf16[32,12288]{1,0:T(8,128)(2,1)} %copy-done), custom_call_target="tpu_custom_call" | custom-call | flops 300000000 | bytes 18000000 | tf_op jit(solution)/shard_map/half_transform/pallas_call | solution.py:138
  118.9 1.6 copy.13
  121.2 11.4 %all-to-all-start = ((bf16[64,2,128]{2,1,0:T(2,128)(2,1)}), bf16[64,2,128]{2,1,0:T(2,128)(2,1)S(1)}, u32[]{:S(2)}, u32[]{:S(2)}) async-start(bf16[64,2,128]{2,1,0:T(2,128)(2,1)} %reshape.11), calls=%async_computation | async-start | bytes 65536 | tf_op jit(solution)/shard_map/all_to_all | solution.py:246
  133.9 8.0 %all-to-all-done = bf16[64,2,128]{2,1,0:T(2,128)(2,1)S(1)} async-done(((bf16[64,2,128]{2,1,0:T(2,128)(2,1)}), bf16[64,2,128]{2,1,0:T(2,128)(2,1)S(1)}, u32[]{:S(2)}, u32[]{:S(2)}) %all-to-all-start) | async-done | bytes 32800 | tf_op jit(solution)/shard_map/all_to_all | solution.py:246
  142.9 28.8 %gather_scale_dot.1 = bf16[4,512,512]{2,1,0:T(8,128)(2,1)} custom-call(s32[8192]{0:T(1024)} %bitcast.11, f32[4,4096]{1,0:T(4,128)} %reshape.10.h_ref, bf16[1536,512]{1,0:T(8,128)(2,1)} %constant_dynamic-update-slice_fusion.18.refs_0_, bf16[1536,512]{1,0:T(8,128)(2,1)} %copy-done.2, bf16[768,512]{1,0:T(8,128)(2,1)} %collective-permute-done.21.refs_2_, ...), custom_call_target="tpu_custom_call" | custom-call | flops 8999999488 | bytes 15000000 | tf_op jit(solution)/shard_map/gather_scale_dot/pallas_call | solution.py:219
  (91 shorter events, 27.9 us)
Async XLA Ops:
  0.0 8.4 %collective-permute-start.2 = (bf16[32,48]{1,0:T(8,128)(2,1)}, bf16[32,48]{1,0:T(8,128)(2,1)S(1)}, u32[]{:S(2)}, u32[]{:S(2)}) collective-permute-start(bf16[32,48]{1,0:T(8,128)(2,1)} %bitcast.12), channel_id=1, source_target_pairs={{3,0},{0,1},{1,2},{2,3},{7,4},{4,5},{5,6},{6,7},{11,8},{8,9},{9,10... | collective-permute-start | bytes 9224 | tf_op jit(solution)/shard_map/ppermute | solution.py:27
  2.1 5.9 %collective-permute-start.1 = (bf16[32,48]{1,0:T(8,128)(2,1)}, bf16[32,48]{1,0:T(8,128)(2,1)S(1)}, u32[]{:S(2)}, u32[]{:S(2)}) collective-permute-start(bf16[32,48]{1,0:T(8,128)(2,1)} %bitcast.13), channel_id=1, source_target_pairs={{2,0},{3,1},{0,2},{1,3},{6,4},{7,5},{4,6},{5,7},{10,8},{11,9},{8,1... | collective-permute-start | bytes 9224 | tf_op jit(solution)/shard_map/ppermute | solution.py:27
  11.8 7.1 %collective-permute-start.5 = (bf16[16,384]{1,0:T(8,128)(2,1)S(1)}, bf16[16,384]{1,0:T(8,128)(2,1)S(1)}, u32[]{:S(2)}, u32[]{:S(2)}) collective-permute-start(bf16[16,384]{1,0:T(8,128)(2,1)S(1)} %fusion.26), channel_id=1, source_target_pairs={{32,0},{36,4},{40,8},{44,12},{48,16},{52,20},{56,24},{60,28},{64,3... | collective-permute-start | bytes 36872 | tf_op jit(solution)/shard_map/ppermute | solution.py:28
  18.1 6.8 %collective-permute-start.12 = (bf16[48,512]{1,0:T(8,128)(2,1)}, bf16[48,512]{1,0:T(8,128)(2,1)S(1)}, u32[]{:S(2)}, u32[]{:S(2)}) collective-permute-start(bf16[48,512]{1,0:T(8,128)(2,1)} %param.8), channel_id=1, source_target_pairs={{224,0},{228,4},{232,8},{236,12},{240,16},{244,20},{248,24},{252,2... | collective-permute-start | bytes 147464 | tf_op jit(solution)/shard_map/ppermute | solution.py:28
  18.8 16.9 %collective-permute-start.4 = (bf16[16,384]{1,0:T(8,128)(2,1)S(1)}, bf16[16,384]{1,0:T(8,128)(2,1)S(1)}, u32[]{:S(2)}, u32[]{:S(2)}) collective-permute-start(bf16[16,384]{1,0:T(8,128)(2,1)S(1)} %fusion.26), channel_id=1, source_target_pairs={{224,0},{228,4},{232,8},{236,12},{240,16},{244,20},{248,24},{252,2... | collective-permute-start | bytes 36872 | tf_op jit(solution)/shard_map/ppermute | solution.py:28
  18.9 38.5 %collective-permute-start.7 = (bf16[16,768]{1,0:T(8,128)(2,1)S(1)}, bf16[16,768]{1,0:T(8,128)(2,1)S(1)}, u32[]{:S(2)}, u32[]{:S(2)}) collective-permute-start(bf16[16,768]{1,0:T(8,128)(2,1)S(1)} %pad_maximum_fusion.3), channel_id=1, source_target_pairs={{160,0},{164,4},{168,8},{172,12},{176,16},{180,20},{184,24},{188,2... | collective-permute-start | bytes 73736 | tf_op jit(solution)/shard_map/ppermute | solution.py:28
  21.4 11.3 %collective-permute-start.15 = (bf16[96,512]{1,0:T(8,128)(2,1)S(1)}, bf16[96,512]{1,0:T(8,128)(2,1)S(1)}, u32[]{:S(2)}, u32[]{:S(2)}) collective-permute-start(bf16[96,512]{1,0:T(8,128)(2,1)S(1)} %pad_maximum_fusion.1), channel_id=1, source_target_pairs={{160,0},{164,4},{168,8},{172,12},{176,16},{180,20},{184,24},{188,2... | collective-permute-start | bytes 294920 | tf_op jit(solution)/shard_map/ppermute | solution.py:28
  25.7 6.3 %collective-permute-start.14 = (bf16[144,512]{1,0:T(8,128)(2,1)S(1)}, bf16[144,512]{1,0:T(8,128)(2,1)S(1)}, u32[]{:S(2)}, u32[]{:S(2)}) collective-permute-start(bf16[144,512]{1,0:T(8,128)(2,1)S(1)} %pad_maximum_fusion), channel_id=1, source_target_pairs={{96,0},{100,4},{104,8},{108,12},{112,16},{116,20},{120,24},{124,28... | collective-permute-start | bytes 442376 | tf_op jit(solution)/shard_map/ppermute | solution.py:28
  33.3 7.2 %collective-permute-start.16 = (bf16[384,512]{1,0:T(8,128)(2,1)S(1)}, bf16[384,512]{1,0:T(8,128)(2,1)S(1)}, u32[]{:S(2)}, u32[]{:S(2)}) collective-permute-start(bf16[384,512]{1,0:T(8,128)(2,1)S(1)} %get-tuple-element.7), channel_id=1, source_target_pairs={{1,0},{2,1},{3,2},{0,3},{12,4},{13,5},{14,6},{15,7},{9,8},{10,9},{... | collective-permute-start | bytes 1179656 | tf_op jit(solution)/shard_map/ppermute | solution.py:48
  35.8 10.9 %collective-permute-start.6 = (bf16[16,1152]{1,0:T(8,128)(2,1)S(1)}, bf16[16,1152]{1,0:T(8,128)(2,1)S(1)}, u32[]{:S(2)}, u32[]{:S(2)}) collective-permute-start(bf16[16,1152]{1,0:T(8,128)(2,1)S(1)} %pad_maximum_fusion.2), channel_id=1, source_target_pairs={{96,0},{100,4},{104,8},{108,12},{112,16},{116,20},{120,24},{124,28... | collective-permute-start | bytes 110600 | tf_op jit(solution)/shard_map/ppermute | solution.py:28
  39.2 8.1 %collective-permute-start.18 = (bf16[384,512]{1,0:T(8,128)(2,1)S(1)}, bf16[384,512]{1,0:T(8,128)(2,1)S(1)}, u32[]{:S(2)}, u32[]{:S(2)}) collective-permute-start(bf16[384,512]{1,0:T(8,128)(2,1)S(1)} %get-tuple-element.7), channel_id=1, source_target_pairs={{3,0},{0,1},{1,2},{2,3},{28,4},{29,5},{30,6},{31,7},{11,8},{8,9},{... | collective-permute-start | bytes 1179656 | tf_op jit(solution)/shard_map/ppermute | solution.py:48
  40.5 7.8 %collective-permute-start.17 = (bf16[192,512]{1,0:T(8,128)(2,1)S(1)}, bf16[192,512]{1,0:T(8,128)(2,1)S(1)}, u32[]{:S(2)}, u32[]{:S(2)}) collective-permute-start(bf16[192,512]{1,0:T(8,128)(2,1)S(1)} %slice.20), channel_id=1, source_target_pairs={{1,0},{2,1},{3,2},{0,3},{12,4},{13,5},{14,6},{15,7},{9,8},{10,9},{... | collective-permute-start | bytes 589832 | tf_op jit(solution)/shard_map/ppermute | solution.py:48
  54.7 35.9 %collective-permute-start.22 = (bf16[1536,512]{1,0:T(8,128)(2,1)}, bf16[1536,512]{1,0:T(8,128)(2,1)S(1)}, u32[]{:S(2)}, u32[]{:S(2)}) collective-permute-start(bf16[1536,512]{1,0:T(8,128)(2,1)} %constant_dynamic-update-slice_fusion.18.refs_0_), channel_id=1, source_target_pairs={{24,0},{25,1},{26,2},{27,3},{7,4},{4,5},{5,6},{6,7},{0,8},{1,9},{2... | collective-permute-start | bytes 4718600 | tf_op jit(solution)/shard_map/ppermute | solution.py:48
  54.7 36.0 %collective-permute-start.20 = (bf16[1536,512]{1,0:T(8,128)(2,1)}, bf16[1536,512]{1,0:T(8,128)(2,1)S(1)}, u32[]{:S(2)}, u32[]{:S(2)}) collective-permute-start(bf16[1536,512]{1,0:T(8,128)(2,1)} %constant_dynamic-update-slice_fusion.18.refs_0_), channel_id=1, source_target_pairs={{8,0},{9,1},{10,2},{11,3},{5,4},{6,5},{7,6},{4,7},{16,8},{17,9},{1... | collective-permute-start | bytes 4718600 | tf_op jit(solution)/shard_map/ppermute | solution.py:48
  57.5 6.4 %collective-permute-start.10 = (bf16[16,3072]{1,0:T(8,128)(2,1)S(1)}, bf16[16,3072]{1,0:T(8,128)(2,1)S(1)}, u32[]{:S(2)}, u32[]{:S(2)}) collective-permute-start(bf16[16,3072]{1,0:T(8,128)(2,1)S(1)} %get-tuple-element.17), channel_id=1, source_target_pairs={{24,0},{28,4},{0,8},{4,12},{8,16},{12,20},{16,24},{20,28},{56,32},... | collective-permute-start | bytes 294920 | tf_op jit(solution)/shard_map/ppermute | solution.py:28
  63.9 29.6 %collective-permute-start.11 = (bf16[16,12288]{1,0:T(8,128)(2,1)S(1)}, bf16[16,12288]{1,0:T(8,128)(2,1)}, u32[]{:S(2)}, u32[]{:S(2)}) collective-permute-start(bf16[16,12288]{1,0:T(8,128)(2,1)S(1)} %constant_dynamic-update-slice_fusion.5), channel_id=1, source_target_pairs={{4,0},{0,4},{12,8},{8,12},{20,16},{16,20},{28,24},{24,28},{36,32},... | collective-permute-start | bytes 1179656 | tf_op jit(solution)/shard_map/ppermute | solution.py:28
  90.6 12.5 %collective-permute-start.23 = (bf16[768,512]{1,0:T(8,128)(2,1)S(1)}, bf16[768,512]{1,0:T(8,128)(2,1)}, u32[]{:S(2)}, u32[]{:S(2)}) collective-permute-start(bf16[768,512]{1,0:T(8,128)(2,1)S(1)} %slice.23), channel_id=1, source_target_pairs={{24,0},{25,1},{26,2},{27,3},{7,4},{4,5},{5,6},{6,7},{0,8},{1,9},{2... | collective-permute-start | bytes 2359304 | tf_op jit(solution)/shard_map/ppermute | solution.py:48
  90.8 13.3 %collective-permute-start.21 = (bf16[768,512]{1,0:T(8,128)(2,1)S(1)}, bf16[768,512]{1,0:T(8,128)(2,1)}, u32[]{:S(2)}, u32[]{:S(2)}) collective-permute-start(bf16[768,512]{1,0:T(8,128)(2,1)S(1)} %slice.22), channel_id=1, source_target_pairs={{8,0},{9,1},{10,2},{11,3},{5,4},{6,5},{7,6},{4,7},{16,8},{17,9},{1... | collective-permute-start | bytes 2359304 | tf_op jit(solution)/shard_map/ppermute | solution.py:48
  94.8 48.0 %collective-permute-start.24 = (bf16[1536,512]{1,0:T(8,128)(2,1)}, bf16[1536,512]{1,0:T(8,128)(2,1)}, u32[]{:S(2)}, u32[]{:S(2)}) collective-permute-start(bf16[1536,512]{1,0:T(8,128)(2,1)} %constant_dynamic-update-slice_fusion.18.refs_0_), channel_id=1, source_target_pairs={{4,0},{0,4},{12,8},{8,12},{20,16},{16,20},{28,24},{24,28},{36,32},... | collective-permute-start | bytes 4718600 | tf_op jit(solution)/shard_map/ppermute | solution.py:28
  95.5 47.3 %collective-permute-start.28 = (bf16[1536,512]{1,0:T(8,128)(2,1)S(1)}, bf16[1536,512]{1,0:T(8,128)(2,1)}, u32[]{:S(2)}, u32[]{:S(2)}) collective-permute-start(bf16[1536,512]{1,0:T(8,128)(2,1)S(1)} %collective-permute-done.22.refs_4_), channel_id=1, source_target_pairs={{4,0},{0,4},{12,8},{8,12},{20,16},{16,20},{28,24},{24,28},{36,32},... | collective-permute-start | bytes 4718600 | tf_op jit(solution)/shard_map/ppermute | solution.py:28
  95.6 47.2 %collective-permute-start.25 = (bf16[1536,512]{1,0:T(8,128)(2,1)S(1)}, bf16[1536,512]{1,0:T(8,128)(2,1)}, u32[]{:S(2)}, u32[]{:S(2)}) collective-permute-start(bf16[1536,512]{1,0:T(8,128)(2,1)S(1)} %collective-permute-done.20.refs_1_), channel_id=1, source_target_pairs={{4,0},{0,4},{12,8},{8,12},{20,16},{16,20},{28,24},{24,28},{36,32},... | collective-permute-start | bytes 4718600 | tf_op jit(solution)/shard_map/ppermute | solution.py:28
  103.2 39.7 %collective-permute-start.27 = (bf16[768,512]{1,0:T(8,128)(2,1)}, bf16[768,512]{1,0:T(8,128)(2,1)}, u32[]{:S(2)}, u32[]{:S(2)}) collective-permute-start(bf16[768,512]{1,0:T(8,128)(2,1)} %collective-permute-done.23.refs_3_), channel_id=1, source_target_pairs={{4,0},{0,4},{12,8},{8,12},{20,16},{16,20},{28,24},{24,28},{36,32},... | collective-permute-start | bytes 2359304 | tf_op jit(solution)/shard_map/ppermute | solution.py:28
  104.1 38.8 %collective-permute-start.26 = (bf16[768,512]{1,0:T(8,128)(2,1)}, bf16[768,512]{1,0:T(8,128)(2,1)}, u32[]{:S(2)}, u32[]{:S(2)}) collective-permute-start(bf16[768,512]{1,0:T(8,128)(2,1)} %collective-permute-done.21.refs_2_), channel_id=1, source_target_pairs={{4,0},{0,4},{12,8},{8,12},{20,16},{16,20},{28,24},{24,28},{36,32},... | collective-permute-start | bytes 2359304 | tf_op jit(solution)/shard_map/ppermute | solution.py:28
  121.2 20.8 %all-to-all-start = ((bf16[64,2,128]{2,1,0:T(2,128)(2,1)}), bf16[64,2,128]{2,1,0:T(2,128)(2,1)S(1)}, u32[]{:S(2)}, u32[]{:S(2)}) async-start(bf16[64,2,128]{2,1,0:T(2,128)(2,1)} %reshape.11), calls=%async_computation | async-start | bytes 65536 | tf_op jit(solution)/shard_map/all_to_all | solution.py:246
  (11 other events, 112.0 us)

commit v3 on v2

--- a/solution.py
+++ b/solution.py
@@ -112,46 +112,62 @@
     return (dx * 8 + (dz + 1) % NZ) * 3 + block % 3
 
 
-def half_kernel(count, scr_ref, ints_ref, own_ref, occ_ref, out_ref):
-    step = pl.program_id(0)
-    firsts, coefs = [], []
-    for t in range(count):
-        p = step * count + t
-        for s in range(8):
-            m = pl.multiple_of(scr_ref[0, p, s] * BLK, BLK)
-            first = jnp.dot(own_ref[:, pl.ds(m, BLK)], ints_ref[t, s], preferred_element_type=F32)
-            firsts.append(first.astype(BF))
-    for t in range(count):
-        p = step * count + t
-        coefs = []
-        for s in range(8):
-            n = pl.multiple_of(scr_ref[1, p, s] * BLK, BLK)
-            coefs.append(occ_ref[:, pl.ds(n, BLK)])
-        out_ref[t] = lax.dot_general(
-            jnp.concatenate(coefs, axis=1), jnp.concatenate(firsts[8 * t : 8 * t + 8], axis=1),
-            (((1,), (1,)), ((), ())), preferred_element_type=F32,
-        ).astype(out_ref.dtype)
+def half_kernel(group, scr_ref, own_ref, occ_ref, ints_ref, out_ref, ints, halves, sem):
+    pairs = ints.shape[0]
+    groups = pairs // group
+
+    def copy(g):
+        part = pl.ds(g * group, group)
+        return pltpu.make_async_copy(ints_ref.at[part], ints.at[part], sem.at[g])
+
+    for g in range(groups):
+        copy(g).start()
+
+    def step(g, _):
+        copy(g).wait()
+        firsts = []
+        for t in range(group):
+            p = g * group + t
+            for s in range(8):
+                m = pl.multiple_of(scr_ref[0, p, s] * BLK, BLK)
+                first = jnp.dot(own_ref[:, pl.ds(m, BLK)], ints[p, s], preferred_element_type=F32)
+                firsts.append(first.astype(BF))
+        for t in range(group):
+            p = g * group + t
+            coefs = []
+            for s in range(8):
+                n = pl.multiple_of(scr_ref[1, p, s] * BLK, BLK)
+                coefs.append(occ_ref[:, pl.ds(n, BLK)])
+            value = lax.dot_general(
+                jnp.concatenate(firsts[8 * t : 8 * t + 8], axis=1), jnp.concatenate(coefs, axis=1),
+                (((1,), (1,)), ((), ())), preferred_element_type=F32,
+            )
+            halves[pl.ds(p, 8, stride=pairs), 0:32] = value
+        return 0
+
+    lax.fori_loop(0, groups, step, 0)
+    for i in range(8):
+        block = halves[i * pairs : (i + 1) * pairs, :].T
+        out_ref[pl.ds(i, 32, stride=8), :] = block[0:32, :]
 
 
 def half_transform(integrals, blocks, own, occ):
-    pairs, count = integrals.shape[0], 8
+    pairs, group = integrals.shape[0], 8
+    vmem = pl.BlockSpec(memory_space=pltpu.VMEM)
     return pl.pallas_call(
-        functools.partial(half_kernel, count),
-        grid_spec=pltpu.PrefetchScalarGridSpec(
-            num_scalar_prefetch=1,
-            grid=(pairs // count,),
-            in_specs=[
-                pl.BlockSpec((count, 8, BLK, BLK), lambda i, s: (i, 0, 0, 0)),
-                pl.BlockSpec(own.shape, lambda i, s: (0, 0)),
-                pl.BlockSpec(occ.shape, lambda i, s: (0, 0)),
-            ],
-            out_specs=pl.BlockSpec((count, 32, own.shape[0]), lambda i, s: (i, 0, 0)),
-        ),
-        out_shape=jax.ShapeDtypeStruct((pairs, 32, own.shape[0]), BF),
-        compiler_params=pltpu.CompilerParams(vmem_limit_bytes=56 * 1024 * 1024),
+        functools.partial(half_kernel, group),
+        in_specs=[pl.BlockSpec(memory_space=pltpu.SMEM), vmem, vmem, pl.BlockSpec(memory_space=pl.ANY)],
+        out_specs=vmem,
+        out_shape=jax.ShapeDtypeStruct((256, pairs), F32),
+        scratch_shapes=[
+            pltpu.VMEM(integrals.shape, BF),
+            pltpu.VMEM((8 * pairs, 128), F32),
+            pltpu.SemaphoreType.DMA((pairs // group,)),
+        ],
+        compiler_params=pltpu.CompilerParams(vmem_limit_bytes=48 * 1024 * 1024),
         cost_estimate=pl.CostEstimate(flops=3 * 10**8, bytes_accessed=18 * 10**6, transcendentals=0),
         name="half_transform",
-    )(blocks, integrals, own, occ)
+    )(blocks, own, occ, integrals)
 
 
 def last_kernel(copies, arrays, idx_ref, h_ref, *refs):
@@ -242,7 +258,7 @@
     occ = gather_occupied(occupied)
     own = lax.dynamic_slice_in_dim(occ, lax.axis_index("orb") * 8, 8, 0)
     half = half_transform(integrals, block_place(screen), own, occ)
-    sent = half.transpose(1, 2, 0).reshape(64, 4, half.shape[0])
+    sent = half.astype(BF).reshape(64, 4, half.shape[1])
     owned = lax.all_to_all(sent, "pair", 0, 0)
     h = owned.transpose(1, 0, 2).reshape(4, -1).astype(F32)
     return last_stage(virtual_place(pair_index).reshape(-1) * 4, h, arrays, copies)[None]

time: 173 us -> 166 us (0.960)
  Pallas kernels: 42.6 us -> 38.7 us
  local copies, waits for them, and re-layouts: 14 us -> 11.8 us
    pallas_call x1, Pallas kernels: 13.8 us -> 9.85 us  [half_transform(): pl.pallas_call(functools.partial(half_kernel, group), in_specs=[pl.BlockS...]
    unnamed x27 -> x25, local copies, waits for them, and re-layouts: 7.75 us -> 7.74 us
  transfers between devices with their start and end apart: 30 -> 30, of which waited for: 11 -> 11; matrix products, arithmetic and copies ran while one was open for 11% -> 10% of each run, Pallas kernels for 8% -> 6%
where the time goes in v3:
time: 166 us; the launch traced here: 165 us
  starting transfers between devices  75.9 us (46%)
  Pallas kernels  38.7 us (23%)
  waiting for transfers between devices  33.6 us (20%)
  local copies, waits for them, and re-layouts  11.8 us (7%)
  other arithmetic  4.71 us (3%)
    ppermute x18, starting transfers between devices, fetch(): return lax.ppermute(value, 'pair', pair_moves(**{'d' + axis: step}))  47.2 us
    pallas_call x1, Pallas kernels, last_stage(): pl.pallas_call(functools.partial(last_kernel, copies, len(arrays)), out_s...  28.8 us
    ppermute x8, waiting for transfers between devices, cross(): return lax.ppermute(value, ('pair', 'orb'), moves)  13.3 us
    all_to_all x1, starting transfers between devices, stages(): owned = lax.all_to_all(sent, 'pair', 0, 0)  11.4 us
    ppermute x8, starting transfers between devices, cross(): return lax.ppermute(value, ('pair', 'orb'), moves)  11.4 us
    ppermute x18, waiting for transfers between devices, fetch(): return lax.ppermute(value, 'pair', pair_moves(**{'d' + axis: step}))  11.1 us
    pallas_call x1, Pallas kernels, half_transform(): pl.pallas_call(functools.partial(half_kernel, group), in_specs=[pl.BlockS...  9.85 us
    all_to_all x1, waiting for transfers between devices, stages(): owned = lax.all_to_all(sent, 'pair', 0, 0)  8.03 us
  transfers between devices with their start and end apart: 30, of which 11 were waited for; matrix products, arithmetic and copies ran while one was open for 10% of the time, Pallas kernels for 6%

profile of v3, /device:TPU:1, one launch (start us, length us, event | category | flops | bytes accessed | tf_op | source)
XLA Modules:
  0.0 165.1 jit_solution(15199908779524671537)
XLA Ops:
  0.0 2.1 %collective-permute-start.2 = (bf16[32,48]{1,0:T(8,128)(2,1)}, bf16[32,48]{1,0:T(8,128)(2,1)S(1)}, u32[]{:S(2)}, u32[]{:S(2)}) collective-permute-start(bf16[32,48]{1,0:T(8,128)(2,1)} %bitcast.10), channel_id=1, source_target_pairs={{3,0},{0,1},{1,2},{2,3},{7,4},{4,5},{5,6},{6,7},{11,8},{8,9},{9,10... | collective-permute-start | bytes 9224 | tf_op jit(solution)/shard_map/ppermute | solution.py:27
  2.1 2.6 %collective-permute-start.1 = (bf16[32,48]{1,0:T(8,128)(2,1)}, bf16[32,48]{1,0:T(8,128)(2,1)S(1)}, u32[]{:S(2)}, u32[]{:S(2)}) collective-permute-start(bf16[32,48]{1,0:T(8,128)(2,1)} %bitcast.11), channel_id=1, source_target_pairs={{2,0},{3,1},{0,2},{1,3},{6,4},{7,5},{4,6},{5,7},{10,8},{11,9},{8,1... | collective-permute-start | bytes 9224 | tf_op jit(solution)/shard_map/ppermute | solution.py:27
  8.7 2.2 %collective-permute-start.3 = (bf16[32,192]{1,0:T(8,128)(2,1)S(1)}, bf16[32,192]{1,0:T(8,128)(2,1)S(1)}, u32[]{:S(2)}, u32[]{:S(2)}) collective-permute-start(bf16[32,192]{1,0:T(8,128)(2,1)S(1)} %dynamic_update_slice.15), channel_id=1, source_target_pairs={{4,0},{0,4},{12,8},{8,12},{20,16},{16,20},{28,24},{24,28},{36,32},... | collective-permute-start | bytes 36872 | tf_op jit(solution)/shard_map/ppermute | solution.py:28
  11.8 5.6 %collective-permute-start.5 = (bf16[16,384]{1,0:T(8,128)(2,1)S(1)}, bf16[16,384]{1,0:T(8,128)(2,1)S(1)}, u32[]{:S(2)}, u32[]{:S(2)}) collective-permute-start(bf16[16,384]{1,0:T(8,128)(2,1)S(1)} %fusion.26), channel_id=1, source_target_pairs={{32,0},{36,4},{40,8},{44,12},{48,16},{52,20},{56,24},{60,28},{64,3... | collective-permute-start | bytes 36872 | tf_op jit(solution)/shard_map/ppermute | solution.py:28
  18.9 1.7 %collective-permute-start.7 = (bf16[16,768]{1,0:T(8,128)(2,1)S(1)}, bf16[16,768]{1,0:T(8,128)(2,1)S(1)}, u32[]{:S(2)}, u32[]{:S(2)}) collective-permute-start(bf16[16,768]{1,0:T(8,128)(2,1)S(1)} %pad_maximum_fusion.3), channel_id=1, source_target_pairs={{160,0},{164,4},{168,8},{172,12},{176,16},{180,20},{184,24},{188,2... | collective-permute-start | bytes 73736 | tf_op jit(solution)/shard_map/ppermute | solution.py:28
  21.4 3.5 %collective-permute-start.15 = (bf16[96,512]{1,0:T(8,128)(2,1)S(1)}, bf16[96,512]{1,0:T(8,128)(2,1)S(1)}, u32[]{:S(2)}, u32[]{:S(2)}) collective-permute-start(bf16[96,512]{1,0:T(8,128)(2,1)S(1)} %pad_maximum_fusion.1), channel_id=1, source_target_pairs={{160,0},{164,4},{168,8},{172,12},{176,16},{180,20},{184,24},{188,2... | collective-permute-start | bytes 294920 | tf_op jit(solution)/shard_map/ppermute | solution.py:28
  27.4 1.4 constant_dynamic-update-slice_fusion.16
  29.4 2.6 %collective-permute-done.14 = bf16[144,512]{1,0:T(8,128)(2,1)S(1)} collective-permute-done((bf16[144,512]{1,0:T(8,128)(2,1)S(1)}, bf16[144,512]{1,0:T(8,128)(2,1)S(1)}, u32[]{:S(2)}, u32[]{:S(2)}) %collective-permute-start.14) | collective-permute-done | bytes 147488 | tf_op jit(solution)/shard_map/ppermute | solution.py:28
  33.3 2.5 %collective-permute-start.16 = (bf16[384,512]{1,0:T(8,128)(2,1)S(1)}, bf16[384,512]{1,0:T(8,128)(2,1)S(1)}, u32[]{:S(2)}, u32[]{:S(2)}) collective-permute-start(bf16[384,512]{1,0:T(8,128)(2,1)S(1)} %get-tuple-element.7), channel_id=1, source_target_pairs={{1,0},{2,1},{3,2},{0,3},{12,4},{13,5},{14,6},{15,7},{9,8},{10,9},{... | collective-permute-start | bytes 1179656 | tf_op jit(solution)/shard_map/ppermute | solution.py:48
  35.8 3.5 %collective-permute-start.6 = (bf16[16,1152]{1,0:T(8,128)(2,1)S(1)}, bf16[16,1152]{1,0:T(8,128)(2,1)S(1)}, u32[]{:S(2)}, u32[]{:S(2)}) collective-permute-start(bf16[16,1152]{1,0:T(8,128)(2,1)S(1)} %pad_maximum_fusion.2), channel_id=1, source_target_pairs={{96,0},{100,4},{104,8},{108,12},{112,16},{116,20},{120,24},{124,28... | collective-permute-start | bytes 110600 | tf_op jit(solution)/shard_map/ppermute | solution.py:28
  40.5 3.4 %collective-permute-start.17 = (bf16[192,512]{1,0:T(8,128)(2,1)S(1)}, bf16[192,512]{1,0:T(8,128)(2,1)S(1)}, u32[]{:S(2)}, u32[]{:S(2)}) collective-permute-start(bf16[192,512]{1,0:T(8,128)(2,1)S(1)} %slice.20), channel_id=1, source_target_pairs={{1,0},{2,1},{3,2},{0,3},{12,4},{13,5},{14,6},{15,7},{9,8},{10,9},{... | collective-permute-start | bytes 589832 | tf_op jit(solution)/shard_map/ppermute | solution.py:48
  43.9 2.8 %collective-permute-done.6 = bf16[16,1152]{1,0:T(8,128)(2,1)S(1)} collective-permute-done((bf16[16,1152]{1,0:T(8,128)(2,1)S(1)}, bf16[16,1152]{1,0:T(8,128)(2,1)S(1)}, u32[]{:S(2)}, u32[]{:S(2)}) %collective-permute-start.6) | collective-permute-done | bytes 36896 | tf_op jit(solution)/shard_map/ppermute | solution.py:28
  49.0 4.2 %collective-permute-done.19 = bf16[192,512]{1,0:T(8,128)(2,1)S(1)} collective-permute-done((bf16[192,512]{1,0:T(8,128)(2,1)S(1)}, bf16[192,512]{1,0:T(8,128)(2,1)S(1)}, u32[]{:S(2)}, u32[]{:S(2)}) %collective-permute-start.19) | collective-permute-done | bytes 196640 | tf_op jit(solution)/shard_map/ppermute | solution.py:48
  54.7 2.7 %collective-permute-start.20 = (bf16[1536,512]{1,0:T(8,128)(2,1)}, bf16[1536,512]{1,0:T(8,128)(2,1)S(1)}, u32[]{:S(2)}, u32[]{:S(2)}) collective-permute-start(bf16[1536,512]{1,0:T(8,128)(2,1)} %constant_dynamic-update-slice_fusion.18.refs_0_), channel_id=1, source_target_pairs={{8,0},{9,1},{10,2},{11,3},{5,4},{6,5},{7,6},{4,7},{16,8},{17,9},{1... | collective-permute-start | bytes 4718600 | tf_op jit(solution)/shard_map/ppermute | solution.py:48
  57.5 1.5 collective-permute-start.10
  58.9 2.0 %collective-permute-done.8 = bf16[16,3072]{1,0:T(8,128)(2,1)S(1)} collective-permute-done((bf16[16,3072]{1,0:T(8,128)(2,1)S(1)}, bf16[16,3072]{1,0:T(8,128)(2,1)S(1)}, u32[]{:S(2)}, u32[]{:S(2)}) %collective-permute-start.8) | collective-permute-done | bytes 98336 | tf_op jit(solution)/shard_map/ppermute | solution.py:28
  60.9 3.0 %collective-permute-done.9 = bf16[16,3072]{1,0:T(8,128)(2,1)S(1)} collective-permute-done((bf16[16,3072]{1,0:T(8,128)(2,1)S(1)}, bf16[16,3072]{1,0:T(8,128)(2,1)S(1)}, u32[]{:S(2)}, u32[]{:S(2)}) %collective-permute-start.9) | collective-permute-done | bytes 98336 | tf_op jit(solution)/shard_map/ppermute | solution.py:28
  63.9 24.3 %collective-permute-start.11 = (bf16[16,12288]{1,0:T(8,128)(2,1)S(1)}, bf16[16,12288]{1,0:T(8,128)(2,1)}, u32[]{:S(2)}, u32[]{:S(2)}) collective-permute-start(bf16[16,12288]{1,0:T(8,128)(2,1)S(1)} %constant_dynamic-update-slice_fusion.5), channel_id=1, source_target_pairs={{4,0},{0,4},{12,8},{8,12},{20,16},{16,20},{28,24},{24,28},{36,32},... | collective-permute-start | bytes 1179656 | tf_op jit(solution)/shard_map/ppermute | solution.py:28
  90.2 2.7 %collective-permute-start.21 = (bf16[768,512]{1,0:T(8,128)(2,1)S(1)}, bf16[768,512]{1,0:T(8,128)(2,1)}, u32[]{:S(2)}, u32[]{:S(2)}) collective-permute-start(bf16[768,512]{1,0:T(8,128)(2,1)S(1)} %slice.22), channel_id=1, source_target_pairs={{8,0},{9,1},{10,2},{11,3},{5,4},{6,5},{7,6},{4,7},{16,8},{17,9},{1... | collective-permute-start | bytes 2359304 | tf_op jit(solution)/shard_map/ppermute | solution.py:48
  95.5 7.1 %collective-permute-done.23.refs_3_ = bf16[768,512]{1,0:T(8,128)(2,1)} collective-permute-done((bf16[768,512]{1,0:T(8,128)(2,1)S(1)}, bf16[768,512]{1,0:T(8,128)(2,1)}, u32[]{:S(2)}, u32[]{:S(2)}) %collective-permute-start.23) | collective-permute-done | bytes 786464 | tf_op jit(solution)/shard_map/ppermute | solution.py:48
  103.9 9.8 %half_transform.1 = f32[256,64]{1,0:T(8,128)S(1)} custom-call(s32[2,64,8]{2,1,0:T(8,128)S(1)} %fusion.4.scr_ref, bf16[8,12288]{1,0:T(8,128)(2,1)S(1)} %constant_dynamic-slice_fusion.own_ref, bf16[32,12288]{1,0:T(8,128)(2,1)S(1)} %maximum_select_fusion.occ_ref, bf16[64,8,128,128]{3,2,1,0:T(8,128)(2,1)} %ints_ref.1), custom_call_target="tpu_custom_call" | custom-call | flops 300000000 | bytes 18000000 | tf_op jit(solution)/shard_map/half_transform/pallas_call | solution.py:157
  114.5 11.4 %all-to-all-start = ((bf16[64,2,128]{2,1,0:T(2,128)(2,1)}), bf16[64,2,128]{2,1,0:T(2,128)(2,1)S(1)}, u32[]{:S(2)}, u32[]{:S(2)}) async-start(bf16[64,2,128]{2,1,0:T(2,128)(2,1)} %reshape.11), calls=%async_computation | async-start | bytes 65536 | tf_op jit(solution)/shard_map/all_to_all | solution.py:262
  127.2 8.0 %all-to-all-done = bf16[64,2,128]{2,1,0:T(2,128)(2,1)S(1)} async-done(((bf16[64,2,128]{2,1,0:T(2,128)(2,1)}), bf16[64,2,128]{2,1,0:T(2,128)(2,1)S(1)}, u32[]{:S(2)}, u32[]{:S(2)}) %all-to-all-start) | async-done | bytes 32800 | tf_op jit(solution)/shard_map/all_to_all | solution.py:262
  136.2 28.8 %gather_scale_dot.1 = bf16[4,512,512]{2,1,0:T(8,128)(2,1)} custom-call(s32[8192]{0:T(1024)} %bitcast.9, f32[4,4096]{1,0:T(4,128)} %reshape.10.h_ref, bf16[1536,512]{1,0:T(8,128)(2,1)} %constant_dynamic-update-slice_fusion.18.refs_0_, bf16[1536,512]{1,0:T(8,128)(2,1)} %copy-done.1, bf16[768,512]{1,0:T(8,128)(2,1)} %collective-permute-done.21.refs_2_, ...), custom_call_target="tpu_custom_call" | custom-call | flops 8999999488 | bytes 15000000 | tf_op jit(solution)/shard_map/gather_scale_dot/pallas_call | solution.py:235
  (89 shorter events, 25.4 us)
Async XLA Ops:
  0.0 8.4 %collective-permute-start.2 = (bf16[32,48]{1,0:T(8,128)(2,1)}, bf16[32,48]{1,0:T(8,128)(2,1)S(1)}, u32[]{:S(2)}, u32[]{:S(2)}) collective-permute-start(bf16[32,48]{1,0:T(8,128)(2,1)} %bitcast.10), channel_id=1, source_target_pairs={{3,0},{0,1},{1,2},{2,3},{7,4},{4,5},{5,6},{6,7},{11,8},{8,9},{9,10... | collective-permute-start | bytes 9224 | tf_op jit(solution)/shard_map/ppermute | solution.py:27
  2.1 5.9 %collective-permute-start.1 = (bf16[32,48]{1,0:T(8,128)(2,1)}, bf16[32,48]{1,0:T(8,128)(2,1)S(1)}, u32[]{:S(2)}, u32[]{:S(2)}) collective-permute-start(bf16[32,48]{1,0:T(8,128)(2,1)} %bitcast.11), channel_id=1, source_target_pairs={{2,0},{3,1},{0,2},{1,3},{6,4},{7,5},{4,6},{5,7},{10,8},{11,9},{8,1... | collective-permute-start | bytes 9224 | tf_op jit(solution)/shard_map/ppermute | solution.py:27
  11.8 7.1 %collective-permute-start.5 = (bf16[16,384]{1,0:T(8,128)(2,1)S(1)}, bf16[16,384]{1,0:T(8,128)(2,1)S(1)}, u32[]{:S(2)}, u32[]{:S(2)}) collective-permute-start(bf16[16,384]{1,0:T(8,128)(2,1)S(1)} %fusion.26), channel_id=1, source_target_pairs={{32,0},{36,4},{40,8},{44,12},{48,16},{52,20},{56,24},{60,28},{64,3... | collective-permute-start | bytes 36872 | tf_op jit(solution)/shard_map/ppermute | solution.py:28
  18.1 6.8 %collective-permute-start.12 = (bf16[48,512]{1,0:T(8,128)(2,1)}, bf16[48,512]{1,0:T(8,128)(2,1)S(1)}, u32[]{:S(2)}, u32[]{:S(2)}) collective-permute-start(bf16[48,512]{1,0:T(8,128)(2,1)} %param.8), channel_id=1, source_target_pairs={{224,0},{228,4},{232,8},{236,12},{240,16},{244,20},{248,24},{252,2... | collective-permute-start | bytes 147464 | tf_op jit(solution)/shard_map/ppermute | solution.py:28
  18.8 16.9 %collective-permute-start.4 = (bf16[16,384]{1,0:T(8,128)(2,1)S(1)}, bf16[16,384]{1,0:T(8,128)(2,1)S(1)}, u32[]{:S(2)}, u32[]{:S(2)}) collective-permute-start(bf16[16,384]{1,0:T(8,128)(2,1)S(1)} %fusion.26), channel_id=1, source_target_pairs={{224,0},{228,4},{232,8},{236,12},{240,16},{244,20},{248,24},{252,2... | collective-permute-start | bytes 36872 | tf_op jit(solution)/shard_map/ppermute | solution.py:28
  18.9 38.5 %collective-permute-start.7 = (bf16[16,768]{1,0:T(8,128)(2,1)S(1)}, bf16[16,768]{1,0:T(8,128)(2,1)S(1)}, u32[]{:S(2)}, u32[]{:S(2)}) collective-permute-start(bf16[16,768]{1,0:T(8,128)(2,1)S(1)} %pad_maximum_fusion.3), channel_id=1, source_target_pairs={{160,0},{164,4},{168,8},{172,12},{176,16},{180,20},{184,24},{188,2... | collective-permute-start | bytes 73736 | tf_op jit(solution)/shard_map/ppermute | solution.py:28
  21.4 11.3 %collective-permute-start.15 = (bf16[96,512]{1,0:T(8,128)(2,1)S(1)}, bf16[96,512]{1,0:T(8,128)(2,1)S(1)}, u32[]{:S(2)}, u32[]{:S(2)}) collective-permute-start(bf16[96,512]{1,0:T(8,128)(2,1)S(1)} %pad_maximum_fusion.1), channel_id=1, source_target_pairs={{160,0},{164,4},{168,8},{172,12},{176,16},{180,20},{184,24},{188,2... | collective-permute-start | bytes 294920 | tf_op jit(solution)/shard_map/ppermute | solution.py:28
  25.7 6.3 %collective-permute-start.14 = (bf16[144,512]{1,0:T(8,128)(2,1)S(1)}, bf16[144,512]{1,0:T(8,128)(2,1)S(1)}, u32[]{:S(2)}, u32[]{:S(2)}) collective-permute-start(bf16[144,512]{1,0:T(8,128)(2,1)S(1)} %pad_maximum_fusion), channel_id=1, source_target_pairs={{96,0},{100,4},{104,8},{108,12},{112,16},{116,20},{120,24},{124,28... | collective-permute-start | bytes 442376 | tf_op jit(solution)/shard_map/ppermute | solution.py:28
  33.3 7.2 %collective-permute-start.16 = (bf16[384,512]{1,0:T(8,128)(2,1)S(1)}, bf16[384,512]{1,0:T(8,128)(2,1)S(1)}, u32[]{:S(2)}, u32[]{:S(2)}) collective-permute-start(bf16[384,512]{1,0:T(8,128)(2,1)S(1)} %get-tuple-element.7), channel_id=1, source_target_pairs={{1,0},{2,1},{3,2},{0,3},{12,4},{13,5},{14,6},{15,7},{9,8},{10,9},{... | collective-permute-start | bytes 1179656 | tf_op jit(solution)/shard_map/ppermute | solution.py:48
  35.8 10.9 %collective-permute-start.6 = (bf16[16,1152]{1,0:T(8,128)(2,1)S(1)}, bf16[16,1152]{1,0:T(8,128)(2,1)S(1)}, u32[]{:S(2)}, u32[]{:S(2)}) collective-permute-start(bf16[16,1152]{1,0:T(8,128)(2,1)S(1)} %pad_maximum_fusion.2), channel_id=1, source_target_pairs={{96,0},{100,4},{104,8},{108,12},{112,16},{116,20},{120,24},{124,28... | collective-permute-start | bytes 110600 | tf_op jit(solution)/shard_map/ppermute | solution.py:28
  39.3 8.1 %collective-permute-start.18 = (bf16[384,512]{1,0:T(8,128)(2,1)S(1)}, bf16[384,512]{1,0:T(8,128)(2,1)S(1)}, u32[]{:S(2)}, u32[]{:S(2)}) collective-permute-start(bf16[384,512]{1,0:T(8,128)(2,1)S(1)} %get-tuple-element.7), channel_id=1, source_target_pairs={{3,0},{0,1},{1,2},{2,3},{28,4},{29,5},{30,6},{31,7},{11,8},{8,9},{... | collective-permute-start | bytes 1179656 | tf_op jit(solution)/shard_map/ppermute | solution.py:48
  40.5 7.8 %collective-permute-start.17 = (bf16[192,512]{1,0:T(8,128)(2,1)S(1)}, bf16[192,512]{1,0:T(8,128)(2,1)S(1)}, u32[]{:S(2)}, u32[]{:S(2)}) collective-permute-start(bf16[192,512]{1,0:T(8,128)(2,1)S(1)} %slice.20), channel_id=1, source_target_pairs={{1,0},{2,1},{3,2},{0,3},{12,4},{13,5},{14,6},{15,7},{9,8},{10,9},{... | collective-permute-start | bytes 589832 | tf_op jit(solution)/shard_map/ppermute | solution.py:48
  54.7 35.3 %collective-permute-start.22 = (bf16[1536,512]{1,0:T(8,128)(2,1)}, bf16[1536,512]{1,0:T(8,128)(2,1)S(1)}, u32[]{:S(2)}, u32[]{:S(2)}) collective-permute-start(bf16[1536,512]{1,0:T(8,128)(2,1)} %constant_dynamic-update-slice_fusion.18.refs_0_), channel_id=1, source_target_pairs={{24,0},{25,1},{26,2},{27,3},{7,4},{4,5},{5,6},{6,7},{0,8},{1,9},{2... | collective-permute-start | bytes 4718600 | tf_op jit(solution)/shard_map/ppermute | solution.py:48
  54.7 35.4 %collective-permute-start.20 = (bf16[1536,512]{1,0:T(8,128)(2,1)}, bf16[1536,512]{1,0:T(8,128)(2,1)S(1)}, u32[]{:S(2)}, u32[]{:S(2)}) collective-permute-start(bf16[1536,512]{1,0:T(8,128)(2,1)} %constant_dynamic-update-slice_fusion.18.refs_0_), channel_id=1, source_target_pairs={{8,0},{9,1},{10,2},{11,3},{5,4},{6,5},{7,6},{4,7},{16,8},{17,9},{1... | collective-permute-start | bytes 4718600 | tf_op jit(solution)/shard_map/ppermute | solution.py:48
  57.5 6.4 %collective-permute-start.10 = (bf16[16,3072]{1,0:T(8,128)(2,1)S(1)}, bf16[16,3072]{1,0:T(8,128)(2,1)S(1)}, u32[]{:S(2)}, u32[]{:S(2)}) collective-permute-start(bf16[16,3072]{1,0:T(8,128)(2,1)S(1)} %get-tuple-element.17), channel_id=1, source_target_pairs={{24,0},{28,4},{0,8},{4,12},{8,16},{12,20},{16,24},{20,28},{56,32},... | collective-permute-start | bytes 294920 | tf_op jit(solution)/shard_map/ppermute | solution.py:28
  63.9 29.0 %collective-permute-start.11 = (bf16[16,12288]{1,0:T(8,128)(2,1)S(1)}, bf16[16,12288]{1,0:T(8,128)(2,1)}, u32[]{:S(2)}, u32[]{:S(2)}) collective-permute-start(bf16[16,12288]{1,0:T(8,128)(2,1)S(1)} %constant_dynamic-update-slice_fusion.5), channel_id=1, source_target_pairs={{4,0},{0,4},{12,8},{8,12},{20,16},{16,20},{28,24},{24,28},{36,32},... | collective-permute-start | bytes 1179656 | tf_op jit(solution)/shard_map/ppermute | solution.py:28
  90.1 12.5 %collective-permute-start.23 = (bf16[768,512]{1,0:T(8,128)(2,1)S(1)}, bf16[768,512]{1,0:T(8,128)(2,1)}, u32[]{:S(2)}, u32[]{:S(2)}) collective-permute-start(bf16[768,512]{1,0:T(8,128)(2,1)S(1)} %slice.23), channel_id=1, source_target_pairs={{24,0},{25,1},{26,2},{27,3},{7,4},{4,5},{5,6},{6,7},{0,8},{1,9},{2... | collective-permute-start | bytes 2359304 | tf_op jit(solution)/shard_map/ppermute | solution.py:48
  90.2 13.3 %collective-permute-start.21 = (bf16[768,512]{1,0:T(8,128)(2,1)S(1)}, bf16[768,512]{1,0:T(8,128)(2,1)}, u32[]{:S(2)}, u32[]{:S(2)}) collective-permute-start(bf16[768,512]{1,0:T(8,128)(2,1)S(1)} %slice.22), channel_id=1, source_target_pairs={{8,0},{9,1},{10,2},{11,3},{5,4},{6,5},{7,6},{4,7},{16,8},{17,9},{1... | collective-permute-start | bytes 2359304 | tf_op jit(solution)/shard_map/ppermute | solution.py:48
  94.2 41.9 %collective-permute-start.24 = (bf16[1536,512]{1,0:T(8,128)(2,1)}, bf16[1536,512]{1,0:T(8,128)(2,1)}, u32[]{:S(2)}, u32[]{:S(2)}) collective-permute-start(bf16[1536,512]{1,0:T(8,128)(2,1)} %constant_dynamic-update-slice_fusion.18.refs_0_), channel_id=1, source_target_pairs={{4,0},{0,4},{12,8},{8,12},{20,16},{16,20},{28,24},{24,28},{36,32},... | collective-permute-start | bytes 4718600 | tf_op jit(solution)/shard_map/ppermute | solution.py:28
  94.9 41.2 %collective-permute-start.28 = (bf16[1536,512]{1,0:T(8,128)(2,1)S(1)}, bf16[1536,512]{1,0:T(8,128)(2,1)}, u32[]{:S(2)}, u32[]{:S(2)}) collective-permute-start(bf16[1536,512]{1,0:T(8,128)(2,1)S(1)} %collective-permute-done.22.refs_4_), channel_id=1, source_target_pairs={{4,0},{0,4},{12,8},{8,12},{20,16},{16,20},{28,24},{24,28},{36,32},... | collective-permute-start | bytes 4718600 | tf_op jit(solution)/shard_map/ppermute | solution.py:28
  95.0 41.1 %collective-permute-start.25 = (bf16[1536,512]{1,0:T(8,128)(2,1)S(1)}, bf16[1536,512]{1,0:T(8,128)(2,1)}, u32[]{:S(2)}, u32[]{:S(2)}) collective-permute-start(bf16[1536,512]{1,0:T(8,128)(2,1)S(1)} %collective-permute-done.20.refs_1_), channel_id=1, source_target_pairs={{4,0},{0,4},{12,8},{8,12},{20,16},{16,20},{28,24},{24,28},{36,32},... | collective-permute-start | bytes 4718600 | tf_op jit(solution)/shard_map/ppermute | solution.py:28
  102.6 33.5 %collective-permute-start.27 = (bf16[768,512]{1,0:T(8,128)(2,1)}, bf16[768,512]{1,0:T(8,128)(2,1)}, u32[]{:S(2)}, u32[]{:S(2)}) collective-permute-start(bf16[768,512]{1,0:T(8,128)(2,1)} %collective-permute-done.23.refs_3_), channel_id=1, source_target_pairs={{4,0},{0,4},{12,8},{8,12},{20,16},{16,20},{28,24},{24,28},{36,32},... | collective-permute-start | bytes 2359304 | tf_op jit(solution)/shard_map/ppermute | solution.py:28
  103.5 32.6 %collective-permute-start.26 = (bf16[768,512]{1,0:T(8,128)(2,1)}, bf16[768,512]{1,0:T(8,128)(2,1)}, u32[]{:S(2)}, u32[]{:S(2)}) collective-permute-start(bf16[768,512]{1,0:T(8,128)(2,1)} %collective-permute-done.21.refs_2_), channel_id=1, source_target_pairs={{4,0},{0,4},{12,8},{8,12},{20,16},{16,20},{28,24},{24,28},{36,32},... | collective-permute-start | bytes 2359304 | tf_op jit(solution)/shard_map/ppermute | solution.py:28
  114.5 20.8 %all-to-all-start = ((bf16[64,2,128]{2,1,0:T(2,128)(2,1)}), bf16[64,2,128]{2,1,0:T(2,128)(2,1)S(1)}, u32[]{:S(2)}, u32[]{:S(2)}) async-start(bf16[64,2,128]{2,1,0:T(2,128)(2,1)} %reshape.11), calls=%async_computation | async-start | bytes 65536 | tf_op jit(solution)/shard_map/all_to_all | solution.py:262
  (10 other events, 96.2 us)

commit v4 on v3

--- a/solution.py
+++ b/solution.py
@@ -172,13 +172,16 @@
 
 def last_kernel(copies, arrays, idx_ref, h_ref, *refs):
     pieces, out_ref = refs[:arrays], refs[arrays]
-    stage, table, picked, left, right, scaled, sem = refs[arrays + 1 :]
-    total, pairs = stage.shape[0], idx_ref.shape[0] // 2
+    stage, table, picked, left, right, scaled, rows_at, sem, isem = refs[arrays + 1 :]
+    total = stage.shape[0]
     order = sorted(copies, key=lambda c: c[2])
     dma = [
         pltpu.make_async_copy(pieces[k].at[pl.ds(src, n)], stage.at[pl.ds(dst, n)], sem.at[j])
         for j, (k, src, dst, n) in enumerate(order)
     ]
+    for slot in range(2):
+        part = pl.ds(slot * 1024, 1024)
+        pltpu.make_async_copy(idx_ref.at[part], rows_at.at[part], isem.at[slot]).start()
     for copy in dma:
         copy.start()
     done = 0
@@ -196,29 +199,39 @@
             return 0
 
         lax.fori_loop(0, total // 6 // 64, widen, 0)
-    CH = 128
-
-    def chunk(ci, _):
-        p0 = pl.multiple_of(ci * CH, CH)
-        for side in range(2):
-
-            def pick(t, _):
-                base = side * pairs + p0 + t * 32
-                got = [table[pl.ds(pl.multiple_of(idx_ref[base + u], 4), 4), :] for u in range(32)]
-                to = pl.multiple_of((side * CH + t * 32) * 4, 128)
-                for u in range(32):
-                    picked[pl.ds(to + 4 * u, 4), :] = got[u]
-                return 0
-
-            lax.fori_loop(0, CH // 32, pick, 0)
+    CH, BATCH = 128, 1024
+    batches = idx_ref.shape[0] // BATCH
+
+    def indices(batch, slot):
+        part = pl.ds(pl.multiple_of(batch * BATCH, BATCH), BATCH)
+        return pltpu.make_async_copy(idx_ref.at[part], rows_at.at[pl.ds(slot * BATCH, BATCH)], isem.at[slot])
+
+    def chunk(p0, at):
+        for lo in range(0, 2 * CH, 32):
+            got = [table[pl.ds(pl.multiple_of(rows_at[at + lo + u], 4), 4), :] for u in range(32)]
+            for u in range(32):
+                picked[pl.ds((lo + u) * 4, 4), :] = got[u]
         for c in range(4):
             block = picked[pl.ds(c, CH, stride=4), :]
             left[c * 128 : (c + 1) * 128, pl.ds(p0, CH)] = block.T.astype(BF)
             block = picked[pl.ds(CH * 4 + c, CH, stride=4), :]
             right[pl.ds(p0, CH), c * 128 : (c + 1) * 128] = block.astype(BF)
+
+    def two(t, _):
+        for slot in range(2):
+            batch = 2 * t + slot
+            indices(batch, slot).wait()
+            for k in range(BATCH // (2 * CH)):
+                p0 = pl.multiple_of(batch * (BATCH // 2) + k * CH, CH)
+                chunk(p0, slot * BATCH + k * 2 * CH)
+
+            @pl.when(batch + 2 < batches)
+            def _():
+                indices(batch + 2, slot).start()
+
         return 0
 
-    lax.fori_loop(0, pairs // CH, chunk, 0)
+    lax.fori_loop(0, batches // 2, two, 0)
 
     def multiply(t, _):
         jk, a0 = t // 2, pl.multiple_of((t % 2) * 256, 256)
@@ -235,7 +248,7 @@
     return pl.pallas_call(
         functools.partial(last_kernel, copies, len(arrays)),
         out_shape=jax.ShapeDtypeStruct((4, 512, 512), BF),
-        in_specs=[pl.BlockSpec(memory_space=pltpu.SMEM), pl.BlockSpec(memory_space=pltpu.VMEM)]
+        in_specs=[pl.BlockSpec(memory_space=pl.ANY), pl.BlockSpec(memory_space=pltpu.VMEM)]
         + [pl.BlockSpec(memory_space=pl.ANY)] * len(arrays),
         out_specs=pl.BlockSpec(memory_space=pltpu.VMEM),
         scratch_shapes=[
@@ -245,7 +258,9 @@
             pltpu.VMEM((512, pairs), BF),
             pltpu.VMEM((pairs, 512), BF),
             pltpu.VMEM((256, pairs), BF),
+            pltpu.SMEM((2048,), jnp.int32),
             pltpu.SemaphoreType.DMA((len(copies),)),
+            pltpu.SemaphoreType.DMA((2,)),
         ],
         compiler_params=pltpu.CompilerParams(vmem_limit_bytes=60 * 1024 * 1024),
         cost_estimate=pl.CostEstimate(flops=9 * 10**9, bytes_accessed=15 * 10**6, transcendentals=0),
@@ -261,7 +276,8 @@
     sent = half.astype(BF).reshape(64, 4, half.shape[1])
     owned = lax.all_to_all(sent, "pair", 0, 0)
     h = owned.transpose(1, 0, 2).reshape(4, -1).astype(F32)
-    return last_stage(virtual_place(pair_index).reshape(-1) * 4, h, arrays, copies)[None]
+    index = virtual_place(pair_index).reshape(2, -1, 128).transpose(1, 0, 2).reshape(-1) * 4
+    return last_stage(index, h, arrays, copies)[None]
 
 
 def solution(mesh):

time: 166 us -> 143 us (0.86)
  starting transfers between devices: 75.9 us -> 53.2 us
  Pallas kernels: 38.7 us -> 34.5 us
  waiting for transfers between devices: 33.6 us -> 37.7 us
  local copies, waits for them, and re-layouts: 11.8 us -> 13.6 us
    ppermute x18, starting transfers between devices: 47.2 us -> 30.2 us  [fetch(): return lax.ppermute(value, 'pair', pair_moves(**{'d' + axis: step}))]
    ppermute x8, waiting for transfers between devices: 13.3 us -> 26 us  [cross(): return lax.ppermute(value, ('pair', 'orb'), moves)]
    ppermute x18, waiting for transfers between devices: 11.1 us -> 3.34 us  [fetch(): return lax.ppermute(value, 'pair', pair_moves(**{'d' + axis: step}))]
    all_to_all x1, starting transfers between devices: 11.4 us -> 6.3 us  [stages(): owned = lax.all_to_all(sent, 'pair', 0, 0)]
    pallas_call x1, Pallas kernels: 28.8 us -> 24.7 us  [last_stage(): pl.pallas_call(functools.partial(last_kernel, copies, len(arrays)), out_s...]
    unnamed x25 -> x22, local copies, waits for them, and re-layouts: 7.74 us -> 8.04 us
  transfers between devices with their start and end apart: 30 -> 30, of which waited for: 11 -> 7; matrix products, arithmetic and copies ran while one was open for 10% -> 11% of each run, Pallas kernels for 6% -> 7%
where the time goes in v4:
time: 143 us
  starting transfers between devices  53.2 us (37%)
  waiting for transfers between devices  37.7 us (26%)
  Pallas kernels  34.5 us (24%)
  local copies, waits for them, and re-layouts  13.6 us (10%)
  other arithmetic  3.33 us (2%)
    ppermute x18, starting transfers between devices, fetch(): return lax.ppermute(value, 'pair', pair_moves(**{'d' + axis: step}))  30.2 us
    ppermute x8, waiting for transfers between devices, cross(): return lax.ppermute(value, ('pair', 'orb'), moves)  26 us
    pallas_call x1, Pallas kernels, last_stage(): pl.pallas_call(functools.partial(last_kernel, copies, len(arrays)), out_s...  24.7 us
    ppermute x8, starting transfers between devices, cross(): return lax.ppermute(value, ('pair', 'orb'), moves)  10.9 us
    pallas_call x1, Pallas kernels, half_transform(): pl.pallas_call(functools.partial(half_kernel, group), in_specs=[pl.BlockS...  9.85 us
    unnamed x22, local copies, waits for them, and re-layouts  8.04 us
    all_to_all x1, waiting for transfers between devices, stages(): owned = lax.all_to_all(sent, 'pair', 0, 0)  7.17 us
    all_to_all x1, starting transfers between devices, stages(): owned = lax.all_to_all(sent, 'pair', 0, 0)  6.3 us
  transfers between devices with their start and end apart: 30, of which 7 were waited for; matrix products, arithmetic and copies ran while one was open for 11% of the time, Pallas kernels for 7%

profile of v4, /device:TPU:1, one launch (start us, length us, event | category | flops | bytes accessed | tf_op | source)
XLA Modules:
  0.0 142.8 jit_solution(8035249190630003079)
XLA Ops:
  0.0 2.1 %collective-permute-start.2 = (bf16[32,48]{1,0:T(8,128)(2,1)}, bf16[32,48]{1,0:T(8,128)(2,1)S(1)}, u32[]{:S(2)}, u32[]{:S(2)}) collective-permute-start(bf16[32,48]{1,0:T(8,128)(2,1)} %bitcast.12), channel_id=1, source_target_pairs={{3,0},{0,1},{1,2},{2,3},{7,4},{4,5},{5,6},{6,7},{11,8},{8,9},{9,10... | collective-permute-start | bytes 9224 | tf_op jit(solution)/shard_map/ppermute | solution.py:27
  2.1 2.6 %collective-permute-start.1 = (bf16[32,48]{1,0:T(8,128)(2,1)}, bf16[32,48]{1,0:T(8,128)(2,1)S(1)}, u32[]{:S(2)}, u32[]{:S(2)}) collective-permute-start(bf16[32,48]{1,0:T(8,128)(2,1)} %bitcast.13), channel_id=1, source_target_pairs={{2,0},{3,1},{0,2},{1,3},{6,4},{7,5},{4,6},{5,7},{10,8},{11,9},{8,1... | collective-permute-start | bytes 9224 | tf_op jit(solution)/shard_map/ppermute | solution.py:27
  8.7 2.2 %collective-permute-start.3 = (bf16[32,192]{1,0:T(8,128)(2,1)S(1)}, bf16[32,192]{1,0:T(8,128)(2,1)S(1)}, u32[]{:S(2)}, u32[]{:S(2)}) collective-permute-start(bf16[32,192]{1,0:T(8,128)(2,1)S(1)} %dynamic_update_slice.15), channel_id=1, source_target_pairs={{4,0},{0,4},{12,8},{8,12},{20,16},{16,20},{28,24},{24,28},{36,32},... | collective-permute-start | bytes 36872 | tf_op jit(solution)/shard_map/ppermute | solution.py:28
  11.8 5.6 %collective-permute-start.5 = (bf16[16,384]{1,0:T(8,128)(2,1)S(1)}, bf16[16,384]{1,0:T(8,128)(2,1)S(1)}, u32[]{:S(2)}, u32[]{:S(2)}) collective-permute-start(bf16[16,384]{1,0:T(8,128)(2,1)S(1)} %fusion.27), channel_id=1, source_target_pairs={{32,0},{36,4},{40,8},{44,12},{48,16},{52,20},{56,24},{60,28},{64,3... | collective-permute-start | bytes 36872 | tf_op jit(solution)/shard_map/ppermute | solution.py:28
  19.8 1.7 %collective-permute-start.7 = (bf16[16,768]{1,0:T(8,128)(2,1)S(1)}, bf16[16,768]{1,0:T(8,128)(2,1)S(1)}, u32[]{:S(2)}, u32[]{:S(2)}) collective-permute-start(bf16[16,768]{1,0:T(8,128)(2,1)S(1)} %pad_maximum_fusion.3), channel_id=1, source_target_pairs={{160,0},{164,4},{168,8},{172,12},{176,16},{180,20},{184,24},{188,2... | collective-permute-start | bytes 73736 | tf_op jit(solution)/shard_map/ppermute | solution.py:28
  21.4 2.5 %collective-permute-done.4 = bf16[16,384]{1,0:T(8,128)(2,1)S(1)} collective-permute-done((bf16[16,384]{1,0:T(8,128)(2,1)S(1)}, bf16[16,384]{1,0:T(8,128)(2,1)S(1)}, u32[]{:S(2)}, u32[]{:S(2)}) %collective-permute-start.4) | collective-permute-done | bytes 12320 | tf_op jit(solution)/shard_map/ppermute | solution.py:28
  25.2 2.8 %collective-permute-start.15 = (bf16[96,512]{1,0:T(8,128)(2,1)S(1)}, bf16[96,512]{1,0:T(8,128)(2,1)S(1)}, u32[]{:S(2)}, u32[]{:S(2)}) collective-permute-start(bf16[96,512]{1,0:T(8,128)(2,1)S(1)} %pad_maximum_fusion.1), channel_id=1, source_target_pairs={{160,0},{164,4},{168,8},{172,12},{176,16},{180,20},{184,24},{188,2... | collective-permute-start | bytes 294920 | tf_op jit(solution)/shard_map/ppermute | solution.py:28
  28.8 1.8 %collective-permute-start.14 = (bf16[144,512]{1,0:T(8,128)(2,1)S(1)}, bf16[144,512]{1,0:T(8,128)(2,1)S(1)}, u32[]{:S(2)}, u32[]{:S(2)}) collective-permute-start(bf16[144,512]{1,0:T(8,128)(2,1)S(1)} %pad_maximum_fusion), channel_id=1, source_target_pairs={{96,0},{100,4},{104,8},{108,12},{112,16},{116,20},{120,24},{124,28... | collective-permute-start | bytes 442376 | tf_op jit(solution)/shard_map/ppermute | solution.py:28
  34.6 2.5 %collective-permute-start.9 = (bf16[16,3072]{1,0:T(8,128)(2,1)S(1)}, bf16[16,3072]{1,0:T(8,128)(2,1)S(1)}, u32[]{:S(2)}, u32[]{:S(2)}) collective-permute-start(bf16[16,3072]{1,0:T(8,128)(2,1)S(1)} %get-tuple-element.17), channel_id=1, source_target_pairs={{16,0},{20,4},{24,8},{28,12},{0,16},{4,20},{8,24},{12,28},{48,32},... | collective-permute-start | bytes 294920 | tf_op jit(solution)/shard_map/ppermute | solution.py:28
  39.5 2.2 %collective-permute-start.16 = (bf16[384,512]{1,0:T(8,128)(2,1)S(1)}, bf16[384,512]{1,0:T(8,128)(2,1)S(1)}, u32[]{:S(2)}, u32[]{:S(2)}) collective-permute-start(bf16[384,512]{1,0:T(8,128)(2,1)S(1)} %get-tuple-element.7), channel_id=1, source_target_pairs={{1,0},{2,1},{3,2},{0,3},{12,4},{13,5},{14,6},{15,7},{9,8},{10,9},{... | collective-permute-start | bytes 1179656 | tf_op jit(solution)/shard_map/ppermute | solution.py:48
  41.9 5.7 %collective-permute-done.16 = bf16[384,512]{1,0:T(8,128)(2,1)S(1)} collective-permute-done((bf16[384,512]{1,0:T(8,128)(2,1)S(1)}, bf16[384,512]{1,0:T(8,128)(2,1)S(1)}, u32[]{:S(2)}, u32[]{:S(2)}) %collective-permute-start.16) | collective-permute-done | bytes 393248 | tf_op jit(solution)/shard_map/ppermute | solution.py:48
  47.6 3.1 %collective-permute-start.17 = (bf16[192,512]{1,0:T(8,128)(2,1)S(1)}, bf16[192,512]{1,0:T(8,128)(2,1)S(1)}, u32[]{:S(2)}, u32[]{:S(2)}) collective-permute-start(bf16[192,512]{1,0:T(8,128)(2,1)S(1)} %slice.20), channel_id=1, source_target_pairs={{1,0},{2,1},{3,2},{0,3},{12,4},{13,5},{14,6},{15,7},{9,8},{10,9},{... | collective-permute-start | bytes 589832 | tf_op jit(solution)/shard_map/ppermute | solution.py:48
  50.8 3.9 %collective-permute-start.11 = (bf16[16,12288]{1,0:T(8,128)(2,1)S(1)}, bf16[16,12288]{1,0:T(8,128)(2,1)S(1)}, u32[]{:S(2)}, u32[]{:S(2)}) collective-permute-start(bf16[16,12288]{1,0:T(8,128)(2,1)S(1)} %constant_dynamic-update-slice_fusion.5), channel_id=1, source_target_pairs={{4,0},{0,4},{12,8},{8,12},{20,16},{16,20},{28,24},{24,28},{36,32},... | collective-permute-start | bytes 1179656 | tf_op jit(solution)/shard_map/ppermute | solution.py:28
  56.6 4.2 %collective-permute-done.19 = bf16[192,512]{1,0:T(8,128)(2,1)S(1)} collective-permute-done((bf16[192,512]{1,0:T(8,128)(2,1)S(1)}, bf16[192,512]{1,0:T(8,128)(2,1)S(1)}, u32[]{:S(2)}, u32[]{:S(2)}) %collective-permute-start.19) | collective-permute-done | bytes 196640 | tf_op jit(solution)/shard_map/ppermute | solution.py:48
  62.2 2.7 %collective-permute-start.20 = (bf16[1536,512]{1,0:T(8,128)(2,1)}, bf16[1536,512]{1,0:T(8,128)(2,1)}, u32[]{:S(2)}, u32[]{:S(2)}) collective-permute-start(bf16[1536,512]{1,0:T(8,128)(2,1)} %constant_dynamic-update-slice_fusion.18.refs_0_), channel_id=1, source_target_pairs={{8,0},{9,1},{10,2},{11,3},{5,4},{6,5},{7,6},{4,7},{16,8},{17,9},{1... | collective-permute-start | bytes 4718600 | tf_op jit(solution)/shard_map/ppermute | solution.py:48
  65.3 1.9 %collective-permute-start.24 = (bf16[1536,512]{1,0:T(8,128)(2,1)}, bf16[1536,512]{1,0:T(8,128)(2,1)}, u32[]{:S(2)}, u32[]{:S(2)}) collective-permute-start(bf16[1536,512]{1,0:T(8,128)(2,1)} %constant_dynamic-update-slice_fusion.18.refs_0_), channel_id=1, source_target_pairs={{4,0},{0,4},{12,8},{8,12},{20,16},{16,20},{28,24},{24,28},{36,32},... | collective-permute-start | bytes 4718600 | tf_op jit(solution)/shard_map/ppermute | solution.py:28
  67.1 16.1 %collective-permute-done.22.refs_4_ = bf16[1536,512]{1,0:T(8,128)(2,1)S(1)} collective-permute-done((bf16[1536,512]{1,0:T(8,128)(2,1)}, bf16[1536,512]{1,0:T(8,128)(2,1)S(1)}, u32[]{:S(2)}, u32[]{:S(2)}) %collective-permute-start.22) | collective-permute-done | bytes 1572896 | tf_op jit(solution)/shard_map/ppermute | solution.py:48
  83.4 1.6 %slice.22 = bf16[768,512]{1,0:T(8,128)(2,1)S(1)} slice(bf16[1536,512]{1,0:T(8,128)(2,1)} %collective-permute-done.20.refs_1_), slice={[0:768], [0:512]} | slice | bytes 1572864 | tf_op jit(solution)/shard_map/slice | solution.py:54
  85.0 2.3 %collective-permute-start.21 = (bf16[768,512]{1,0:T(8,128)(2,1)S(1)}, bf16[768,512]{1,0:T(8,128)(2,1)}, u32[]{:S(2)}, u32[]{:S(2)}) collective-permute-start(bf16[768,512]{1,0:T(8,128)(2,1)S(1)} %slice.22), channel_id=1, source_target_pairs={{8,0},{9,1},{10,2},{11,3},{5,4},{6,5},{7,6},{4,7},{16,8},{17,9},{1... | collective-permute-start | bytes 2359304 | tf_op jit(solution)/shard_map/ppermute | solution.py:48
  87.3 2.6 %collective-permute-start.28 = (bf16[1536,512]{1,0:T(8,128)(2,1)S(1)}, bf16[1536,512]{1,0:T(8,128)(2,1)}, u32[]{:S(2)}, u32[]{:S(2)}) collective-permute-start(bf16[1536,512]{1,0:T(8,128)(2,1)S(1)} %collective-permute-done.22.refs_4_), channel_id=1, source_target_pairs={{4,0},{0,4},{12,8},{8,12},{20,16},{16,20},{28,24},{24,28},{36,32},... | collective-permute-start | bytes 4718600 | tf_op jit(solution)/shard_map/ppermute | solution.py:28
  90.0 9.8 %half_transform.1 = f32[256,64]{1,0:T(8,128)S(1)} custom-call(s32[2,64,8]{2,1,0:T(8,128)S(1)} %fusion.4.scr_ref, bf16[8,12288]{1,0:T(8,128)(2,1)S(1)} %constant_dynamic-slice_fusion.own_ref, bf16[32,12288]{1,0:T(8,128)(2,1)S(1)} %maximum_select_fusion.occ_ref, bf16[64,8,128,128]{3,2,1,0:T(8,128)(2,1)} %ints_ref.1), custom_call_target="tpu_custom_call" | custom-call | flops 300000000 | bytes 18000000 | tf_op jit(solution)/shard_map/half_transform/pallas_call | solution.py:157
  100.6 6.3 %all-to-all-start = ((bf16[64,2,128]{2,1,0:T(2,128)(2,1)}), bf16[64,2,128]{2,1,0:T(2,128)(2,1)S(1)}, u32[]{:S(2)}, u32[]{:S(2)}) async-start(bf16[64,2,128]{2,1,0:T(2,128)(2,1)} %reshape.14), calls=%async_computation | async-start | bytes 65536 | tf_op jit(solution)/shard_map/all_to_all | solution.py:277
  109.0 7.2 %all-to-all-done = bf16[64,2,128]{2,1,0:T(2,128)(2,1)S(1)} async-done(((bf16[64,2,128]{2,1,0:T(2,128)(2,1)}), bf16[64,2,128]{2,1,0:T(2,128)(2,1)S(1)}, u32[]{:S(2)}, u32[]{:S(2)}) %all-to-all-start) | async-done | bytes 32800 | tf_op jit(solution)/shard_map/all_to_all | solution.py:277
  118.0 24.7 %gather_scale_dot.1 = bf16[4,512,512]{2,1,0:T(8,128)(2,1)} custom-call(s32[8192]{0:T(1024)} %bitcast.11, f32[4,4096]{1,0:T(4,128)} %reshape.13.h_ref, bf16[1536,512]{1,0:T(8,128)(2,1)} %constant_dynamic-update-slice_fusion.18.refs_0_, bf16[1536,512]{1,0:T(8,128)(2,1)} %collective-permute-done.20.refs_1_, bf16[768,512]{1,0:T(8,128)(2,1)} %collective-permute-done.21.refs_2_, ...), custom_call_target="tpu_custom_call" | custom-call | flops 8999999488 | bytes 15000000 | tf_op jit(solution)/shard_map/gather_scale_dot/pallas_call | solution.py:248
  (86 shorter events, 24.3 us)
Async XLA Ops:
  0.0 8.4 %collective-permute-start.2 = (bf16[32,48]{1,0:T(8,128)(2,1)}, bf16[32,48]{1,0:T(8,128)(2,1)S(1)}, u32[]{:S(2)}, u32[]{:S(2)}) collective-permute-start(bf16[32,48]{1,0:T(8,128)(2,1)} %bitcast.12), channel_id=1, source_target_pairs={{3,0},{0,1},{1,2},{2,3},{7,4},{4,5},{5,6},{6,7},{11,8},{8,9},{9,10... | collective-permute-start | bytes 9224 | tf_op jit(solution)/shard_map/ppermute | solution.py:27
  11.8 8.0 %collective-permute-start.5 = (bf16[16,384]{1,0:T(8,128)(2,1)S(1)}, bf16[16,384]{1,0:T(8,128)(2,1)S(1)}, u32[]{:S(2)}, u32[]{:S(2)}) collective-permute-start(bf16[16,384]{1,0:T(8,128)(2,1)S(1)} %fusion.27), channel_id=1, source_target_pairs={{32,0},{36,4},{40,8},{44,12},{48,16},{52,20},{56,24},{60,28},{64,3... | collective-permute-start | bytes 36872 | tf_op jit(solution)/shard_map/ppermute | solution.py:28
  17.4 7.1 %collective-permute-start.13 = (bf16[48,512]{1,0:T(8,128)(2,1)}, bf16[48,512]{1,0:T(8,128)(2,1)S(1)}, u32[]{:S(2)}, u32[]{:S(2)}) collective-permute-start(bf16[48,512]{1,0:T(8,128)(2,1)} %param.8), channel_id=1, source_target_pairs={{32,0},{36,4},{40,8},{44,12},{48,16},{52,20},{56,24},{60,28},{64,3... | collective-permute-start | bytes 147464 | tf_op jit(solution)/shard_map/ppermute | solution.py:28
  18.1 9.9 %collective-permute-start.12 = (bf16[48,512]{1,0:T(8,128)(2,1)}, bf16[48,512]{1,0:T(8,128)(2,1)S(1)}, u32[]{:S(2)}, u32[]{:S(2)}) collective-permute-start(bf16[48,512]{1,0:T(8,128)(2,1)} %param.8), channel_id=1, source_target_pairs={{224,0},{228,4},{232,8},{236,12},{240,16},{244,20},{248,24},{252,2... | collective-permute-start | bytes 147464 | tf_op jit(solution)/shard_map/ppermute | solution.py:28
  19.8 13.5 %collective-permute-start.7 = (bf16[16,768]{1,0:T(8,128)(2,1)S(1)}, bf16[16,768]{1,0:T(8,128)(2,1)S(1)}, u32[]{:S(2)}, u32[]{:S(2)}) collective-permute-start(bf16[16,768]{1,0:T(8,128)(2,1)S(1)} %pad_maximum_fusion.3), channel_id=1, source_target_pairs={{160,0},{164,4},{168,8},{172,12},{176,16},{180,20},{184,24},{188,2... | collective-permute-start | bytes 73736 | tf_op jit(solution)/shard_map/ppermute | solution.py:28
  23.9 9.4 %collective-permute-start.6 = (bf16[16,1152]{1,0:T(8,128)(2,1)S(1)}, bf16[16,1152]{1,0:T(8,128)(2,1)S(1)}, u32[]{:S(2)}, u32[]{:S(2)}) collective-permute-start(bf16[16,1152]{1,0:T(8,128)(2,1)S(1)} %pad_maximum_fusion.2), channel_id=1, source_target_pairs={{96,0},{100,4},{104,8},{108,12},{112,16},{116,20},{120,24},{124,28... | collective-permute-start | bytes 110600 | tf_op jit(solution)/shard_map/ppermute | solution.py:28
  25.2 13.7 %collective-permute-start.15 = (bf16[96,512]{1,0:T(8,128)(2,1)S(1)}, bf16[96,512]{1,0:T(8,128)(2,1)S(1)}, u32[]{:S(2)}, u32[]{:S(2)}) collective-permute-start(bf16[96,512]{1,0:T(8,128)(2,1)S(1)} %pad_maximum_fusion.1), channel_id=1, source_target_pairs={{160,0},{164,4},{168,8},{172,12},{176,16},{180,20},{184,24},{188,2... | collective-permute-start | bytes 294920 | tf_op jit(solution)/shard_map/ppermute | solution.py:28
  28.8 9.4 %collective-permute-start.14 = (bf16[144,512]{1,0:T(8,128)(2,1)S(1)}, bf16[144,512]{1,0:T(8,128)(2,1)S(1)}, u32[]{:S(2)}, u32[]{:S(2)}) collective-permute-start(bf16[144,512]{1,0:T(8,128)(2,1)S(1)} %pad_maximum_fusion), channel_id=1, source_target_pairs={{96,0},{100,4},{104,8},{108,12},{112,16},{116,20},{120,24},{124,28... | collective-permute-start | bytes 442376 | tf_op jit(solution)/shard_map/ppermute | solution.py:28
  33.3 17.4 %collective-permute-start.10 = (bf16[16,3072]{1,0:T(8,128)(2,1)S(1)}, bf16[16,3072]{1,0:T(8,128)(2,1)S(1)}, u32[]{:S(2)}, u32[]{:S(2)}) collective-permute-start(bf16[16,3072]{1,0:T(8,128)(2,1)S(1)} %get-tuple-element.17), channel_id=1, source_target_pairs={{24,0},{28,4},{0,8},{4,12},{8,16},{12,20},{16,24},{20,28},{56,32},... | collective-permute-start | bytes 294920 | tf_op jit(solution)/shard_map/ppermute | solution.py:28
  34.6 7.3 %collective-permute-start.9 = (bf16[16,3072]{1,0:T(8,128)(2,1)S(1)}, bf16[16,3072]{1,0:T(8,128)(2,1)S(1)}, u32[]{:S(2)}, u32[]{:S(2)}) collective-permute-start(bf16[16,3072]{1,0:T(8,128)(2,1)S(1)} %get-tuple-element.17), channel_id=1, source_target_pairs={{16,0},{20,4},{24,8},{28,12},{0,16},{4,20},{8,24},{12,28},{48,32},... | collective-permute-start | bytes 294920 | tf_op jit(solution)/shard_map/ppermute | solution.py:28
  39.5 8.1 %collective-permute-start.16 = (bf16[384,512]{1,0:T(8,128)(2,1)S(1)}, bf16[384,512]{1,0:T(8,128)(2,1)S(1)}, u32[]{:S(2)}, u32[]{:S(2)}) collective-permute-start(bf16[384,512]{1,0:T(8,128)(2,1)S(1)} %get-tuple-element.7), channel_id=1, source_target_pairs={{1,0},{2,1},{3,2},{0,3},{12,4},{13,5},{14,6},{15,7},{9,8},{10,9},{... | collective-permute-start | bytes 1179656 | tf_op jit(solution)/shard_map/ppermute | solution.py:48
  41.8 12.9 %collective-permute-start.18 = (bf16[384,512]{1,0:T(8,128)(2,1)S(1)}, bf16[384,512]{1,0:T(8,128)(2,1)S(1)}, u32[]{:S(2)}, u32[]{:S(2)}) collective-permute-start(bf16[384,512]{1,0:T(8,128)(2,1)S(1)} %get-tuple-element.7), channel_id=1, source_target_pairs={{3,0},{0,1},{1,2},{2,3},{28,4},{29,5},{30,6},{31,7},{11,8},{8,9},{... | collective-permute-start | bytes 1179656 | tf_op jit(solution)/shard_map/ppermute | solution.py:48
  47.6 8.3 %collective-permute-start.17 = (bf16[192,512]{1,0:T(8,128)(2,1)S(1)}, bf16[192,512]{1,0:T(8,128)(2,1)S(1)}, u32[]{:S(2)}, u32[]{:S(2)}) collective-permute-start(bf16[192,512]{1,0:T(8,128)(2,1)S(1)} %slice.20), channel_id=1, source_target_pairs={{1,0},{2,1},{3,2},{0,3},{12,4},{13,5},{14,6},{15,7},{9,8},{10,9},{... | collective-permute-start | bytes 589832 | tf_op jit(solution)/shard_map/ppermute | solution.py:48
  50.8 14.4 %collective-permute-start.11 = (bf16[16,12288]{1,0:T(8,128)(2,1)S(1)}, bf16[16,12288]{1,0:T(8,128)(2,1)S(1)}, u32[]{:S(2)}, u32[]{:S(2)}) collective-permute-start(bf16[16,12288]{1,0:T(8,128)(2,1)S(1)} %constant_dynamic-update-slice_fusion.5), channel_id=1, source_target_pairs={{4,0},{0,4},{12,8},{8,12},{20,16},{16,20},{28,24},{24,28},{36,32},... | collective-permute-start | bytes 1179656 | tf_op jit(solution)/shard_map/ppermute | solution.py:28
  62.2 21.0 %collective-permute-start.22 = (bf16[1536,512]{1,0:T(8,128)(2,1)}, bf16[1536,512]{1,0:T(8,128)(2,1)S(1)}, u32[]{:S(2)}, u32[]{:S(2)}) collective-permute-start(bf16[1536,512]{1,0:T(8,128)(2,1)} %constant_dynamic-update-slice_fusion.18.refs_0_), channel_id=1, source_target_pairs={{24,0},{25,1},{26,2},{27,3},{7,4},{4,5},{5,6},{6,7},{0,8},{1,9},{2... | collective-permute-start | bytes 4718600 | tf_op jit(solution)/shard_map/ppermute | solution.py:48
  62.2 21.1 %collective-permute-start.20 = (bf16[1536,512]{1,0:T(8,128)(2,1)}, bf16[1536,512]{1,0:T(8,128)(2,1)}, u32[]{:S(2)}, u32[]{:S(2)}) collective-permute-start(bf16[1536,512]{1,0:T(8,128)(2,1)} %constant_dynamic-update-slice_fusion.18.refs_0_), channel_id=1, source_target_pairs={{8,0},{9,1},{10,2},{11,3},{5,4},{6,5},{7,6},{4,7},{16,8},{17,9},{1... | collective-permute-start | bytes 4718600 | tf_op jit(solution)/shard_map/ppermute | solution.py:48
  65.3 51.8 %collective-permute-start.24 = (bf16[1536,512]{1,0:T(8,128)(2,1)}, bf16[1536,512]{1,0:T(8,128)(2,1)}, u32[]{:S(2)}, u32[]{:S(2)}) collective-permute-start(bf16[1536,512]{1,0:T(8,128)(2,1)} %constant_dynamic-update-slice_fusion.18.refs_0_), channel_id=1, source_target_pairs={{4,0},{0,4},{12,8},{8,12},{20,16},{16,20},{28,24},{24,28},{36,32},... | collective-permute-start | bytes 4718600 | tf_op jit(solution)/shard_map/ppermute | solution.py:28
  83.3 23.6 %collective-permute-start.23 = (bf16[768,512]{1,0:T(8,128)(2,1)S(1)}, bf16[768,512]{1,0:T(8,128)(2,1)}, u32[]{:S(2)}, u32[]{:S(2)}) collective-permute-start(bf16[768,512]{1,0:T(8,128)(2,1)S(1)} %slice.23), channel_id=1, source_target_pairs={{24,0},{25,1},{26,2},{27,3},{7,4},{4,5},{5,6},{6,7},{0,8},{1,9},{2... | collective-permute-start | bytes 2359304 | tf_op jit(solution)/shard_map/ppermute | solution.py:48
  85.0 22.4 %collective-permute-start.21 = (bf16[768,512]{1,0:T(8,128)(2,1)S(1)}, bf16[768,512]{1,0:T(8,128)(2,1)}, u32[]{:S(2)}, u32[]{:S(2)}) collective-permute-start(bf16[768,512]{1,0:T(8,128)(2,1)S(1)} %slice.22), channel_id=1, source_target_pairs={{8,0},{9,1},{10,2},{11,3},{5,4},{6,5},{7,6},{4,7},{16,8},{17,9},{1... | collective-permute-start | bytes 2359304 | tf_op jit(solution)/shard_map/ppermute | solution.py:48
  87.3 29.8 %collective-permute-start.28 = (bf16[1536,512]{1,0:T(8,128)(2,1)S(1)}, bf16[1536,512]{1,0:T(8,128)(2,1)}, u32[]{:S(2)}, u32[]{:S(2)}) collective-permute-start(bf16[1536,512]{1,0:T(8,128)(2,1)S(1)} %collective-permute-done.22.refs_4_), channel_id=1, source_target_pairs={{4,0},{0,4},{12,8},{8,12},{20,16},{16,20},{28,24},{24,28},{36,32},... | collective-permute-start | bytes 4718600 | tf_op jit(solution)/shard_map/ppermute | solution.py:28
  89.9 27.2 %collective-permute-start.25 = (bf16[1536,512]{1,0:T(8,128)(2,1)}, bf16[1536,512]{1,0:T(8,128)(2,1)}, u32[]{:S(2)}, u32[]{:S(2)}) collective-permute-start(bf16[1536,512]{1,0:T(8,128)(2,1)} %collective-permute-done.20.refs_1_), channel_id=1, source_target_pairs={{4,0},{0,4},{12,8},{8,12},{20,16},{16,20},{28,24},{24,28},{36,32},... | collective-permute-start | bytes 4718600 | tf_op jit(solution)/shard_map/ppermute | solution.py:28
  100.6 15.6 %all-to-all-start = ((bf16[64,2,128]{2,1,0:T(2,128)(2,1)}), bf16[64,2,128]{2,1,0:T(2,128)(2,1)S(1)}, u32[]{:S(2)}, u32[]{:S(2)}) async-start(bf16[64,2,128]{2,1,0:T(2,128)(2,1)} %reshape.14), calls=%async_computation | async-start | bytes 65536 | tf_op jit(solution)/shard_map/all_to_all | solution.py:277
  106.9 10.2 %collective-permute-start.27 = (bf16[768,512]{1,0:T(8,128)(2,1)}, bf16[768,512]{1,0:T(8,128)(2,1)}, u32[]{:S(2)}, u32[]{:S(2)}) collective-permute-start(bf16[768,512]{1,0:T(8,128)(2,1)} %collective-permute-done.23.refs_3_), channel_id=1, source_target_pairs={{4,0},{0,4},{12,8},{8,12},{20,16},{16,20},{28,24},{24,28},{36,32},... | collective-permute-start | bytes 2359304 | tf_op jit(solution)/shard_map/ppermute | solution.py:28
  107.4 9.6 %collective-permute-start.26 = (bf16[768,512]{1,0:T(8,128)(2,1)}, bf16[768,512]{1,0:T(8,128)(2,1)S(1)}, u32[]{:S(2)}, u32[]{:S(2)}) collective-permute-start(bf16[768,512]{1,0:T(8,128)(2,1)} %collective-permute-done.21.refs_2_), channel_id=1, source_target_pairs={{4,0},{0,4},{12,8},{8,12},{20,16},{16,20},{28,24},{24,28},{36,32},... | collective-permute-start | bytes 2359304 | tf_op jit(solution)/shard_map/ppermute | solution.py:28
  (9 other events, 49.8 us)

commit v5 on v4

--- a/solution.py
+++ b/solution.py
@@ -56,9 +56,9 @@
 
 
 def gather_virtual(v):
-    near = rows(fetch(v, "z", -1), v, fetch(v, "z", 1))
-    far_up = fetch(near, "z", 3)
-    far_down = fetch(near[48:], "z", -3)
+    up, down = fetch(v, "z", 1), fetch(v, "z", -1)
+    near = rows(down, v, up)
+    far_up, far_down = fetch(near, "z", 3), fetch(near[48:], "z", -3)
     z_all = rows(near, far_up, far_down)
     b = rows(*ring(z_all, lambda t, d: cross(t, d, 0)))
     arrays = ring(b, lambda t, d: cross(t, d, 1))
@@ -91,14 +91,16 @@
     _, _, mc, my = place()
     ot = o.T
     row = jnp.zeros((32, 192), BF)
-    for step, piece in enumerate(four(ot, "y")):
+    pieces = four(ot, "y")
+    for step, piece in enumerate(pieces):
         row = lax.dynamic_update_slice(row, piece, (0, ((my + step) % NY) * 48))
     other = fetch(row, "c", 1)
     chip = jnp.where(mc == 0, jnp.concatenate([row, other], 1), jnp.concatenate([other, row], 1))
     mine = lax.dynamic_slice_in_dim(chip, mc * 16, 16, 0)
     cols = lambda *t: jnp.concatenate(t, axis=1)
     near = cols(fetch(mine, "z", -1), mine, fetch(mine, "z", 1))
-    z_all = cols(near, fetch(near, "z", 3), fetch(near[:, 384:], "z", -3))
+    far_up, far_down = fetch(near, "z", 3), fetch(near[:, 384:], "z", -3)
+    z_all = cols(near, far_up, far_down)
     mine = cols(*four(z_all, "x"))
     other = fetch(mine, "c", 1)
     return jnp.where(mc == 0, rows(mine, other), rows(other, mine))

time: 143 us -> 143 us (level)
  no operation moved by 1% of the time
where the time goes in v5:
time: 143 us
  starting transfers between devices  53.2 us (37%)
  waiting for transfers between devices  37.7 us (26%)
  Pallas kernels  34.5 us (24%)
  local copies, waits for them, and re-layouts  13.6 us (10%)
  other arithmetic  3.33 us (2%)
    ppermute x18, starting transfers between devices, fetch(): return lax.ppermute(value, 'pair', pair_moves(**{'d' + axis: step}))  30.2 us
    ppermute x8, waiting for transfers between devices, cross(): return lax.ppermute(value, ('pair', 'orb'), moves)  26 us
    pallas_call x1, Pallas kernels, last_stage(): pl.pallas_call(functools.partial(last_kernel, copies, len(arrays)), out_s...  24.7 us
    ppermute x8, starting transfers between devices, cross(): return lax.ppermute(value, ('pair', 'orb'), moves)  10.9 us
    pallas_call x1, Pallas kernels, half_transform(): pl.pallas_call(functools.partial(half_kernel, group), in_specs=[pl.BlockS...  9.85 us
    unnamed x22, local copies, waits for them, and re-layouts  8.04 us
    all_to_all x1, waiting for transfers between devices, stages(): owned = lax.all_to_all(sent, 'pair', 0, 0)  7.17 us
    all_to_all x1, starting transfers between devices, stages(): owned = lax.all_to_all(sent, 'pair', 0, 0)  6.3 us
  transfers between devices with their start and end apart: 30, of which 7 were waited for; matrix products, arithmetic and copies ran while one was open for 11% of the time, Pallas kernels for 7%

profile of v5, /device:TPU:1, one launch (start us, length us, event | category | flops | bytes accessed | tf_op | source)
XLA Modules:
  0.0 142.8 jit_solution(8035249190630003079)
XLA Ops:
  0.0 2.1 %collective-permute-start.2 = (bf16[32,48]{1,0:T(8,128)(2,1)}, bf16[32,48]{1,0:T(8,128)(2,1)S(1)}, u32[]{:S(2)}, u32[]{:S(2)}) collective-permute-start(bf16[32,48]{1,0:T(8,128)(2,1)} %bitcast.12), channel_id=1, source_target_pairs={{3,0},{0,1},{1,2},{2,3},{7,4},{4,5},{5,6},{6,7},{11,8},{8,9},{9,10... | collective-permute-start | bytes 9224 | tf_op jit(solution)/shard_map/ppermute | solution.py:27
  2.1 2.6 %collective-permute-start.1 = (bf16[32,48]{1,0:T(8,128)(2,1)}, bf16[32,48]{1,0:T(8,128)(2,1)S(1)}, u32[]{:S(2)}, u32[]{:S(2)}) collective-permute-start(bf16[32,48]{1,0:T(8,128)(2,1)} %bitcast.13), channel_id=1, source_target_pairs={{2,0},{3,1},{0,2},{1,3},{6,4},{7,5},{4,6},{5,7},{10,8},{11,9},{8,1... | collective-permute-start | bytes 9224 | tf_op jit(solution)/shard_map/ppermute | solution.py:27
  8.7 2.2 %collective-permute-start.3 = (bf16[32,192]{1,0:T(8,128)(2,1)S(1)}, bf16[32,192]{1,0:T(8,128)(2,1)S(1)}, u32[]{:S(2)}, u32[]{:S(2)}) collective-permute-start(bf16[32,192]{1,0:T(8,128)(2,1)S(1)} %dynamic_update_slice.15), channel_id=1, source_target_pairs={{4,0},{0,4},{12,8},{8,12},{20,16},{16,20},{28,24},{24,28},{36,32},... | collective-permute-start | bytes 36872 | tf_op jit(solution)/shard_map/ppermute | solution.py:28
  11.8 5.6 %collective-permute-start.5 = (bf16[16,384]{1,0:T(8,128)(2,1)S(1)}, bf16[16,384]{1,0:T(8,128)(2,1)S(1)}, u32[]{:S(2)}, u32[]{:S(2)}) collective-permute-start(bf16[16,384]{1,0:T(8,128)(2,1)S(1)} %fusion.27), channel_id=1, source_target_pairs={{32,0},{36,4},{40,8},{44,12},{48,16},{52,20},{56,24},{60,28},{64,3... | collective-permute-start | bytes 36872 | tf_op jit(solution)/shard_map/ppermute | solution.py:28
  19.8 1.7 %collective-permute-start.7 = (bf16[16,768]{1,0:T(8,128)(2,1)S(1)}, bf16[16,768]{1,0:T(8,128)(2,1)S(1)}, u32[]{:S(2)}, u32[]{:S(2)}) collective-permute-start(bf16[16,768]{1,0:T(8,128)(2,1)S(1)} %pad_maximum_fusion.3), channel_id=1, source_target_pairs={{160,0},{164,4},{168,8},{172,12},{176,16},{180,20},{184,24},{188,2... | collective-permute-start | bytes 73736 | tf_op jit(solution)/shard_map/ppermute | solution.py:28
  21.4 2.5 %collective-permute-done.4 = bf16[16,384]{1,0:T(8,128)(2,1)S(1)} collective-permute-done((bf16[16,384]{1,0:T(8,128)(2,1)S(1)}, bf16[16,384]{1,0:T(8,128)(2,1)S(1)}, u32[]{:S(2)}, u32[]{:S(2)}) %collective-permute-start.4) | collective-permute-done | bytes 12320 | tf_op jit(solution)/shard_map/ppermute | solution.py:28
  25.2 2.8 %collective-permute-start.15 = (bf16[96,512]{1,0:T(8,128)(2,1)S(1)}, bf16[96,512]{1,0:T(8,128)(2,1)S(1)}, u32[]{:S(2)}, u32[]{:S(2)}) collective-permute-start(bf16[96,512]{1,0:T(8,128)(2,1)S(1)} %pad_maximum_fusion.1), channel_id=1, source_target_pairs={{160,0},{164,4},{168,8},{172,12},{176,16},{180,20},{184,24},{188,2... | collective-permute-start | bytes 294920 | tf_op jit(solution)/shard_map/ppermute | solution.py:28
  28.8 1.8 %collective-permute-start.14 = (bf16[144,512]{1,0:T(8,128)(2,1)S(1)}, bf16[144,512]{1,0:T(8,128)(2,1)S(1)}, u32[]{:S(2)}, u32[]{:S(2)}) collective-permute-start(bf16[144,512]{1,0:T(8,128)(2,1)S(1)} %pad_maximum_fusion), channel_id=1, source_target_pairs={{96,0},{100,4},{104,8},{108,12},{112,16},{116,20},{120,24},{124,28... | collective-permute-start | bytes 442376 | tf_op jit(solution)/shard_map/ppermute | solution.py:28
  34.6 2.5 %collective-permute-start.9 = (bf16[16,3072]{1,0:T(8,128)(2,1)S(1)}, bf16[16,3072]{1,0:T(8,128)(2,1)S(1)}, u32[]{:S(2)}, u32[]{:S(2)}) collective-permute-start(bf16[16,3072]{1,0:T(8,128)(2,1)S(1)} %get-tuple-element.17), channel_id=1, source_target_pairs={{16,0},{20,4},{24,8},{28,12},{0,16},{4,20},{8,24},{12,28},{48,32},... | collective-permute-start | bytes 294920 | tf_op jit(solution)/shard_map/ppermute | solution.py:28
  39.5 2.2 %collective-permute-start.16 = (bf16[384,512]{1,0:T(8,128)(2,1)S(1)}, bf16[384,512]{1,0:T(8,128)(2,1)S(1)}, u32[]{:S(2)}, u32[]{:S(2)}) collective-permute-start(bf16[384,512]{1,0:T(8,128)(2,1)S(1)} %get-tuple-element.7), channel_id=1, source_target_pairs={{1,0},{2,1},{3,2},{0,3},{12,4},{13,5},{14,6},{15,7},{9,8},{10,9},{... | collective-permute-start | bytes 1179656 | tf_op jit(solution)/shard_map/ppermute | solution.py:48
  41.9 5.7 %collective-permute-done.16 = bf16[384,512]{1,0:T(8,128)(2,1)S(1)} collective-permute-done((bf16[384,512]{1,0:T(8,128)(2,1)S(1)}, bf16[384,512]{1,0:T(8,128)(2,1)S(1)}, u32[]{:S(2)}, u32[]{:S(2)}) %collective-permute-start.16) | collective-permute-done | bytes 393248 | tf_op jit(solution)/shard_map/ppermute | solution.py:48
  47.6 3.1 %collective-permute-start.17 = (bf16[192,512]{1,0:T(8,128)(2,1)S(1)}, bf16[192,512]{1,0:T(8,128)(2,1)S(1)}, u32[]{:S(2)}, u32[]{:S(2)}) collective-permute-start(bf16[192,512]{1,0:T(8,128)(2,1)S(1)} %slice.20), channel_id=1, source_target_pairs={{1,0},{2,1},{3,2},{0,3},{12,4},{13,5},{14,6},{15,7},{9,8},{10,9},{... | collective-permute-start | bytes 589832 | tf_op jit(solution)/shard_map/ppermute | solution.py:48
  50.8 3.9 %collective-permute-start.11 = (bf16[16,12288]{1,0:T(8,128)(2,1)S(1)}, bf16[16,12288]{1,0:T(8,128)(2,1)S(1)}, u32[]{:S(2)}, u32[]{:S(2)}) collective-permute-start(bf16[16,12288]{1,0:T(8,128)(2,1)S(1)} %constant_dynamic-update-slice_fusion.5), channel_id=1, source_target_pairs={{4,0},{0,4},{12,8},{8,12},{20,16},{16,20},{28,24},{24,28},{36,32},... | collective-permute-start | bytes 1179656 | tf_op jit(solution)/shard_map/ppermute | solution.py:28
  56.6 4.2 %collective-permute-done.19 = bf16[192,512]{1,0:T(8,128)(2,1)S(1)} collective-permute-done((bf16[192,512]{1,0:T(8,128)(2,1)S(1)}, bf16[192,512]{1,0:T(8,128)(2,1)S(1)}, u32[]{:S(2)}, u32[]{:S(2)}) %collective-permute-start.19) | collective-permute-done | bytes 196640 | tf_op jit(solution)/shard_map/ppermute | solution.py:48
  62.2 2.7 %collective-permute-start.20 = (bf16[1536,512]{1,0:T(8,128)(2,1)}, bf16[1536,512]{1,0:T(8,128)(2,1)}, u32[]{:S(2)}, u32[]{:S(2)}) collective-permute-start(bf16[1536,512]{1,0:T(8,128)(2,1)} %constant_dynamic-update-slice_fusion.18.refs_0_), channel_id=1, source_target_pairs={{8,0},{9,1},{10,2},{11,3},{5,4},{6,5},{7,6},{4,7},{16,8},{17,9},{1... | collective-permute-start | bytes 4718600 | tf_op jit(solution)/shard_map/ppermute | solution.py:48
  65.3 1.9 %collective-permute-start.24 = (bf16[1536,512]{1,0:T(8,128)(2,1)}, bf16[1536,512]{1,0:T(8,128)(2,1)}, u32[]{:S(2)}, u32[]{:S(2)}) collective-permute-start(bf16[1536,512]{1,0:T(8,128)(2,1)} %constant_dynamic-update-slice_fusion.18.refs_0_), channel_id=1, source_target_pairs={{4,0},{0,4},{12,8},{8,12},{20,16},{16,20},{28,24},{24,28},{36,32},... | collective-permute-start | bytes 4718600 | tf_op jit(solution)/shard_map/ppermute | solution.py:28
  67.1 16.1 %collective-permute-done.22.refs_4_ = bf16[1536,512]{1,0:T(8,128)(2,1)S(1)} collective-permute-done((bf16[1536,512]{1,0:T(8,128)(2,1)}, bf16[1536,512]{1,0:T(8,128)(2,1)S(1)}, u32[]{:S(2)}, u32[]{:S(2)}) %collective-permute-start.22) | collective-permute-done | bytes 1572896 | tf_op jit(solution)/shard_map/ppermute | solution.py:48
  83.4 1.6 %slice.22 = bf16[768,512]{1,0:T(8,128)(2,1)S(1)} slice(bf16[1536,512]{1,0:T(8,128)(2,1)} %collective-permute-done.20.refs_1_), slice={[0:768], [0:512]} | slice | bytes 1572864 | tf_op jit(solution)/shard_map/slice | solution.py:54
  85.0 2.3 %collective-permute-start.21 = (bf16[768,512]{1,0:T(8,128)(2,1)S(1)}, bf16[768,512]{1,0:T(8,128)(2,1)}, u32[]{:S(2)}, u32[]{:S(2)}) collective-permute-start(bf16[768,512]{1,0:T(8,128)(2,1)S(1)} %slice.22), channel_id=1, source_target_pairs={{8,0},{9,1},{10,2},{11,3},{5,4},{6,5},{7,6},{4,7},{16,8},{17,9},{1... | collective-permute-start | bytes 2359304 | tf_op jit(solution)/shard_map/ppermute | solution.py:48
  87.3 2.6 %collective-permute-start.28 = (bf16[1536,512]{1,0:T(8,128)(2,1)S(1)}, bf16[1536,512]{1,0:T(8,128)(2,1)}, u32[]{:S(2)}, u32[]{:S(2)}) collective-permute-start(bf16[1536,512]{1,0:T(8,128)(2,1)S(1)} %collective-permute-done.22.refs_4_), channel_id=1, source_target_pairs={{4,0},{0,4},{12,8},{8,12},{20,16},{16,20},{28,24},{24,28},{36,32},... | collective-permute-start | bytes 4718600 | tf_op jit(solution)/shard_map/ppermute | solution.py:28
  90.0 9.8 %half_transform.1 = f32[256,64]{1,0:T(8,128)S(1)} custom-call(s32[2,64,8]{2,1,0:T(8,128)S(1)} %fusion.4.scr_ref, bf16[8,12288]{1,0:T(8,128)(2,1)S(1)} %constant_dynamic-slice_fusion.own_ref, bf16[32,12288]{1,0:T(8,128)(2,1)S(1)} %maximum_select_fusion.occ_ref, bf16[64,8,128,128]{3,2,1,0:T(8,128)(2,1)} %ints_ref.1), custom_call_target="tpu_custom_call" | custom-call | flops 300000000 | bytes 18000000 | tf_op jit(solution)/shard_map/half_transform/pallas_call | solution.py:159
  100.6 6.3 %all-to-all-start = ((bf16[64,2,128]{2,1,0:T(2,128)(2,1)}), bf16[64,2,128]{2,1,0:T(2,128)(2,1)S(1)}, u32[]{:S(2)}, u32[]{:S(2)}) async-start(bf16[64,2,128]{2,1,0:T(2,128)(2,1)} %reshape.14), calls=%async_computation | async-start | bytes 65536 | tf_op jit(solution)/shard_map/all_to_all | solution.py:279
  109.0 7.2 %all-to-all-done = bf16[64,2,128]{2,1,0:T(2,128)(2,1)S(1)} async-done(((bf16[64,2,128]{2,1,0:T(2,128)(2,1)}), bf16[64,2,128]{2,1,0:T(2,128)(2,1)S(1)}, u32[]{:S(2)}, u32[]{:S(2)}) %all-to-all-start) | async-done | bytes 32800 | tf_op jit(solution)/shard_map/all_to_all | solution.py:279
  118.0 24.7 %gather_scale_dot.1 = bf16[4,512,512]{2,1,0:T(8,128)(2,1)} custom-call(s32[8192]{0:T(1024)} %bitcast.11, f32[4,4096]{1,0:T(4,128)} %reshape.13.h_ref, bf16[1536,512]{1,0:T(8,128)(2,1)} %constant_dynamic-update-slice_fusion.18.refs_0_, bf16[1536,512]{1,0:T(8,128)(2,1)} %collective-permute-done.20.refs_1_, bf16[768,512]{1,0:T(8,128)(2,1)} %collective-permute-done.21.refs_2_, ...), custom_call_target="tpu_custom_call" | custom-call | flops 8999999488 | bytes 15000000 | tf_op jit(solution)/shard_map/gather_scale_dot/pallas_call | solution.py:250
  (86 shorter events, 24.3 us)
Async XLA Ops:
  0.0 8.4 %collective-permute-start.2 = (bf16[32,48]{1,0:T(8,128)(2,1)}, bf16[32,48]{1,0:T(8,128)(2,1)S(1)}, u32[]{:S(2)}, u32[]{:S(2)}) collective-permute-start(bf16[32,48]{1,0:T(8,128)(2,1)} %bitcast.12), channel_id=1, source_target_pairs={{3,0},{0,1},{1,2},{2,3},{7,4},{4,5},{5,6},{6,7},{11,8},{8,9},{9,10... | collective-permute-start | bytes 9224 | tf_op jit(solution)/shard_map/ppermute | solution.py:27
  11.8 8.0 %collective-permute-start.5 = (bf16[16,384]{1,0:T(8,128)(2,1)S(1)}, bf16[16,384]{1,0:T(8,128)(2,1)S(1)}, u32[]{:S(2)}, u32[]{:S(2)}) collective-permute-start(bf16[16,384]{1,0:T(8,128)(2,1)S(1)} %fusion.27), channel_id=1, source_target_pairs={{32,0},{36,4},{40,8},{44,12},{48,16},{52,20},{56,24},{60,28},{64,3... | collective-permute-start | bytes 36872 | tf_op jit(solution)/shard_map/ppermute | solution.py:28
  17.4 7.1 %collective-permute-start.13 = (bf16[48,512]{1,0:T(8,128)(2,1)}, bf16[48,512]{1,0:T(8,128)(2,1)S(1)}, u32[]{:S(2)}, u32[]{:S(2)}) collective-permute-start(bf16[48,512]{1,0:T(8,128)(2,1)} %param.8), channel_id=1, source_target_pairs={{32,0},{36,4},{40,8},{44,12},{48,16},{52,20},{56,24},{60,28},{64,3... | collective-permute-start | bytes 147464 | tf_op jit(solution)/shard_map/ppermute | solution.py:28
  18.1 9.9 %collective-permute-start.12 = (bf16[48,512]{1,0:T(8,128)(2,1)}, bf16[48,512]{1,0:T(8,128)(2,1)S(1)}, u32[]{:S(2)}, u32[]{:S(2)}) collective-permute-start(bf16[48,512]{1,0:T(8,128)(2,1)} %param.8), channel_id=1, source_target_pairs={{224,0},{228,4},{232,8},{236,12},{240,16},{244,20},{248,24},{252,2... | collective-permute-start | bytes 147464 | tf_op jit(solution)/shard_map/ppermute | solution.py:28
  19.8 13.5 %collective-permute-start.7 = (bf16[16,768]{1,0:T(8,128)(2,1)S(1)}, bf16[16,768]{1,0:T(8,128)(2,1)S(1)}, u32[]{:S(2)}, u32[]{:S(2)}) collective-permute-start(bf16[16,768]{1,0:T(8,128)(2,1)S(1)} %pad_maximum_fusion.3), channel_id=1, source_target_pairs={{160,0},{164,4},{168,8},{172,12},{176,16},{180,20},{184,24},{188,2... | collective-permute-start | bytes 73736 | tf_op jit(solution)/shard_map/ppermute | solution.py:28
  23.9 9.4 %collective-permute-start.6 = (bf16[16,1152]{1,0:T(8,128)(2,1)S(1)}, bf16[16,1152]{1,0:T(8,128)(2,1)S(1)}, u32[]{:S(2)}, u32[]{:S(2)}) collective-permute-start(bf16[16,1152]{1,0:T(8,128)(2,1)S(1)} %pad_maximum_fusion.2), channel_id=1, source_target_pairs={{96,0},{100,4},{104,8},{108,12},{112,16},{116,20},{120,24},{124,28... | collective-permute-start | bytes 110600 | tf_op jit(solution)/shard_map/ppermute | solution.py:28
  25.2 13.7 %collective-permute-start.15 = (bf16[96,512]{1,0:T(8,128)(2,1)S(1)}, bf16[96,512]{1,0:T(8,128)(2,1)S(1)}, u32[]{:S(2)}, u32[]{:S(2)}) collective-permute-start(bf16[96,512]{1,0:T(8,128)(2,1)S(1)} %pad_maximum_fusion.1), channel_id=1, source_target_pairs={{160,0},{164,4},{168,8},{172,12},{176,16},{180,20},{184,24},{188,2... | collective-permute-start | bytes 294920 | tf_op jit(solution)/shard_map/ppermute | solution.py:28
  28.8 9.4 %collective-permute-start.14 = (bf16[144,512]{1,0:T(8,128)(2,1)S(1)}, bf16[144,512]{1,0:T(8,128)(2,1)S(1)}, u32[]{:S(2)}, u32[]{:S(2)}) collective-permute-start(bf16[144,512]{1,0:T(8,128)(2,1)S(1)} %pad_maximum_fusion), channel_id=1, source_target_pairs={{96,0},{100,4},{104,8},{108,12},{112,16},{116,20},{120,24},{124,28... | collective-permute-start | bytes 442376 | tf_op jit(solution)/shard_map/ppermute | solution.py:28
  33.3 17.4 %collective-permute-start.10 = (bf16[16,3072]{1,0:T(8,128)(2,1)S(1)}, bf16[16,3072]{1,0:T(8,128)(2,1)S(1)}, u32[]{:S(2)}, u32[]{:S(2)}) collective-permute-start(bf16[16,3072]{1,0:T(8,128)(2,1)S(1)} %get-tuple-element.17), channel_id=1, source_target_pairs={{24,0},{28,4},{0,8},{4,12},{8,16},{12,20},{16,24},{20,28},{56,32},... | collective-permute-start | bytes 294920 | tf_op jit(solution)/shard_map/ppermute | solution.py:28
  34.6 7.3 %collective-permute-start.9 = (bf16[16,3072]{1,0:T(8,128)(2,1)S(1)}, bf16[16,3072]{1,0:T(8,128)(2,1)S(1)}, u32[]{:S(2)}, u32[]{:S(2)}) collective-permute-start(bf16[16,3072]{1,0:T(8,128)(2,1)S(1)} %get-tuple-element.17), channel_id=1, source_target_pairs={{16,0},{20,4},{24,8},{28,12},{0,16},{4,20},{8,24},{12,28},{48,32},... | collective-permute-start | bytes 294920 | tf_op jit(solution)/shard_map/ppermute | solution.py:28
  39.5 8.1 %collective-permute-start.16 = (bf16[384,512]{1,0:T(8,128)(2,1)S(1)}, bf16[384,512]{1,0:T(8,128)(2,1)S(1)}, u32[]{:S(2)}, u32[]{:S(2)}) collective-permute-start(bf16[384,512]{1,0:T(8,128)(2,1)S(1)} %get-tuple-element.7), channel_id=1, source_target_pairs={{1,0},{2,1},{3,2},{0,3},{12,4},{13,5},{14,6},{15,7},{9,8},{10,9},{... | collective-permute-start | bytes 1179656 | tf_op jit(solution)/shard_map/ppermute | solution.py:48
  41.8 12.9 %collective-permute-start.18 = (bf16[384,512]{1,0:T(8,128)(2,1)S(1)}, bf16[384,512]{1,0:T(8,128)(2,1)S(1)}, u32[]{:S(2)}, u32[]{:S(2)}) collective-permute-start(bf16[384,512]{1,0:T(8,128)(2,1)S(1)} %get-tuple-element.7), channel_id=1, source_target_pairs={{3,0},{0,1},{1,2},{2,3},{28,4},{29,5},{30,6},{31,7},{11,8},{8,9},{... | collective-permute-start | bytes 1179656 | tf_op jit(solution)/shard_map/ppermute | solution.py:48
  47.6 8.3 %collective-permute-start.17 = (bf16[192,512]{1,0:T(8,128)(2,1)S(1)}, bf16[192,512]{1,0:T(8,128)(2,1)S(1)}, u32[]{:S(2)}, u32[]{:S(2)}) collective-permute-start(bf16[192,512]{1,0:T(8,128)(2,1)S(1)} %slice.20), channel_id=1, source_target_pairs={{1,0},{2,1},{3,2},{0,3},{12,4},{13,5},{14,6},{15,7},{9,8},{10,9},{... | collective-permute-start | bytes 589832 | tf_op jit(solution)/shard_map/ppermute | solution.py:48
  50.8 14.4 %collective-permute-start.11 = (bf16[16,12288]{1,0:T(8,128)(2,1)S(1)}, bf16[16,12288]{1,0:T(8,128)(2,1)S(1)}, u32[]{:S(2)}, u32[]{:S(2)}) collective-permute-start(bf16[16,12288]{1,0:T(8,128)(2,1)S(1)} %constant_dynamic-update-slice_fusion.5), channel_id=1, source_target_pairs={{4,0},{0,4},{12,8},{8,12},{20,16},{16,20},{28,24},{24,28},{36,32},... | collective-permute-start | bytes 1179656 | tf_op jit(solution)/shard_map/ppermute | solution.py:28
  62.2 21.0 %collective-permute-start.22 = (bf16[1536,512]{1,0:T(8,128)(2,1)}, bf16[1536,512]{1,0:T(8,128)(2,1)S(1)}, u32[]{:S(2)}, u32[]{:S(2)}) collective-permute-start(bf16[1536,512]{1,0:T(8,128)(2,1)} %constant_dynamic-update-slice_fusion.18.refs_0_), channel_id=1, source_target_pairs={{24,0},{25,1},{26,2},{27,3},{7,4},{4,5},{5,6},{6,7},{0,8},{1,9},{2... | collective-permute-start | bytes 4718600 | tf_op jit(solution)/shard_map/ppermute | solution.py:48
  62.2 21.1 %collective-permute-start.20 = (bf16[1536,512]{1,0:T(8,128)(2,1)}, bf16[1536,512]{1,0:T(8,128)(2,1)}, u32[]{:S(2)}, u32[]{:S(2)}) collective-permute-start(bf16[1536,512]{1,0:T(8,128)(2,1)} %constant_dynamic-update-slice_fusion.18.refs_0_), channel_id=1, source_target_pairs={{8,0},{9,1},{10,2},{11,3},{5,4},{6,5},{7,6},{4,7},{16,8},{17,9},{1... | collective-permute-start | bytes 4718600 | tf_op jit(solution)/shard_map/ppermute | solution.py:48
  65.3 51.8 %collective-permute-start.24 = (bf16[1536,512]{1,0:T(8,128)(2,1)}, bf16[1536,512]{1,0:T(8,128)(2,1)}, u32[]{:S(2)}, u32[]{:S(2)}) collective-permute-start(bf16[1536,512]{1,0:T(8,128)(2,1)} %constant_dynamic-update-slice_fusion.18.refs_0_), channel_id=1, source_target_pairs={{4,0},{0,4},{12,8},{8,12},{20,16},{16,20},{28,24},{24,28},{36,32},... | collective-permute-start | bytes 4718600 | tf_op jit(solution)/shard_map/ppermute | solution.py:28
  83.3 23.6 %collective-permute-start.23 = (bf16[768,512]{1,0:T(8,128)(2,1)S(1)}, bf16[768,512]{1,0:T(8,128)(2,1)}, u32[]{:S(2)}, u32[]{:S(2)}) collective-permute-start(bf16[768,512]{1,0:T(8,128)(2,1)S(1)} %slice.23), channel_id=1, source_target_pairs={{24,0},{25,1},{26,2},{27,3},{7,4},{4,5},{5,6},{6,7},{0,8},{1,9},{2... | collective-permute-start | bytes 2359304 | tf_op jit(solution)/shard_map/ppermute | solution.py:48
  85.0 22.4 %collective-permute-start.21 = (bf16[768,512]{1,0:T(8,128)(2,1)S(1)}, bf16[768,512]{1,0:T(8,128)(2,1)}, u32[]{:S(2)}, u32[]{:S(2)}) collective-permute-start(bf16[768,512]{1,0:T(8,128)(2,1)S(1)} %slice.22), channel_id=1, source_target_pairs={{8,0},{9,1},{10,2},{11,3},{5,4},{6,5},{7,6},{4,7},{16,8},{17,9},{1... | collective-permute-start | bytes 2359304 | tf_op jit(solution)/shard_map/ppermute | solution.py:48
  87.3 29.8 %collective-permute-start.28 = (bf16[1536,512]{1,0:T(8,128)(2,1)S(1)}, bf16[1536,512]{1,0:T(8,128)(2,1)}, u32[]{:S(2)}, u32[]{:S(2)}) collective-permute-start(bf16[1536,512]{1,0:T(8,128)(2,1)S(1)} %collective-permute-done.22.refs_4_), channel_id=1, source_target_pairs={{4,0},{0,4},{12,8},{8,12},{20,16},{16,20},{28,24},{24,28},{36,32},... | collective-permute-start | bytes 4718600 | tf_op jit(solution)/shard_map/ppermute | solution.py:28
  89.9 27.2 %collective-permute-start.25 = (bf16[1536,512]{1,0:T(8,128)(2,1)}, bf16[1536,512]{1,0:T(8,128)(2,1)}, u32[]{:S(2)}, u32[]{:S(2)}) collective-permute-start(bf16[1536,512]{1,0:T(8,128)(2,1)} %collective-permute-done.20.refs_1_), channel_id=1, source_target_pairs={{4,0},{0,4},{12,8},{8,12},{20,16},{16,20},{28,24},{24,28},{36,32},... | collective-permute-start | bytes 4718600 | tf_op jit(solution)/shard_map/ppermute | solution.py:28
  100.6 15.6 %all-to-all-start = ((bf16[64,2,128]{2,1,0:T(2,128)(2,1)}), bf16[64,2,128]{2,1,0:T(2,128)(2,1)S(1)}, u32[]{:S(2)}, u32[]{:S(2)}) async-start(bf16[64,2,128]{2,1,0:T(2,128)(2,1)} %reshape.14), calls=%async_computation | async-start | bytes 65536 | tf_op jit(solution)/shard_map/all_to_all | solution.py:279
  106.9 10.2 %collective-permute-start.27 = (bf16[768,512]{1,0:T(8,128)(2,1)}, bf16[768,512]{1,0:T(8,128)(2,1)}, u32[]{:S(2)}, u32[]{:S(2)}) collective-permute-start(bf16[768,512]{1,0:T(8,128)(2,1)} %collective-permute-done.23.refs_3_), channel_id=1, source_target_pairs={{4,0},{0,4},{12,8},{8,12},{20,16},{16,20},{28,24},{24,28},{36,32},... | collective-permute-start | bytes 2359304 | tf_op jit(solution)/shard_map/ppermute | solution.py:28
  107.4 9.6 %collective-permute-start.26 = (bf16[768,512]{1,0:T(8,128)(2,1)}, bf16[768,512]{1,0:T(8,128)(2,1)S(1)}, u32[]{:S(2)}, u32[]{:S(2)}) collective-permute-start(bf16[768,512]{1,0:T(8,128)(2,1)} %collective-permute-done.21.refs_2_), channel_id=1, source_target_pairs={{4,0},{0,4},{12,8},{8,12},{20,16},{16,20},{28,24},{24,28},{36,32},... | collective-permute-start | bytes 2359304 | tf_op jit(solution)/shard_map/ppermute | solution.py:28
  (9 other events, 49.8 us)

commit v6 on v4

--- a/solution.py
+++ b/solution.py
@@ -234,13 +234,12 @@
     lax.fori_loop(0, batches // 2, two, 0)
 
     def multiply(t, _):
-        jk, a0 = t // 2, pl.multiple_of((t % 2) * 256, 256)
-        h = h_ref[pl.ds(jk, 1), :].astype(BF)
-        scaled[...] = left[pl.ds(a0, 256), :] * h
-        out_ref[jk, pl.ds(a0, 256), :] = jnp.dot(scaled[...], right[...], preferred_element_type=F32).astype(BF)
+        h = h_ref[pl.ds(t, 1), :].astype(BF)
+        scaled[...] = left[...] * h
+        out_ref[t] = jnp.dot(scaled[...], right[...], preferred_element_type=F32).astype(BF)
         return 0
 
-    lax.fori_loop(0, 8, multiply, 0)
+    lax.fori_loop(0, 4, multiply, 0)
 
 
 def last_stage(index, h, arrays, copies):
@@ -257,7 +256,7 @@
             pltpu.VMEM((128 * 8, 128), F32),
             pltpu.VMEM((512, pairs), BF),
             pltpu.VMEM((pairs, 512), BF),
-            pltpu.VMEM((256, pairs), BF),
+            pltpu.VMEM((512, pairs), BF),
             pltpu.SMEM((2048,), jnp.int32),
             pltpu.SemaphoreType.DMA((len(copies),)),
             pltpu.SemaphoreType.DMA((2,)),

time: 143 us -> 143 us (level)
  no operation moved by 1% of the time
where the time goes in v6:
time: 143 us; the launch traced here: 142 us
  starting transfers between devices  53.2 us (37%)
  waiting for transfers between devices  37.7 us (26%)
  Pallas kernels  33.9 us (24%)
  local copies, waits for them, and re-layouts  13.6 us (10%)
  other arithmetic  3.33 us (2%)
    ppermute x18, starting transfers between devices, fetch(): return lax.ppermute(value, 'pair', pair_moves(**{'d' + axis: step}))  30.2 us
    ppermute x8, waiting for transfers between devices, cross(): return lax.ppermute(value, ('pair', 'orb'), moves)  26 us
    pallas_call x1, Pallas kernels, last_stage(): pl.pallas_call(functools.partial(last_kernel, copies, len(arrays)), out_s...  24 us
    ppermute x8, starting transfers between devices, cross(): return lax.ppermute(value, ('pair', 'orb'), moves)  10.9 us
    pallas_call x1, Pallas kernels, half_transform(): pl.pallas_call(functools.partial(half_kernel, group), in_specs=[pl.BlockS...  9.85 us
    unnamed x22, local copies, waits for them, and re-layouts  8.04 us
    all_to_all x1, waiting for transfers between devices, stages(): owned = lax.all_to_all(sent, 'pair', 0, 0)  7.17 us
    all_to_all x1, starting transfers between devices, stages(): owned = lax.all_to_all(sent, 'pair', 0, 0)  6.3 us
  transfers between devices with their start and end apart: 30, of which 7 were waited for; matrix products, arithmetic and copies ran while one was open for 11% of the time, Pallas kernels for 7%

profile of v6, /device:TPU:1, one launch (start us, length us, event | category | flops | bytes accessed | tf_op | source)
XLA Modules:
  0.0 142.2 jit_solution(8643789904141733011)
XLA Ops:
  0.0 2.1 %collective-permute-start.2 = (bf16[32,48]{1,0:T(8,128)(2,1)}, bf16[32,48]{1,0:T(8,128)(2,1)S(1)}, u32[]{:S(2)}, u32[]{:S(2)}) collective-permute-start(bf16[32,48]{1,0:T(8,128)(2,1)} %bitcast.12), channel_id=1, source_target_pairs={{3,0},{0,1},{1,2},{2,3},{7,4},{4,5},{5,6},{6,7},{11,8},{8,9},{9,10... | collective-permute-start | bytes 9224 | tf_op jit(solution)/shard_map/ppermute | solution.py:27
  2.1 2.6 %collective-permute-start.1 = (bf16[32,48]{1,0:T(8,128)(2,1)}, bf16[32,48]{1,0:T(8,128)(2,1)S(1)}, u32[]{:S(2)}, u32[]{:S(2)}) collective-permute-start(bf16[32,48]{1,0:T(8,128)(2,1)} %bitcast.13), channel_id=1, source_target_pairs={{2,0},{3,1},{0,2},{1,3},{6,4},{7,5},{4,6},{5,7},{10,8},{11,9},{8,1... | collective-permute-start | bytes 9224 | tf_op jit(solution)/shard_map/ppermute | solution.py:27
  8.7 2.2 %collective-permute-start.3 = (bf16[32,192]{1,0:T(8,128)(2,1)S(1)}, bf16[32,192]{1,0:T(8,128)(2,1)S(1)}, u32[]{:S(2)}, u32[]{:S(2)}) collective-permute-start(bf16[32,192]{1,0:T(8,128)(2,1)S(1)} %dynamic_update_slice.15), channel_id=1, source_target_pairs={{4,0},{0,4},{12,8},{8,12},{20,16},{16,20},{28,24},{24,28},{36,32},... | collective-permute-start | bytes 36872 | tf_op jit(solution)/shard_map/ppermute | solution.py:28
  11.8 5.6 %collective-permute-start.5 = (bf16[16,384]{1,0:T(8,128)(2,1)S(1)}, bf16[16,384]{1,0:T(8,128)(2,1)S(1)}, u32[]{:S(2)}, u32[]{:S(2)}) collective-permute-start(bf16[16,384]{1,0:T(8,128)(2,1)S(1)} %fusion.27), channel_id=1, source_target_pairs={{32,0},{36,4},{40,8},{44,12},{48,16},{52,20},{56,24},{60,28},{64,3... | collective-permute-start | bytes 36872 | tf_op jit(solution)/shard_map/ppermute | solution.py:28
  19.8 1.7 %collective-permute-start.7 = (bf16[16,768]{1,0:T(8,128)(2,1)S(1)}, bf16[16,768]{1,0:T(8,128)(2,1)S(1)}, u32[]{:S(2)}, u32[]{:S(2)}) collective-permute-start(bf16[16,768]{1,0:T(8,128)(2,1)S(1)} %pad_maximum_fusion.3), channel_id=1, source_target_pairs={{160,0},{164,4},{168,8},{172,12},{176,16},{180,20},{184,24},{188,2... | collective-permute-start | bytes 73736 | tf_op jit(solution)/shard_map/ppermute | solution.py:28
  21.4 2.5 %collective-permute-done.4 = bf16[16,384]{1,0:T(8,128)(2,1)S(1)} collective-permute-done((bf16[16,384]{1,0:T(8,128)(2,1)S(1)}, bf16[16,384]{1,0:T(8,128)(2,1)S(1)}, u32[]{:S(2)}, u32[]{:S(2)}) %collective-permute-start.4) | collective-permute-done | bytes 12320 | tf_op jit(solution)/shard_map/ppermute | solution.py:28
  25.2 2.8 %collective-permute-start.15 = (bf16[96,512]{1,0:T(8,128)(2,1)S(1)}, bf16[96,512]{1,0:T(8,128)(2,1)S(1)}, u32[]{:S(2)}, u32[]{:S(2)}) collective-permute-start(bf16[96,512]{1,0:T(8,128)(2,1)S(1)} %pad_maximum_fusion.1), channel_id=1, source_target_pairs={{160,0},{164,4},{168,8},{172,12},{176,16},{180,20},{184,24},{188,2... | collective-permute-start | bytes 294920 | tf_op jit(solution)/shard_map/ppermute | solution.py:28
  28.8 1.8 %collective-permute-start.14 = (bf16[144,512]{1,0:T(8,128)(2,1)S(1)}, bf16[144,512]{1,0:T(8,128)(2,1)S(1)}, u32[]{:S(2)}, u32[]{:S(2)}) collective-permute-start(bf16[144,512]{1,0:T(8,128)(2,1)S(1)} %pad_maximum_fusion), channel_id=1, source_target_pairs={{96,0},{100,4},{104,8},{108,12},{112,16},{116,20},{120,24},{124,28... | collective-permute-start | bytes 442376 | tf_op jit(solution)/shard_map/ppermute | solution.py:28
  34.6 2.5 %collective-permute-start.9 = (bf16[16,3072]{1,0:T(8,128)(2,1)S(1)}, bf16[16,3072]{1,0:T(8,128)(2,1)S(1)}, u32[]{:S(2)}, u32[]{:S(2)}) collective-permute-start(bf16[16,3072]{1,0:T(8,128)(2,1)S(1)} %get-tuple-element.17), channel_id=1, source_target_pairs={{16,0},{20,4},{24,8},{28,12},{0,16},{4,20},{8,24},{12,28},{48,32},... | collective-permute-start | bytes 294920 | tf_op jit(solution)/shard_map/ppermute | solution.py:28
  39.5 2.2 %collective-permute-start.16 = (bf16[384,512]{1,0:T(8,128)(2,1)S(1)}, bf16[384,512]{1,0:T(8,128)(2,1)S(1)}, u32[]{:S(2)}, u32[]{:S(2)}) collective-permute-start(bf16[384,512]{1,0:T(8,128)(2,1)S(1)} %get-tuple-element.7), channel_id=1, source_target_pairs={{1,0},{2,1},{3,2},{0,3},{12,4},{13,5},{14,6},{15,7},{9,8},{10,9},{... | collective-permute-start | bytes 1179656 | tf_op jit(solution)/shard_map/ppermute | solution.py:48
  41.9 5.7 %collective-permute-done.16 = bf16[384,512]{1,0:T(8,128)(2,1)S(1)} collective-permute-done((bf16[384,512]{1,0:T(8,128)(2,1)S(1)}, bf16[384,512]{1,0:T(8,128)(2,1)S(1)}, u32[]{:S(2)}, u32[]{:S(2)}) %collective-permute-start.16) | collective-permute-done | bytes 393248 | tf_op jit(solution)/shard_map/ppermute | solution.py:48
  47.6 3.1 %collective-permute-start.17 = (bf16[192,512]{1,0:T(8,128)(2,1)S(1)}, bf16[192,512]{1,0:T(8,128)(2,1)S(1)}, u32[]{:S(2)}, u32[]{:S(2)}) collective-permute-start(bf16[192,512]{1,0:T(8,128)(2,1)S(1)} %slice.20), channel_id=1, source_target_pairs={{1,0},{2,1},{3,2},{0,3},{12,4},{13,5},{14,6},{15,7},{9,8},{10,9},{... | collective-permute-start | bytes 589832 | tf_op jit(solution)/shard_map/ppermute | solution.py:48
  50.8 3.9 %collective-permute-start.11 = (bf16[16,12288]{1,0:T(8,128)(2,1)S(1)}, bf16[16,12288]{1,0:T(8,128)(2,1)S(1)}, u32[]{:S(2)}, u32[]{:S(2)}) collective-permute-start(bf16[16,12288]{1,0:T(8,128)(2,1)S(1)} %constant_dynamic-update-slice_fusion.5), channel_id=1, source_target_pairs={{4,0},{0,4},{12,8},{8,12},{20,16},{16,20},{28,24},{24,28},{36,32},... | collective-permute-start | bytes 1179656 | tf_op jit(solution)/shard_map/ppermute | solution.py:28
  56.6 4.2 %collective-permute-done.19 = bf16[192,512]{1,0:T(8,128)(2,1)S(1)} collective-permute-done((bf16[192,512]{1,0:T(8,128)(2,1)S(1)}, bf16[192,512]{1,0:T(8,128)(2,1)S(1)}, u32[]{:S(2)}, u32[]{:S(2)}) %collective-permute-start.19) | collective-permute-done | bytes 196640 | tf_op jit(solution)/shard_map/ppermute | solution.py:48
  62.2 2.7 %collective-permute-start.20 = (bf16[1536,512]{1,0:T(8,128)(2,1)}, bf16[1536,512]{1,0:T(8,128)(2,1)}, u32[]{:S(2)}, u32[]{:S(2)}) collective-permute-start(bf16[1536,512]{1,0:T(8,128)(2,1)} %constant_dynamic-update-slice_fusion.18.refs_0_), channel_id=1, source_target_pairs={{8,0},{9,1},{10,2},{11,3},{5,4},{6,5},{7,6},{4,7},{16,8},{17,9},{1... | collective-permute-start | bytes 4718600 | tf_op jit(solution)/shard_map/ppermute | solution.py:48
  65.3 1.9 %collective-permute-start.24 = (bf16[1536,512]{1,0:T(8,128)(2,1)}, bf16[1536,512]{1,0:T(8,128)(2,1)}, u32[]{:S(2)}, u32[]{:S(2)}) collective-permute-start(bf16[1536,512]{1,0:T(8,128)(2,1)} %constant_dynamic-update-slice_fusion.18.refs_0_), channel_id=1, source_target_pairs={{4,0},{0,4},{12,8},{8,12},{20,16},{16,20},{28,24},{24,28},{36,32},... | collective-permute-start | bytes 4718600 | tf_op jit(solution)/shard_map/ppermute | solution.py:28
  67.1 16.1 %collective-permute-done.22.refs_4_ = bf16[1536,512]{1,0:T(8,128)(2,1)S(1)} collective-permute-done((bf16[1536,512]{1,0:T(8,128)(2,1)}, bf16[1536,512]{1,0:T(8,128)(2,1)S(1)}, u32[]{:S(2)}, u32[]{:S(2)}) %collective-permute-start.22) | collective-permute-done | bytes 1572896 | tf_op jit(solution)/shard_map/ppermute | solution.py:48
  83.4 1.6 %slice.22 = bf16[768,512]{1,0:T(8,128)(2,1)S(1)} slice(bf16[1536,512]{1,0:T(8,128)(2,1)} %collective-permute-done.20.refs_1_), slice={[0:768], [0:512]} | slice | bytes 1572864 | tf_op jit(solution)/shard_map/slice | solution.py:54
  85.0 2.3 %collective-permute-start.21 = (bf16[768,512]{1,0:T(8,128)(2,1)S(1)}, bf16[768,512]{1,0:T(8,128)(2,1)}, u32[]{:S(2)}, u32[]{:S(2)}) collective-permute-start(bf16[768,512]{1,0:T(8,128)(2,1)S(1)} %slice.22), channel_id=1, source_target_pairs={{8,0},{9,1},{10,2},{11,3},{5,4},{6,5},{7,6},{4,7},{16,8},{17,9},{1... | collective-permute-start | bytes 2359304 | tf_op jit(solution)/shard_map/ppermute | solution.py:48
  87.3 2.6 %collective-permute-start.28 = (bf16[1536,512]{1,0:T(8,128)(2,1)S(1)}, bf16[1536,512]{1,0:T(8,128)(2,1)}, u32[]{:S(2)}, u32[]{:S(2)}) collective-permute-start(bf16[1536,512]{1,0:T(8,128)(2,1)S(1)} %collective-permute-done.22.refs_4_), channel_id=1, source_target_pairs={{4,0},{0,4},{12,8},{8,12},{20,16},{16,20},{28,24},{24,28},{36,32},... | collective-permute-start | bytes 4718600 | tf_op jit(solution)/shard_map/ppermute | solution.py:28
  90.0 9.8 %half_transform.1 = f32[256,64]{1,0:T(8,128)S(1)} custom-call(s32[2,64,8]{2,1,0:T(8,128)S(1)} %fusion.4.scr_ref, bf16[8,12288]{1,0:T(8,128)(2,1)S(1)} %constant_dynamic-slice_fusion.own_ref, bf16[32,12288]{1,0:T(8,128)(2,1)S(1)} %maximum_select_fusion.occ_ref, bf16[64,8,128,128]{3,2,1,0:T(8,128)(2,1)} %ints_ref.1), custom_call_target="tpu_custom_call" | custom-call | flops 300000000 | bytes 18000000 | tf_op jit(solution)/shard_map/half_transform/pallas_call | solution.py:157
  100.6 6.3 %all-to-all-start = ((bf16[64,2,128]{2,1,0:T(2,128)(2,1)}), bf16[64,2,128]{2,1,0:T(2,128)(2,1)S(1)}, u32[]{:S(2)}, u32[]{:S(2)}) async-start(bf16[64,2,128]{2,1,0:T(2,128)(2,1)} %reshape.14), calls=%async_computation | async-start | bytes 65536 | tf_op jit(solution)/shard_map/all_to_all | solution.py:276
  109.0 7.2 %all-to-all-done = bf16[64,2,128]{2,1,0:T(2,128)(2,1)S(1)} async-done(((bf16[64,2,128]{2,1,0:T(2,128)(2,1)}), bf16[64,2,128]{2,1,0:T(2,128)(2,1)S(1)}, u32[]{:S(2)}, u32[]{:S(2)}) %all-to-all-start) | async-done | bytes 32800 | tf_op jit(solution)/shard_map/all_to_all | solution.py:276
  118.0 24.0 %gather_scale_dot.1 = bf16[4,512,512]{2,1,0:T(8,128)(2,1)} custom-call(s32[8192]{0:T(1024)} %bitcast.11, f32[4,4096]{1,0:T(4,128)} %reshape.13.h_ref, bf16[1536,512]{1,0:T(8,128)(2,1)} %constant_dynamic-update-slice_fusion.18.refs_0_, bf16[1536,512]{1,0:T(8,128)(2,1)} %collective-permute-done.20.refs_1_, bf16[768,512]{1,0:T(8,128)(2,1)} %collective-permute-done.21.refs_2_, ...), custom_call_target="tpu_custom_call" | custom-call | flops 8999999488 | bytes 15000000 | tf_op jit(solution)/shard_map/gather_scale_dot/pallas_call | solution.py:247
  (86 shorter events, 24.3 us)
Async XLA Ops:
  0.0 8.4 %collective-permute-start.2 = (bf16[32,48]{1,0:T(8,128)(2,1)}, bf16[32,48]{1,0:T(8,128)(2,1)S(1)}, u32[]{:S(2)}, u32[]{:S(2)}) collective-permute-start(bf16[32,48]{1,0:T(8,128)(2,1)} %bitcast.12), channel_id=1, source_target_pairs={{3,0},{0,1},{1,2},{2,3},{7,4},{4,5},{5,6},{6,7},{11,8},{8,9},{9,10... | collective-permute-start | bytes 9224 | tf_op jit(solution)/shard_map/ppermute | solution.py:27
  11.8 8.0 %collective-permute-start.5 = (bf16[16,384]{1,0:T(8,128)(2,1)S(1)}, bf16[16,384]{1,0:T(8,128)(2,1)S(1)}, u32[]{:S(2)}, u32[]{:S(2)}) collective-permute-start(bf16[16,384]{1,0:T(8,128)(2,1)S(1)} %fusion.27), channel_id=1, source_target_pairs={{32,0},{36,4},{40,8},{44,12},{48,16},{52,20},{56,24},{60,28},{64,3... | collective-permute-start | bytes 36872 | tf_op jit(solution)/shard_map/ppermute | solution.py:28
  17.4 7.1 %collective-permute-start.13 = (bf16[48,512]{1,0:T(8,128)(2,1)}, bf16[48,512]{1,0:T(8,128)(2,1)S(1)}, u32[]{:S(2)}, u32[]{:S(2)}) collective-permute-start(bf16[48,512]{1,0:T(8,128)(2,1)} %param.8), channel_id=1, source_target_pairs={{32,0},{36,4},{40,8},{44,12},{48,16},{52,20},{56,24},{60,28},{64,3... | collective-permute-start | bytes 147464 | tf_op jit(solution)/shard_map/ppermute | solution.py:28
  18.1 9.9 %collective-permute-start.12 = (bf16[48,512]{1,0:T(8,128)(2,1)}, bf16[48,512]{1,0:T(8,128)(2,1)S(1)}, u32[]{:S(2)}, u32[]{:S(2)}) collective-permute-start(bf16[48,512]{1,0:T(8,128)(2,1)} %param.8), channel_id=1, source_target_pairs={{224,0},{228,4},{232,8},{236,12},{240,16},{244,20},{248,24},{252,2... | collective-permute-start | bytes 147464 | tf_op jit(solution)/shard_map/ppermute | solution.py:28
  19.8 13.5 %collective-permute-start.7 = (bf16[16,768]{1,0:T(8,128)(2,1)S(1)}, bf16[16,768]{1,0:T(8,128)(2,1)S(1)}, u32[]{:S(2)}, u32[]{:S(2)}) collective-permute-start(bf16[16,768]{1,0:T(8,128)(2,1)S(1)} %pad_maximum_fusion.3), channel_id=1, source_target_pairs={{160,0},{164,4},{168,8},{172,12},{176,16},{180,20},{184,24},{188,2... | collective-permute-start | bytes 73736 | tf_op jit(solution)/shard_map/ppermute | solution.py:28
  23.9 9.4 %collective-permute-start.6 = (bf16[16,1152]{1,0:T(8,128)(2,1)S(1)}, bf16[16,1152]{1,0:T(8,128)(2,1)S(1)}, u32[]{:S(2)}, u32[]{:S(2)}) collective-permute-start(bf16[16,1152]{1,0:T(8,128)(2,1)S(1)} %pad_maximum_fusion.2), channel_id=1, source_target_pairs={{96,0},{100,4},{104,8},{108,12},{112,16},{116,20},{120,24},{124,28... | collective-permute-start | bytes 110600 | tf_op jit(solution)/shard_map/ppermute | solution.py:28
  25.2 13.7 %collective-permute-start.15 = (bf16[96,512]{1,0:T(8,128)(2,1)S(1)}, bf16[96,512]{1,0:T(8,128)(2,1)S(1)}, u32[]{:S(2)}, u32[]{:S(2)}) collective-permute-start(bf16[96,512]{1,0:T(8,128)(2,1)S(1)} %pad_maximum_fusion.1), channel_id=1, source_target_pairs={{160,0},{164,4},{168,8},{172,12},{176,16},{180,20},{184,24},{188,2... | collective-permute-start | bytes 294920 | tf_op jit(solution)/shard_map/ppermute | solution.py:28
  28.8 9.4 %collective-permute-start.14 = (bf16[144,512]{1,0:T(8,128)(2,1)S(1)}, bf16[144,512]{1,0:T(8,128)(2,1)S(1)}, u32[]{:S(2)}, u32[]{:S(2)}) collective-permute-start(bf16[144,512]{1,0:T(8,128)(2,1)S(1)} %pad_maximum_fusion), channel_id=1, source_target_pairs={{96,0},{100,4},{104,8},{108,12},{112,16},{116,20},{120,24},{124,28... | collective-permute-start | bytes 442376 | tf_op jit(solution)/shard_map/ppermute | solution.py:28
  33.3 17.4 %collective-permute-start.10 = (bf16[16,3072]{1,0:T(8,128)(2,1)S(1)}, bf16[16,3072]{1,0:T(8,128)(2,1)S(1)}, u32[]{:S(2)}, u32[]{:S(2)}) collective-permute-start(bf16[16,3072]{1,0:T(8,128)(2,1)S(1)} %get-tuple-element.17), channel_id=1, source_target_pairs={{24,0},{28,4},{0,8},{4,12},{8,16},{12,20},{16,24},{20,28},{56,32},... | collective-permute-start | bytes 294920 | tf_op jit(solution)/shard_map/ppermute | solution.py:28
  34.6 7.3 %collective-permute-start.9 = (bf16[16,3072]{1,0:T(8,128)(2,1)S(1)}, bf16[16,3072]{1,0:T(8,128)(2,1)S(1)}, u32[]{:S(2)}, u32[]{:S(2)}) collective-permute-start(bf16[16,3072]{1,0:T(8,128)(2,1)S(1)} %get-tuple-element.17), channel_id=1, source_target_pairs={{16,0},{20,4},{24,8},{28,12},{0,16},{4,20},{8,24},{12,28},{48,32},... | collective-permute-start | bytes 294920 | tf_op jit(solution)/shard_map/ppermute | solution.py:28
  39.5 8.1 %collective-permute-start.16 = (bf16[384,512]{1,0:T(8,128)(2,1)S(1)}, bf16[384,512]{1,0:T(8,128)(2,1)S(1)}, u32[]{:S(2)}, u32[]{:S(2)}) collective-permute-start(bf16[384,512]{1,0:T(8,128)(2,1)S(1)} %get-tuple-element.7), channel_id=1, source_target_pairs={{1,0},{2,1},{3,2},{0,3},{12,4},{13,5},{14,6},{15,7},{9,8},{10,9},{... | collective-permute-start | bytes 1179656 | tf_op jit(solution)/shard_map/ppermute | solution.py:48
  41.8 12.9 %collective-permute-start.18 = (bf16[384,512]{1,0:T(8,128)(2,1)S(1)}, bf16[384,512]{1,0:T(8,128)(2,1)S(1)}, u32[]{:S(2)}, u32[]{:S(2)}) collective-permute-start(bf16[384,512]{1,0:T(8,128)(2,1)S(1)} %get-tuple-element.7), channel_id=1, source_target_pairs={{3,0},{0,1},{1,2},{2,3},{28,4},{29,5},{30,6},{31,7},{11,8},{8,9},{... | collective-permute-start | bytes 1179656 | tf_op jit(solution)/shard_map/ppermute | solution.py:48
  47.6 8.3 %collective-permute-start.17 = (bf16[192,512]{1,0:T(8,128)(2,1)S(1)}, bf16[192,512]{1,0:T(8,128)(2,1)S(1)}, u32[]{:S(2)}, u32[]{:S(2)}) collective-permute-start(bf16[192,512]{1,0:T(8,128)(2,1)S(1)} %slice.20), channel_id=1, source_target_pairs={{1,0},{2,1},{3,2},{0,3},{12,4},{13,5},{14,6},{15,7},{9,8},{10,9},{... | collective-permute-start | bytes 589832 | tf_op jit(solution)/shard_map/ppermute | solution.py:48
  50.8 14.4 %collective-permute-start.11 = (bf16[16,12288]{1,0:T(8,128)(2,1)S(1)}, bf16[16,12288]{1,0:T(8,128)(2,1)S(1)}, u32[]{:S(2)}, u32[]{:S(2)}) collective-permute-start(bf16[16,12288]{1,0:T(8,128)(2,1)S(1)} %constant_dynamic-update-slice_fusion.5), channel_id=1, source_target_pairs={{4,0},{0,4},{12,8},{8,12},{20,16},{16,20},{28,24},{24,28},{36,32},... | collective-permute-start | bytes 1179656 | tf_op jit(solution)/shard_map/ppermute | solution.py:28
  62.2 21.0 %collective-permute-start.22 = (bf16[1536,512]{1,0:T(8,128)(2,1)}, bf16[1536,512]{1,0:T(8,128)(2,1)S(1)}, u32[]{:S(2)}, u32[]{:S(2)}) collective-permute-start(bf16[1536,512]{1,0:T(8,128)(2,1)} %constant_dynamic-update-slice_fusion.18.refs_0_), channel_id=1, source_target_pairs={{24,0},{25,1},{26,2},{27,3},{7,4},{4,5},{5,6},{6,7},{0,8},{1,9},{2... | collective-permute-start | bytes 4718600 | tf_op jit(solution)/shard_map/ppermute | solution.py:48
  62.2 21.1 %collective-permute-start.20 = (bf16[1536,512]{1,0:T(8,128)(2,1)}, bf16[1536,512]{1,0:T(8,128)(2,1)}, u32[]{:S(2)}, u32[]{:S(2)}) collective-permute-start(bf16[1536,512]{1,0:T(8,128)(2,1)} %constant_dynamic-update-slice_fusion.18.refs_0_), channel_id=1, source_target_pairs={{8,0},{9,1},{10,2},{11,3},{5,4},{6,5},{7,6},{4,7},{16,8},{17,9},{1... | collective-permute-start | bytes 4718600 | tf_op jit(solution)/shard_map/ppermute | solution.py:48
  65.3 51.8 %collective-permute-start.24 = (bf16[1536,512]{1,0:T(8,128)(2,1)}, bf16[1536,512]{1,0:T(8,128)(2,1)}, u32[]{:S(2)}, u32[]{:S(2)}) collective-permute-start(bf16[1536,512]{1,0:T(8,128)(2,1)} %constant_dynamic-update-slice_fusion.18.refs_0_), channel_id=1, source_target_pairs={{4,0},{0,4},{12,8},{8,12},{20,16},{16,20},{28,24},{24,28},{36,32},... | collective-permute-start | bytes 4718600 | tf_op jit(solution)/shard_map/ppermute | solution.py:28
  83.3 23.6 %collective-permute-start.23 = (bf16[768,512]{1,0:T(8,128)(2,1)S(1)}, bf16[768,512]{1,0:T(8,128)(2,1)}, u32[]{:S(2)}, u32[]{:S(2)}) collective-permute-start(bf16[768,512]{1,0:T(8,128)(2,1)S(1)} %slice.23), channel_id=1, source_target_pairs={{24,0},{25,1},{26,2},{27,3},{7,4},{4,5},{5,6},{6,7},{0,8},{1,9},{2... | collective-permute-start | bytes 2359304 | tf_op jit(solution)/shard_map/ppermute | solution.py:48
  85.0 22.4 %collective-permute-start.21 = (bf16[768,512]{1,0:T(8,128)(2,1)S(1)}, bf16[768,512]{1,0:T(8,128)(2,1)}, u32[]{:S(2)}, u32[]{:S(2)}) collective-permute-start(bf16[768,512]{1,0:T(8,128)(2,1)S(1)} %slice.22), channel_id=1, source_target_pairs={{8,0},{9,1},{10,2},{11,3},{5,4},{6,5},{7,6},{4,7},{16,8},{17,9},{1... | collective-permute-start | bytes 2359304 | tf_op jit(solution)/shard_map/ppermute | solution.py:48
  87.3 29.8 %collective-permute-start.28 = (bf16[1536,512]{1,0:T(8,128)(2,1)S(1)}, bf16[1536,512]{1,0:T(8,128)(2,1)}, u32[]{:S(2)}, u32[]{:S(2)}) collective-permute-start(bf16[1536,512]{1,0:T(8,128)(2,1)S(1)} %collective-permute-done.22.refs_4_), channel_id=1, source_target_pairs={{4,0},{0,4},{12,8},{8,12},{20,16},{16,20},{28,24},{24,28},{36,32},... | collective-permute-start | bytes 4718600 | tf_op jit(solution)/shard_map/ppermute | solution.py:28
  89.9 27.2 %collective-permute-start.25 = (bf16[1536,512]{1,0:T(8,128)(2,1)}, bf16[1536,512]{1,0:T(8,128)(2,1)}, u32[]{:S(2)}, u32[]{:S(2)}) collective-permute-start(bf16[1536,512]{1,0:T(8,128)(2,1)} %collective-permute-done.20.refs_1_), channel_id=1, source_target_pairs={{4,0},{0,4},{12,8},{8,12},{20,16},{16,20},{28,24},{24,28},{36,32},... | collective-permute-start | bytes 4718600 | tf_op jit(solution)/shard_map/ppermute | solution.py:28
  100.6 15.6 %all-to-all-start = ((bf16[64,2,128]{2,1,0:T(2,128)(2,1)}), bf16[64,2,128]{2,1,0:T(2,128)(2,1)S(1)}, u32[]{:S(2)}, u32[]{:S(2)}) async-start(bf16[64,2,128]{2,1,0:T(2,128)(2,1)} %reshape.14), calls=%async_computation | async-start | bytes 65536 | tf_op jit(solution)/shard_map/all_to_all | solution.py:276
  106.9 10.2 %collective-permute-start.27 = (bf16[768,512]{1,0:T(8,128)(2,1)}, bf16[768,512]{1,0:T(8,128)(2,1)}, u32[]{:S(2)}, u32[]{:S(2)}) collective-permute-start(bf16[768,512]{1,0:T(8,128)(2,1)} %collective-permute-done.23.refs_3_), channel_id=1, source_target_pairs={{4,0},{0,4},{12,8},{8,12},{20,16},{16,20},{28,24},{24,28},{36,32},... | collective-permute-start | bytes 2359304 | tf_op jit(solution)/shard_map/ppermute | solution.py:28
  107.4 9.6 %collective-permute-start.26 = (bf16[768,512]{1,0:T(8,128)(2,1)}, bf16[768,512]{1,0:T(8,128)(2,1)S(1)}, u32[]{:S(2)}, u32[]{:S(2)}) collective-permute-start(bf16[768,512]{1,0:T(8,128)(2,1)} %collective-permute-done.21.refs_2_), channel_id=1, source_target_pairs={{4,0},{0,4},{12,8},{8,12},{20,16},{16,20},{28,24},{24,28},{36,32},... | collective-permute-start | bytes 2359304 | tf_op jit(solution)/shard_map/ppermute | solution.py:28
  (9 other events, 49.8 us)
